TPU v7x, 128 devices: a whole 4x4x4 slice. The times are simulated.
128 devices in a mesh: mp: 4 (over y_lo, core), latent: 32 (over y_hi, x, z).
Axes of the slice: x: 4, y: 4 (y_hi: 2, y_lo: 2; y = y_hi * 2 + y_lo), z: 4, core: 2. Of those that a mesh axis runs over, the one named last changes fastest.
Arguments:
- resid_clean: bfloat16 [128, 4608], P(('mp', 'latent')), may hold values from -6 to 6
- resid_corrupt: bfloat16 [128, 4608], P(('mp', 'latent')), may hold values from -6 to 6
- answer_ids: int32 [128, 2], replicated, may hold values from 0 to 127, all different within a row
- unembed: bfloat16 [128, 4608], replicated, may hold values from -1.5 to 1.5
- pre_gain: float32 [4608], replicated, may hold values from 0.25 to 1.75
- post_gain: float32 [4608], replicated, may hold values from 0.25 to 1.75
- final_gain: float32 [4608], replicated, may hold values from 0.25 to 1.75
- w_gate: bfloat16 [4608, 36864], P(None, ('mp', 'latent')), may hold values from -0.09375 to 0.09375
- w_up: bfloat16 [4608, 36864], P(None, ('mp', 'latent')), may hold values from -0.09375 to 0.09375
- w_down: bfloat16 [36864, 4608], P(('mp', 'latent')), may hold values from -0.03125 to 0.03125
- w_enc: bfloat16 [4608, 65536], P(None, ('mp', 'latent')), may hold values from -0.09375 to 0.09375
- b_enc: float32 [65536], P(('mp', 'latent')), may hold values from -3 to 3
- w_dec: bfloat16 [65536, 4608], P(('mp', 'latent')), may hold values from -0.09375 to 0.09375
Outputs:
- attribution: float32 [1, 65536], P(None, ('mp', 'latent'))
Inputs may be any that keep to these rules, and one draw needn't show every extreme that they name: `answer_ids`: the two indices of a token differ.
All inputs are finite; a program needn't handle non-finite values.
Results may differ from a plain program's by a relative error of at most 0.0056.
Values may be sent and summed in bfloat16 or wider, within the bound.
No kernel may reach another device: no remote copies, remote signals or barrier semaphores. Data moves between devices by JAX's collectives and lax.ppermute only.
A program may use at most 128 MiB of HBM per device.

v0:
```python
import jax
import jax.numpy as jnp
from jax import lax
from jax.experimental import pallas as pl
from jax.experimental.pallas import tpu as pltpu
from jax.sharding import Mesh
from jax.sharding import PartitionSpec as P

epsilon = 1e-06
gelu_scale = 0.7978845608028654
gelu_cubic = 0.044715

DEVICES = ("y_lo", "core", "y_hi", "x", "z")
COLUMN = ("y_lo", "core", "y_hi")
PLANE = ("x", "z")
SWAP = [(0, 1), (1, 0)]
F32 = jnp.float32
BF16 = jnp.bfloat16
VMEM = pl.BlockSpec(memory_space=pltpu.VMEM)
SMEM = pl.BlockSpec(memory_space=pltpu.SMEM)


def shape(dims, dtype):
    return jax.ShapeDtypeStruct(dims, dtype)


def call(kernel, outs, *args, scratch=()):
    specs = [SMEM if a.dtype == jnp.int32 else VMEM for a in args]
    return pl.pallas_call(
        kernel,
        out_shape=outs,
        in_specs=specs,
        out_specs=jax.tree.map(lambda _: VMEM, outs),
        scratch_shapes=scratch,
        compiler_params=pltpu.CompilerParams(vmem_limit_bytes=56 << 20),
    )(*args)


def gelu_tanh(value):
    return 0.5 * value * (1.0 + jnp.tanh(gelu_scale * (value + gelu_cubic * value * value * value)))


def gelu_slope(value):
    inner = jnp.tanh(gelu_scale * (value + gelu_cubic * value * value * value))
    return 0.5 * (1.0 + inner) + 0.5 * value * (1.0 - inner * inner) * gelu_scale * (
        1.0 + 3.0 * gelu_cubic * value * value
    )


def dot_nn(left, right):
    return jnp.dot(left, right, preferred_element_type=F32)


def dot_nt(left, right):
    return lax.dot_general(left, right, (((1,), (1,)), ((), ())), preferred_element_type=F32)


def mean_row(value):
    return jnp.mean(value, axis=-1, keepdims=True)


def halves(core_ref, width):
    core = core_ref[0]
    return (
        pl.ds(pl.multiple_of(core * width, 128), width),
        pl.ds(pl.multiple_of((1 - core) * width, 128), width),
    )


def forward_kernel(core, own, other, w_gate, w_up, w_down, gain, send, hidden, gate, up, normed):
    width = own.shape[1]
    mine, theirs = halves(core, width)
    a, b = own[...].astype(F32), other[...].astype(F32)
    total = jnp.sum(a * a, axis=-1, keepdims=True) + jnp.sum(b * b, axis=-1, keepdims=True)
    inv = lax.rsqrt(total / (2 * width) + epsilon)
    normed[:, mine] = (a * inv * gain[:, mine]).astype(BF16)
    normed[:, theirs] = (b * inv * gain[:, theirs]).astype(BF16)
    gate_pre = dot_nt(normed[...], w_gate[...])
    up_proj = dot_nt(normed[...], w_up[...])
    gate[...] = gate_pre
    up[...] = up_proj
    act = (gelu_tanh(gate_pre) * up_proj).astype(BF16)
    hidden[...] = act
    send[...] = dot_nn(act, w_down[:, theirs]).astype(BF16)


def forward_sum_kernel(core, hidden, w_down, arrived, out):
    mine, _ = halves(core, arrived.shape[1])
    total = dot_nn(hidden[...], w_down[:, mine]) + arrived[...].astype(F32)
    out[...] = total.astype(BF16).reshape(out.shape)


def plane_sum_kernel(pieces, out):
    total = jnp.sum(pieces[...].astype(F32), axis=0).astype(BF16)
    for peer in range(out.shape[0]):
        out[peer] = total


def column_total(pieces):
    sums = []
    for core in range(2):
        total = None
        for peer in range(pieces.shape[0]):
            if (peer // 2) % 2 == core:
                part = pieces[peer].astype(F32)
                total = part if total is None else total + part
        sums.append(total)
    return jnp.concatenate(sums, axis=1)


def direction_kernel(answers, unembed, gain, out):
    lanes = lax.broadcasted_iota(jnp.int32, (1, unembed.shape[0]), 1)
    rows = []
    for token in range(out.shape[0]):
        rows.append(
            (lanes == answers[token, 0]).astype(F32) - (lanes == answers[token, 1]).astype(F32)
        )
    selector = jnp.concatenate(rows, axis=0).astype(BF16)
    out[...] = gain[...] * dot_nn(selector, unembed[...])


def output_kernel(core, pieces, stream, weighted, post_gain, out, grad_output, grad_mlp):
    mine, _ = halves(core, out.shape[2])
    mlp_out = column_total(pieces)
    inv_post = lax.rsqrt(mean_row(mlp_out * mlp_out) + epsilon)
    output = stream[...].astype(F32) + mlp_out * inv_post * post_gain[...]
    inv_final = lax.rsqrt(mean_row(output * output) + epsilon)
    wanted = weighted[...]
    grad_out = inv_final * wanted - output * (inv_final * inv_final * inv_final) * mean_row(
        wanted * output
    )
    grad_output[...] = grad_out
    post_grad = post_gain[...] * grad_out
    grad_mlp[...] = inv_post * post_grad - mlp_out * (inv_post * inv_post * inv_post) * mean_row(
        post_grad * mlp_out
    )
    value = grad_mlp[:, mine].astype(BF16)
    for peer in range(out.shape[0]):
        out[peer] = value


def backward_kernel(core, own, other, gate, up, w_gate, w_up, w_down, send, grad_gate, grad_up):
    mine, theirs = halves(core, own.shape[1])
    grad_hidden = dot_nt(own[...], w_down[:, mine]) + dot_nt(other[...], w_down[:, theirs])
    gate_pre = gate[...]
    to_gate = (grad_hidden * up[...] * gelu_slope(gate_pre)).astype(BF16)
    to_up = (grad_hidden * gelu_tanh(gate_pre)).astype(BF16)
    grad_gate[...] = to_gate
    grad_up[...] = to_up
    send[...] = (dot_nn(to_gate, w_gate[:, theirs]) + dot_nn(to_up, w_up[:, theirs])).astype(BF16)


def backward_sum_kernel(core, grad_gate, grad_up, w_gate, w_up, arrived, out):
    mine, _ = halves(core, arrived.shape[1])
    total = dot_nn(grad_gate[...], w_gate[:, mine]) + dot_nn(grad_up[...], w_up[:, mine])
    out[...] = (total + arrived[...].astype(F32)).astype(BF16).reshape(out.shape)


def input_kernel(core, pieces, stream, grad_output, pre_gain, out, grad_stream):
    mine, _ = halves(core, out.shape[2])
    rows = stream[...].astype(F32)
    inv_pre = lax.rsqrt(mean_row(rows * rows) + epsilon)
    pre_grad = pre_gain[...] * column_total(pieces)
    grad_stream[...] = (
        grad_output[...]
        + inv_pre * pre_grad
        - rows * (inv_pre * inv_pre * inv_pre) * mean_row(pre_grad * rows)
    )
    value = grad_stream[:, mine].astype(BF16)
    for peer in range(out.shape[0]):
        out[peer] = value


def change_kernel(core, own, other, own_corrupt, other_corrupt, w_enc, b_enc, out):
    width = own.shape[1]
    first, second = halves(core, width)
    bias = b_enc[...]

    def code(a, b):
        return jax.nn.relu(dot_nn(a[...], w_enc[first, :]) + dot_nn(b[...], w_enc[second, :]) + bias)

    out[...] = code(own, other) - code(own_corrupt, other_corrupt)


def attribution_kernel(core, own, other, w_dec, change, out):
    mine, theirs = halves(core, own.shape[1])
    projected = dot_nt(own[...], w_dec[:, mine]) + dot_nt(other[...], w_dec[:, theirs])
    out[...] = jnp.sum(change[...] * projected, axis=0, keepdims=True)


def exchanged(blocks, axes):
    return lax.all_to_all(blocks, axes, 0, 0, tiled=True)


def swapped(value):
    return lax.ppermute(value, "core", SWAP)


def local(
    resid_clean,
    resid_corrupt,
    answer_ids,
    unembed,
    pre_gain,
    post_gain,
    final_gain,
    w_gate,
    w_up,
    w_down,
    w_enc,
    b_enc,
    w_dec,
):
    width = resid_clean.shape[1]
    half = width // 2
    column, plane = lax.axis_size(COLUMN), lax.axis_size(PLANE)
    tokens = column * plane
    core_index = lax.axis_index("core")
    core = core_index.astype(jnp.int32).reshape(1)
    hidden_units, latents = w_gate.shape[1], w_enc.shape[1]
    w_gate, w_up = w_gate.T, w_up.T
    pre_gain, post_gain, final_gain = (g[None] for g in (pre_gain, post_gain, final_gain))

    both = jnp.concatenate([resid_clean, resid_corrupt], axis=0)
    mixed = exchanged(jnp.broadcast_to(both[None], (column, 2, width)), COLUMN)
    stream = mixed[:, 0]
    corrupt = mixed[:, 1]

    def spread(block):
        mine = lax.dynamic_slice_in_dim(block, core_index * half, half, 1)
        return jnp.broadcast_to(mine[None], (plane, column, half))

    def gathered(blocks):
        own = exchanged(blocks, PLANE).reshape(tokens, half)
        return own, swapped(own)

    blocks = shape((plane, column, half), BF16)
    peers = shape((column, column, half), BF16)
    rows = shape((column, width), F32)
    send = shape((tokens, half), BF16)
    units = shape((tokens, hidden_units), BF16)
    units32 = shape((tokens, hidden_units), F32)

    own, other = gathered(spread(stream))
    sent, hidden, gate, up = call(
        forward_kernel,
        (send, units, units32, units32),
        core, own, other, w_gate, w_up, w_down, pre_gain,
        scratch=[pltpu.VMEM((tokens, width), BF16)],
    )
    pieces = call(forward_sum_kernel, blocks, core, hidden, w_down, swapped(sent))
    pieces = call(plane_sum_kernel, peers, exchanged(pieces, PLANE))

    place = lax.axis_index(PLANE)
    answers = lax.dynamic_slice_in_dim(answer_ids.reshape(column, plane, 2), place, 1, 1)[:, 0]
    weighted = call(direction_kernel, rows, answers, unembed, final_gain)
    spread_grad, grad_output = call(
        output_kernel,
        (blocks, rows),
        core, exchanged(pieces, COLUMN), stream, weighted, post_gain,
        scratch=[pltpu.VMEM((column, width), F32)],
    )

    grad_own, grad_other = gathered(spread_grad)
    sent, grad_gate, grad_up = call(
        backward_kernel,
        (send, units, units),
        core, grad_own, grad_other, gate, up, w_gate, w_up, w_down,
    )
    pieces = call(
        backward_sum_kernel, blocks, core, grad_gate, grad_up, w_gate, w_up, swapped(sent)
    )
    pieces = call(plane_sum_kernel, peers, exchanged(pieces, PLANE))
    spread_stream = call(
        input_kernel,
        blocks,
        core, exchanged(pieces, COLUMN), stream, grad_output, pre_gain,
        scratch=[pltpu.VMEM((column, width), F32)],
    )

    own_corrupt, other_corrupt = gathered(spread(corrupt))
    change = call(
        change_kernel,
        shape((tokens, latents), F32),
        core, own, other, own_corrupt, other_corrupt, w_enc, b_enc[None],
    )
    last_own, last_other = gathered(spread_stream)
    return call(
        attribution_kernel, shape((1, latents), F32), core, last_own, last_other, w_dec, change
    )


def solution(mesh):
    fine = Mesh(mesh.devices.reshape(2, 2, 2, 4, 4), DEVICES)
    return jax.shard_map(
        local,
        mesh=fine,
        in_specs=(
            P(DEVICES, None),
            P(DEVICES, None),
            P(),
            P(),
            P(),
            P(),
            P(),
            P(None, DEVICES),
            P(None, DEVICES),
            P(DEVICES, None),
            P(None, DEVICES),
            P(DEVICES),
            P(DEVICES, None),
        ),
        out_specs=P(None, DEVICES),
        check_vma=False,
    )
```

profile of v0, /device:TPU:1, one launch (start us, length us, event | category | flops | bytes accessed | tf_op | source)
XLA Modules:
  0.0 191.2 jit_solution(11921032189231666146)
XLA Ops:
  0.0 0.8 pad_maximum_fusion
  0.8 0.7 broadcast_in_dim.34
  1.5 6.0 %all-to-all-start = ((bf16[8,2,4608]{2,1,0:T(2,128)(2,1)}), bf16[8,2,4608]{2,1,0:T(2,128)(2,1)S(1)}, u32[]{:S(2)}, u32[]{:S(2)}) async-start(bf16[8,2,4608]{2,1,0:T(2,128)(2,1)} %broadcast_in_dim.34), calls=%async_computation | async-start | bytes 294912 | tf_op jit(solution)/shard_map/all_to_all | solution.py:192
  7.5 5.4 %all-to-all-done = bf16[8,2,4608]{2,1,0:T(2,128)(2,1)S(1)} async-done(((bf16[8,2,4608]{2,1,0:T(2,128)(2,1)}), bf16[8,2,4608]{2,1,0:T(2,128)(2,1)S(1)}, u32[]{:S(2)}, u32[]{:S(2)}) %all-to-all-start) | async-done | bytes 147488 | tf_op jit(solution)/shard_map/all_to_all | solution.py:192
  13.2 19.0 %all_to_all.45 = bf16[16,8,2304]{2,1,0:T(8,128)(2,1)S(1)} all-to-all(bf16[16,8,2304]{2,1,0:T(8,128)(2,1)S(1)} %broadcast_in_dim.36), channel_id=1, replica_groups=mesh['y_lo'=2,'core'=2,'y_hi'=2,'x'=4,'z'=4] {'x','z'}, dimensions={0} | all-to-all | bytes 1179648 | tf_op jit(solution)/shard_map/all_to_all | solution.py:192
  32.1 1.6 collective-permute-start
  33.8 0.6 broadcast_in_dim.37.gain.pre_gain
  34.4 1.0 collective-permute-done.other
  35.4 0.8 copy-done.3
  36.2 7.6 %shard_map.127 = (bf16[128,2304]{1,0:T(8,128)(2,1)}, bf16[128,288]{1,0:T(8,128)(2,1)}, f32[128,288]{1,0:T(8,128)}, f32[128,288]{1,0:T(8,128)}) custom-call(s32[1]{0:T(128)} %bitcast.core, bf16[128,2304]{1,0:T(8,128)(2,1)} %bitcast.26, bf16[128,2304]{1,0:T(8,128)(2,1)} %copy-done.3, bf16[288,4608]{1,0:T(8,128)(2,1)} %bitcast.19, bf16[288,4608]{1,0:T(8,128)(2,1)} %bitcast.22, ...), custom_call_target="tpu_custom_call" | custom-call | tf_op jit(solution)/shard_map/pallas_call | solution.py:29
  44.2 1.8 collective-permute-done.1.arrived
  46.1 0.8 copy-done.11
  46.9 3.2 %shard_map.128 = bf16[16,8,2304]{2,1,0:T(8,128)(2,1)} custom-call(s32[1]{0:T(128)} %bitcast.core, bf16[128,288]{1,0:T(8,128)(2,1)} %get-tuple-element.14.hidden, bf16[288,4608]{1,0:T(8,128)(2,1)} %w_down.5, bf16[128,2304]{1,0:T(8,128)(2,1)} %copy-done.11), custom_call_target="tpu_custom_call" | custom-call | tf_op jit(solution)/shard_map/pallas_call | solution.py:29
  50.1 16.0 %all_to_all.46.pieces = bf16[16,8,2304]{2,1,0:T(8,128)(2,1)} all-to-all(bf16[16,8,2304]{2,1,0:T(8,128)(2,1)} %shard_map.128), channel_id=1, replica_groups=mesh['y_lo'=2,'core'=2,'y_hi'=2,'x'=4,'z'=4] {'x','z'}, dimensions={0} | all-to-all | bytes 1179648 | tf_op jit(solution)/shard_map/all_to_all | solution.py:192
  66.1 1.9 shard_map.129
  68.0 4.7 %all-to-all-start.3 = ((bf16[8,8,2304]{2,1,0:T(8,128)(2,1)}), bf16[8,8,2304]{2,1,0:T(8,128)(2,1)S(1)}, u32[]{:S(2)}, u32[]{:S(2)}) async-start(bf16[8,8,2304]{2,1,0:T(8,128)(2,1)} %shard_map.129), calls=%async_computation.3 | async-start | bytes 589824 | tf_op jit(solution)/shard_map/all_to_all | solution.py:192
  73.0 0.7 copy.21.answers
  73.7 0.6 broadcast_in_dim.39.post_gain
  74.3 0.6 broadcast_in_dim.38.gain
  74.9 2.2 %shard_map.130.weighted = f32[8,4608]{1,0:T(8,128)} custom-call(s32[8,2]{1,0:T(8,128)} %copy.21.answers, bf16[128,4608]{1,0:T(8,128)(2,1)} %unembed.1, f32[1,4608]{1,0:T(1,128)} %broadcast_in_dim.38.gain), custom_call_target="tpu_custom_call" | custom-call | tf_op jit(solution)/shard_map/pallas_call | solution.py:29
  77.1 0.6 copy.30
  77.8 1.9 all-to-all-done.3.pieces
  79.7 0.7 copy-done.5
  80.4 2.3 %shard_map.131 = (bf16[16,8,2304]{2,1,0:T(8,128)(2,1)}, f32[8,4608]{1,0:T(8,128)}) custom-call(s32[1]{0:T(128)} %bitcast.core, bf16[8,8,2304]{2,1,0:T(8,128)(2,1)} %copy-done.5, bf16[8,4608]{1,0:T(8,128)(2,1)} %bitcast.34, f32[8,4608]{1,0:T(8,128)} %shard_map.130.weighted, f32[1,4608]{1,0:T(1,128)} %broadcast_in_dim.39.post_gain), custom_call_target="tpu_custom_call" | custom-call | tf_op jit(solution)/shard_map/pallas_call | solution.py:29
  82.7 15.7 %all_to_all.47 = bf16[16,8,2304]{2,1,0:T(8,128)(2,1)S(1)} all-to-all(bf16[16,8,2304]{2,1,0:T(8,128)(2,1)} %get-tuple-element.16), channel_id=1, replica_groups=mesh['y_lo'=2,'core'=2,'y_hi'=2,'x'=4,'z'=4] {'x','z'}, dimensions={0} | all-to-all | bytes 1179648 | tf_op jit(solution)/shard_map/all_to_all | solution.py:192
  98.4 1.0 collective-permute-start.2
  99.4 1.6 collective-permute-done.2.other
  101.0 0.8 copy-done.8
  101.9 7.6 %shard_map.132 = (bf16[128,2304]{1,0:T(8,128)(2,1)}, bf16[128,288]{1,0:T(8,128)(2,1)}, bf16[128,288]{1,0:T(8,128)(2,1)}) custom-call(s32[1]{0:T(128)} %bitcast.core, bf16[128,2304]{1,0:T(8,128)(2,1)} %bitcast.31, bf16[128,2304]{1,0:T(8,128)(2,1)} %copy-done.8, f32[128,288]{1,0:T(8,128)} %get-tuple-element.17.gate, f32[128,288]{1,0:T(8,128)} %get-tuple-element.18.up, ...), custom_call_target="tpu_custom_call" | custom-call | tf_op jit(solution)/shard_map/pallas_call | solution.py:29
  109.8 1.8 collective-permute-done.3.arrived
  111.7 0.8 copy-done.10
  112.5 4.4 %shard_map.133 = bf16[16,8,2304]{2,1,0:T(8,128)(2,1)} custom-call(s32[1]{0:T(128)} %bitcast.core, bf16[128,288]{1,0:T(8,128)(2,1)} %get-tuple-element.19.grad_gate, bf16[128,288]{1,0:T(8,128)(2,1)} %get-tuple-element.20.grad_up, bf16[288,4608]{1,0:T(8,128)(2,1)} %bitcast.21, bf16[288,4608]{1,0:T(8,128)(2,1)} %bitcast.24, bf16[128,2304]{1,0:T(8,128)(2,1)} %copy-done.10), custom_call_target="tpu_custom_call" | custom-call | tf_op jit(solution)/shard_map/pallas_call | solution.py:29
  116.9 16.0 %all_to_all.48.pieces = bf16[16,8,2304]{2,1,0:T(8,128)(2,1)} all-to-all(bf16[16,8,2304]{2,1,0:T(8,128)(2,1)} %shard_map.133), channel_id=1, replica_groups=mesh['y_lo'=2,'core'=2,'y_hi'=2,'x'=4,'z'=4] {'x','z'}, dimensions={0} | all-to-all | bytes 1179648 | tf_op jit(solution)/shard_map/all_to_all | solution.py:192
  132.9 1.9 shard_map.134
  134.8 4.7 %all-to-all-start.6 = ((bf16[8,8,2304]{2,1,0:T(8,128)(2,1)}), bf16[8,8,2304]{2,1,0:T(8,128)(2,1)S(1)}, u32[]{:S(2)}, u32[]{:S(2)}) async-start(bf16[8,8,2304]{2,1,0:T(8,128)(2,1)} %shard_map.134), calls=%async_computation.6 | async-start | bytes 589824 | tf_op jit(solution)/shard_map/all_to_all | solution.py:192
  139.6 6.8 %all-to-all-done.6.pieces = bf16[8,8,2304]{2,1,0:T(8,128)(2,1)S(1)} async-done(((bf16[8,8,2304]{2,1,0:T(8,128)(2,1)}), bf16[8,8,2304]{2,1,0:T(8,128)(2,1)S(1)}, u32[]{:S(2)}, u32[]{:S(2)}) %all-to-all-start.6) | async-done | bytes 294944 | tf_op jit(solution)/shard_map/all_to_all | solution.py:192
  146.4 0.9 broadcast_in_dim.41
  147.4 3.6 %all-to-all-start.8 = ((bf16[16,8,2304]{2,1,0:T(8,128)(2,1)}), bf16[16,8,2304]{2,1,0:T(8,128)(2,1)S(1)}, u32[]{:S(2)}, u32[]{:S(2)}) async-start(bf16[16,8,2304]{2,1,0:T(8,128)(2,1)} %broadcast_in_dim.41), calls=%async_computation.8 | async-start | bytes 1179648 | tf_op jit(solution)/shard_map/all_to_all | solution.py:192
  151.0 2.1 %shard_map.135 = bf16[16,8,2304]{2,1,0:T(8,128)(2,1)} custom-call(s32[1]{0:T(128)} %bitcast.core, bf16[8,8,2304]{2,1,0:T(8,128)(2,1)} %copy-done.6, bf16[8,4608]{1,0:T(8,128)(2,1)} %bitcast.35, f32[8,4608]{1,0:T(8,128)} %get-tuple-element.22.grad_output, f32[1,4608]{1,0:T(1,128)} %broadcast_in_dim.37.gain.pre_gain), custom_call_target="tpu_custom_call" | custom-call | tf_op jit(solution)/shard_map/pallas_call | solution.py:29
  153.0 10.0 %all-to-all-done.8 = bf16[16,8,2304]{2,1,0:T(8,128)(2,1)S(1)} async-done(((bf16[16,8,2304]{2,1,0:T(8,128)(2,1)}), bf16[16,8,2304]{2,1,0:T(8,128)(2,1)S(1)}, u32[]{:S(2)}, u32[]{:S(2)}) %all-to-all-start.8) | async-done | bytes 589856 | tf_op jit(solution)/shard_map/all_to_all | solution.py:192
  163.0 3.6 %all-to-all-start.7 = ((bf16[16,8,2304]{2,1,0:T(8,128)(2,1)}), bf16[16,8,2304]{2,1,0:T(8,128)(2,1)S(1)}, u32[]{:S(2)}, u32[]{:S(2)}) async-start(bf16[16,8,2304]{2,1,0:T(8,128)(2,1)} %shard_map.135), calls=%async_computation.7 | async-start | bytes 1179648 | tf_op jit(solution)/shard_map/all_to_all | solution.py:192
  166.6 1.2 collective-permute-start.5
  167.8 9.8 %all-to-all-done.7 = bf16[16,8,2304]{2,1,0:T(8,128)(2,1)S(1)} async-done(((bf16[16,8,2304]{2,1,0:T(8,128)(2,1)}), bf16[16,8,2304]{2,1,0:T(8,128)(2,1)S(1)}, u32[]{:S(2)}, u32[]{:S(2)}) %all-to-all-start.7) | async-done | bytes 589856 | tf_op jit(solution)/shard_map/all_to_all | solution.py:192
  177.5 1.9 collective-permute-start.4
  179.4 0.8 copy-done.9
  180.3 5.2 %shard_map.136.change = f32[128,512]{1,0:T(8,128)} custom-call(s32[1]{0:T(128)} %bitcast.core, bf16[128,2304]{1,0:T(8,128)(2,1)} %bitcast.27, bf16[128,2304]{1,0:T(8,128)(2,1)} %copy-done.3, bf16[128,2304]{1,0:T(8,128)(2,1)} %bitcast.33, bf16[128,2304]{1,0:T(8,128)(2,1)} %copy-done.9, bf16[4608,512]{1,0:T(8,128)(2,1)} %w_enc.1, f32[1,512]{1,0:T(1,128)} %bitcast.38), custom_call_target="tpu_custom_call" | custom-call | tf_op jit(solution)/shard_map/pallas_call | solution.py:29
  185.4 0.8 copy-done.7
  186.2 4.9 %shard_map.137 = f32[1,512]{1,0:T(1,128)} custom-call(s32[1]{0:T(128)} %bitcast.core, bf16[128,2304]{1,0:T(8,128)(2,1)} %bitcast.29, bf16[128,2304]{1,0:T(8,128)(2,1)} %copy-done.7, bf16[512,4608]{1,0:T(8,128)(2,1)} %w_dec.1, f32[128,512]{1,0:T(8,128)} %shard_map.136.change), custom_call_target="tpu_custom_call" | custom-call | tf_op jit(solution)/shard_map/pallas_call | solution.py:29
  (38 shorter events, 1.4 us)
Async XLA Ops:
  0.0 33.8 %copy-start.12 = (f32[4608]{0:T(1024)S(1)}, f32[4608]{0:T(1024)}, u32[]{:S(2)}) copy-start(f32[4608]{0:T(1024)} %param.17) | copy-start | bytes 55300
  1.5 11.4 %all-to-all-start = ((bf16[8,2,4608]{2,1,0:T(2,128)(2,1)}), bf16[8,2,4608]{2,1,0:T(2,128)(2,1)S(1)}, u32[]{:S(2)}, u32[]{:S(2)}) async-start(bf16[8,2,4608]{2,1,0:T(2,128)(2,1)} %broadcast_in_dim.34), calls=%async_computation | async-start | bytes 294912 | tf_op jit(solution)/shard_map/all_to_all | solution.py:192
  32.1 3.3 %copy-start = (bf16[16,8,2304]{2,1,0:T(8,128)(2,1)}, bf16[16,8,2304]{2,1,0:T(8,128)(2,1)S(1)}, u32[]{:S(2)}) copy-start(bf16[16,8,2304]{2,1,0:T(8,128)(2,1)S(1)} %all_to_all.45) | copy-start | bytes 1769476
  32.1 3.3 %collective-permute-start = (bf16[128,2304]{1,0:T(8,128)(2,1)S(1)}, bf16[128,2304]{1,0:T(8,128)(2,1)S(1)}, u32[]{:S(2)}, u32[]{:S(2)}) collective-permute-start(bf16[128,2304]{1,0:T(8,128)(2,1)S(1)} %bitcast.25), channel_id=1, source_target_pairs={{0,32},{32,0},{1,33},{33,1},{2,34},{34,2},{3,35},{35,3},{4,36},{36... | collective-permute-start | bytes 1769480 | tf_op jit(solution)/shard_map/ppermute | solution.py:196
  35.4 0.8 copy-start.3
  43.9 2.2 %collective-permute-start.1 = (bf16[128,2304]{1,0:T(8,128)(2,1)}, bf16[128,2304]{1,0:T(8,128)(2,1)S(1)}, u32[]{:S(2)}, u32[]{:S(2)}) collective-permute-start(bf16[128,2304]{1,0:T(8,128)(2,1)} %get-tuple-element.15), channel_id=1, source_target_pairs={{0,32},{32,0},{1,33},{33,1},{2,34},{34,2},{3,35},{35,3},{4,36},{36... | collective-permute-start | bytes 1769480 | tf_op jit(solution)/shard_map/ppermute | solution.py:196
  46.1 0.8 copy-start.11
  46.9 25.8 %copy-start.15 = (s32[128,2]{0,1:T(2,128)S(1)}, s32[128,2]{0,1:T(2,128)}, u32[]{:S(2)}) copy-start(s32[128,2]{0,1:T(2,128)} %param.15) | copy-start | bytes 3076
  46.9 26.8 %copy-start.13 = (f32[4608]{0:T(1024)S(1)}, f32[4608]{0:T(1024)}, u32[]{:S(2)}) copy-start(f32[4608]{0:T(1024)} %param.18) | copy-start | bytes 55300
  46.9 27.4 %copy-start.14 = (f32[4608]{0:T(1024)S(1)}, f32[4608]{0:T(1024)}, u32[]{:S(2)}) copy-start(f32[4608]{0:T(1024)} %param.19) | copy-start | bytes 55300
  68.0 11.7 %all-to-all-start.3 = ((bf16[8,8,2304]{2,1,0:T(8,128)(2,1)}), bf16[8,8,2304]{2,1,0:T(8,128)(2,1)S(1)}, u32[]{:S(2)}, u32[]{:S(2)}) async-start(bf16[8,8,2304]{2,1,0:T(8,128)(2,1)} %shard_map.129), calls=%async_computation.3 | async-start | bytes 589824 | tf_op jit(solution)/shard_map/all_to_all | solution.py:192
  79.7 0.7 copy-start.5
  98.4 2.6 %copy-start.2 = (bf16[16,8,2304]{2,1,0:T(8,128)(2,1)}, bf16[16,8,2304]{2,1,0:T(8,128)(2,1)S(1)}, u32[]{:S(2)}) copy-start(bf16[16,8,2304]{2,1,0:T(8,128)(2,1)S(1)} %all_to_all.47) | copy-start | bytes 1769476
  98.4 2.6 %collective-permute-start.2 = (bf16[128,2304]{1,0:T(8,128)(2,1)S(1)}, bf16[128,2304]{1,0:T(8,128)(2,1)S(1)}, u32[]{:S(2)}, u32[]{:S(2)}) collective-permute-start(bf16[128,2304]{1,0:T(8,128)(2,1)S(1)} %bitcast.30), channel_id=1, source_target_pairs={{0,32},{32,0},{1,33},{33,1},{2,34},{34,2},{3,35},{35,3},{4,36},{36... | collective-permute-start | bytes 1769480 | tf_op jit(solution)/shard_map/ppermute | solution.py:196
  101.0 0.8 copy-start.8
  109.5 2.2 %collective-permute-start.3 = (bf16[128,2304]{1,0:T(8,128)(2,1)}, bf16[128,2304]{1,0:T(8,128)(2,1)S(1)}, u32[]{:S(2)}, u32[]{:S(2)}) collective-permute-start(bf16[128,2304]{1,0:T(8,128)(2,1)} %get-tuple-element.21), channel_id=1, source_target_pairs={{0,32},{32,0},{1,33},{33,1},{2,34},{34,2},{3,35},{35,3},{4,36},{36... | collective-permute-start | bytes 1769480 | tf_op jit(solution)/shard_map/ppermute | solution.py:196
  111.7 0.8 copy-start.10
  134.8 11.7 %all-to-all-start.6 = ((bf16[8,8,2304]{2,1,0:T(8,128)(2,1)}), bf16[8,8,2304]{2,1,0:T(8,128)(2,1)S(1)}, u32[]{:S(2)}, u32[]{:S(2)}) async-start(bf16[8,8,2304]{2,1,0:T(8,128)(2,1)} %shard_map.134), calls=%async_computation.6 | async-start | bytes 589824 | tf_op jit(solution)/shard_map/all_to_all | solution.py:192
  146.4 4.5 %copy-start.6 = (bf16[8,8,2304]{2,1,0:T(8,128)(2,1)}, bf16[8,8,2304]{2,1,0:T(8,128)(2,1)S(1)}, u32[]{:S(2)}) copy-start(bf16[8,8,2304]{2,1,0:T(8,128)(2,1)S(1)} %all-to-all-done.6.pieces) | copy-start | bytes 884740
  147.4 15.7 %all-to-all-start.8 = ((bf16[16,8,2304]{2,1,0:T(8,128)(2,1)}), bf16[16,8,2304]{2,1,0:T(8,128)(2,1)S(1)}, u32[]{:S(2)}, u32[]{:S(2)}) async-start(bf16[16,8,2304]{2,1,0:T(8,128)(2,1)} %broadcast_in_dim.41), calls=%async_computation.8 | async-start | bytes 1179648 | tf_op jit(solution)/shard_map/all_to_all | solution.py:192
  163.0 16.4 %copy-start.4 = (bf16[16,8,2304]{2,1,0:T(8,128)(2,1)}, bf16[16,8,2304]{2,1,0:T(8,128)(2,1)S(1)}, u32[]{:S(2)}) copy-start(bf16[16,8,2304]{2,1,0:T(8,128)(2,1)S(1)} %all-to-all-done.8) | copy-start | bytes 1769476
  163.0 14.5 %all-to-all-start.7 = ((bf16[16,8,2304]{2,1,0:T(8,128)(2,1)}), bf16[16,8,2304]{2,1,0:T(8,128)(2,1)S(1)}, u32[]{:S(2)}, u32[]{:S(2)}) async-start(bf16[16,8,2304]{2,1,0:T(8,128)(2,1)} %shard_map.135), calls=%async_computation.7 | async-start | bytes 1179648 | tf_op jit(solution)/shard_map/all_to_all | solution.py:192
  166.6 12.8 %collective-permute-start.5 = (bf16[128,2304]{1,0:T(8,128)(2,1)S(1)}, bf16[128,2304]{1,0:T(8,128)(2,1)S(1)}, u32[]{:S(2)}, u32[]{:S(2)}) collective-permute-start(bf16[128,2304]{1,0:T(8,128)(2,1)S(1)} %bitcast.32), channel_id=1, source_target_pairs={{0,32},{32,0},{1,33},{33,1},{2,34},{34,2},{3,35},{35,3},{4,36},{36... | collective-permute-start | bytes 1769480 | tf_op jit(solution)/shard_map/ppermute | solution.py:196
  177.5 7.9 %copy-start.1 = (bf16[16,8,2304]{2,1,0:T(8,128)(2,1)}, bf16[16,8,2304]{2,1,0:T(8,128)(2,1)S(1)}, u32[]{:S(2)}) copy-start(bf16[16,8,2304]{2,1,0:T(8,128)(2,1)S(1)} %all-to-all-done.7) | copy-start | bytes 1769476
  177.5 7.9 %collective-permute-start.4 = (bf16[128,2304]{1,0:T(8,128)(2,1)S(1)}, bf16[128,2304]{1,0:T(8,128)(2,1)S(1)}, u32[]{:S(2)}, u32[]{:S(2)}) collective-permute-start(bf16[128,2304]{1,0:T(8,128)(2,1)S(1)} %bitcast.28), channel_id=1, source_target_pairs={{0,32},{32,0},{1,33},{33,1},{2,34},{34,2},{3,35},{35,3},{4,36},{36... | collective-permute-start | bytes 1769480 | tf_op jit(solution)/shard_map/ppermute | solution.py:196
  179.4 0.8 copy-start.9
  185.4 0.8 copy-start.7
where the time goes:
time: 192 us; the launch traced here: 191 us
  blocking collectives  66.6 us (35%)
  Pallas kernels  43.3 us (23%)
  waiting for transfers between devices  40.2 us (21%)
  starting transfers between devices  29 us (15%)
  local copies, waits for them, and re-layouts  11.1 us (6%)
    all_to_all x4, blocking collectives, exchanged(): return lax.all_to_all(blocks, axes, 0, 0, tiled=True)  66.6 us
    pallas_call x11, Pallas kernels, call(): pl.pallas_call(kernel, out_shape=outs, in_specs=specs, out_specs=jax.tree...  43.3 us
    all_to_all x5, waiting for transfers between devices, exchanged(): return lax.all_to_all(blocks, axes, 0, 0, tiled=True)  33.8 us
    all_to_all x5, starting transfers between devices, exchanged(): return lax.all_to_all(blocks, axes, 0, 0, tiled=True)  22.6 us
    unnamed x36, local copies, waits for them, and re-layouts  6.44 us
    ppermute x6, starting transfers between devices, swapped(): return lax.ppermute(value, 'core', SWAP)  6.42 us
    ppermute x6, waiting for transfers between devices, swapped(): return lax.ppermute(value, 'core', SWAP)  6.34 us
  transfers between devices with their start and end apart: 11, of which 9 were waited for; matrix products, arithmetic and copies ran while one was open for 2% of the time, Pallas kernels for 5%

commit v1 on v0

v1 whole, which is shorter than its diff:
```python
import jax
import jax.numpy as jnp
from jax import lax
from jax.experimental import pallas as pl
from jax.experimental.pallas import tpu as pltpu
from jax.sharding import Mesh
from jax.sharding import PartitionSpec as P

epsilon = 1e-06
gelu_scale = 0.7978845608028654
gelu_cubic = 0.044715

DEVICES = ("y_lo", "core", "y_hi", "x", "z")
CHIPS = ("x", "z", "y_lo", "y_hi")
SWAP = [(0, 1), (1, 0)]
F32 = jnp.float32
BF16 = jnp.bfloat16
VMEM = pl.BlockSpec(memory_space=pltpu.VMEM)
SMEM = pl.BlockSpec(memory_space=pltpu.SMEM)


def shape(dims, dtype):
    return jax.ShapeDtypeStruct(dims, dtype)


def call(kernel, outs, *args, space=pltpu.VMEM, scratch=()):
    return pl.pallas_call(
        kernel,
        out_shape=jax.tree.map(lambda o: space(o.shape, o.dtype), outs),
        in_specs=[SMEM if a.dtype == jnp.int32 else VMEM for a in args],
        out_specs=jax.tree.map(lambda _: VMEM, outs),
        scratch_shapes=scratch,
        compiler_params=pltpu.CompilerParams(vmem_limit_bytes=8 << 20),
    )(
        *(
            a if a.dtype == jnp.int32 else pltpu.with_memory_space_constraint(a, pltpu.VMEM)
            for a in args
        )
    )


def gelu_tanh(value):
    return 0.5 * value * (1.0 + jnp.tanh(gelu_scale * (value + gelu_cubic * value * value * value)))


def gelu_slope(value):
    inner = jnp.tanh(gelu_scale * (value + gelu_cubic * value * value * value))
    return 0.5 * (1.0 + inner) + 0.5 * value * (1.0 - inner * inner) * gelu_scale * (
        1.0 + 3.0 * gelu_cubic * value * value
    )


def dot_nn(left, right):
    return jnp.dot(left, right, preferred_element_type=F32)


def dot_nt(left, right):
    return lax.dot_general(left, right, (((1,), (1,)), ((), ())), preferred_element_type=F32)


def mean_row(value):
    return jnp.mean(value, axis=-1, keepdims=True)


def halves(core_ref, width):
    core = core_ref[0]
    return (
        pl.ds(pl.multiple_of(core * width, 128), width),
        pl.ds(pl.multiple_of((1 - core) * width, 128), width),
    )


def merge_kernel(clean, corrupt, out):
    out[0:1] = clean[...]
    out[1:2] = corrupt[...]


def spread(value, out):
    for chip in range(out.shape[0]):
        out[chip] = value


def chip_rows_kernel(where, both, partner, out, stream):
    first = where[0] == 0
    mine, _ = halves(where, out.shape[2])
    a, b = both[...].astype(F32), partner[...].astype(F32)
    low, high = jnp.where(first, a, b), jnp.where(first, b, a)
    stream[0:1] = low[0:1]
    stream[1:2] = high[0:1]
    a, b = both[:, mine].astype(F32), partner[:, mine].astype(F32)
    low, high = jnp.where(first, a, b), jnp.where(first, b, a)
    quad = jnp.concatenate([low[0:1], high[0:1], low[1:2], high[1:2]], axis=0)
    spread(quad.astype(BF16), out)


def rows_kernel(pieces, clean, corrupt):
    clean[...] = pieces[:, :2].reshape(clean.shape)
    corrupt[...] = pieces[:, 2:].reshape(corrupt.shape)


def forward_kernel(where, own, other, w_gate, w_up, w_down, gain, send, hidden, gate, up, normed):
    width = own.shape[1]
    mine, theirs = halves(where, width)
    a, b = own[...].astype(F32), other[...].astype(F32)
    total = jnp.sum(a * a, axis=-1, keepdims=True) + jnp.sum(b * b, axis=-1, keepdims=True)
    inv = lax.rsqrt(total / (2 * width) + epsilon)
    normed[:, mine] = (a * inv * gain[:, mine]).astype(BF16)
    normed[:, theirs] = (b * inv * gain[:, theirs]).astype(BF16)
    gate_pre = dot_nt(normed[...], w_gate[...])
    up_proj = dot_nt(normed[...], w_up[...])
    gate[...] = gate_pre
    up[...] = up_proj
    act = (gelu_tanh(gate_pre) * up_proj).astype(BF16)
    hidden[...] = act
    send[...] = dot_nn(act, w_down[:, theirs]).astype(BF16)


def forward_own_kernel(where, hidden, w_down, out):
    mine, _ = halves(where, out.shape[1])
    out[...] = dot_nn(hidden[...], w_down[:, mine])


def chip_sum_kernel(own, arrived, out):
    out[...] = (own[...] + arrived[...].astype(F32)).astype(BF16).reshape(out.shape)


def total_kernel(pieces, out):
    rows = pieces.shape[0] * pieces.shape[1]
    token = lax.broadcasted_iota(jnp.int32, (8, rows), 0)
    source = lax.broadcasted_iota(jnp.int32, (8, rows), 1)
    pick = (source % 2 == token).astype(F32).astype(BF16)
    out[...] = dot_nn(pick, pieces[...].reshape(rows, out.shape[1]))[: out.shape[0]]


def joined(where, own, other, out):
    mine, theirs = halves(where, own.shape[1])
    out[:, mine] = own[...]
    out[:, theirs] = other[...]
    return out[...]


def wanted_rows(where, answers, unembed, gain):
    lanes = lax.broadcasted_iota(jnp.int32, (1, unembed.shape[0]), 1)
    rows = []
    for core in range(2):
        token = where[1 + core]
        rows.append(
            (lanes == answers[0, token]).astype(F32) - (lanes == answers[1, token]).astype(F32)
        )
    selector = jnp.concatenate(rows + rows + rows + rows, axis=0).astype(BF16)
    return gain[...] * dot_nn(selector, unembed[...])[:2]


def output_kernel(
    where,
    answers,
    own,
    other,
    stream,
    unembed,
    final_gain,
    post_gain,
    out,
    grad_output,
    whole,
):
    mine, _ = halves(where, out.shape[2])
    mlp_out = joined(where, own, other, whole)
    inv_post = lax.rsqrt(mean_row(mlp_out * mlp_out) + epsilon)
    output = stream[...] + mlp_out * inv_post * post_gain[...]
    inv_final = lax.rsqrt(mean_row(output * output) + epsilon)
    wanted = wanted_rows(where, answers, unembed, final_gain)
    grad_out = inv_final * wanted - output * (inv_final * inv_final * inv_final) * mean_row(
        wanted * output
    )
    grad_output[...] = grad_out
    post_grad = post_gain[...] * grad_out
    whole[...] = inv_post * post_grad - mlp_out * (inv_post * inv_post * inv_post) * mean_row(
        post_grad * mlp_out
    )
    spread(whole[:, mine].astype(BF16), out)


def backward_own_half_kernel(where, own, w_down, out):
    mine, _ = halves(where, own.shape[2])
    out[...] = dot_nt(own[...].reshape(out.shape[0], own.shape[2]), w_down[:, mine])


def backward_kernel(
    where, own_part, other, gate, up, w_gate, w_up, w_down, send, grad_gate, grad_up
):
    width = other.shape[2]
    _, theirs = halves(where, width)
    grad_hidden = own_part[...] + dot_nt(
        other[...].reshape(own_part.shape[0], width), w_down[:, theirs]
    )
    gate_pre = gate[...]
    to_gate = (grad_hidden * up[...] * gelu_slope(gate_pre)).astype(BF16)
    to_up = (grad_hidden * gelu_tanh(gate_pre)).astype(BF16)
    grad_gate[...] = to_gate
    grad_up[...] = to_up
    send[...] = (dot_nn(to_gate, w_gate[:, theirs]) + dot_nn(to_up, w_up[:, theirs])).astype(BF16)


def backward_own_kernel(where, grad_gate, grad_up, w_gate, w_up, out):
    mine, _ = halves(where, out.shape[1])
    out[...] = dot_nn(grad_gate[...], w_gate[:, mine]) + dot_nn(grad_up[...], w_up[:, mine])


def input_kernel(where, own, other, stream, grad_output, pre_gain, out, whole):
    mine, _ = halves(where, out.shape[2])
    rows = stream[...]
    inv_pre = lax.rsqrt(mean_row(rows * rows) + epsilon)
    pre_grad = pre_gain[...] * joined(where, own, other, whole)
    whole[...] = (
        grad_output[...]
        + inv_pre * pre_grad
        - rows * (inv_pre * inv_pre * inv_pre) * mean_row(pre_grad * rows)
    )
    spread(whole[:, mine].astype(BF16), out)


def code_of(where, own, other, w_enc, b_enc):
    first, second = halves(where, own.shape[1])
    return jax.nn.relu(
        dot_nn(own[...], w_enc[first, :]) + dot_nn(other[...], w_enc[second, :]) + b_enc[...]
    )


def code_kernel(where, own, other, w_enc, b_enc, out):
    out[...] = code_of(where, own, other, w_enc, b_enc)


def change_kernel(where, own, other, w_enc, b_enc, clean_code, out):
    out[...] = clean_code[...] - code_of(where, own, other, w_enc, b_enc)


def attribution_own_kernel(where, own, w_dec, out):
    mine, _ = halves(where, own.shape[2])
    out[...] = dot_nt(own[...].reshape(out.shape[0], own.shape[2]), w_dec[:, mine])


def attribution_kernel(where, part, other, w_dec, change, out):
    width = other.shape[2]
    _, theirs = halves(where, width)
    projected = part[...] + dot_nt(other[...].reshape(part.shape[0], width), w_dec[:, theirs])
    out[...] = jnp.sum(change[...] * projected, axis=0, keepdims=True)


def exchanged(blocks):
    return lax.all_to_all(blocks, CHIPS, 0, 0, tiled=True)


def swapped(value):
    return lax.ppermute(value, "core", SWAP)


def local(
    resid_clean,
    resid_corrupt,
    answer_ids,
    unembed,
    pre_gain,
    post_gain,
    final_gain,
    w_gate,
    w_up,
    w_down,
    w_enc,
    b_enc,
    w_dec,
):
    width = resid_clean.shape[1]
    half = width // 2
    chips, plane = lax.axis_size(CHIPS), lax.axis_size(("x", "z"))
    tokens = 2 * chips
    core_index = lax.axis_index("core")
    pair = (
        lax.axis_index("y_lo") * (4 * plane)
        + lax.axis_index("y_hi") * plane
        + lax.axis_index(("x", "z"))
    )
    where = jnp.stack([core_index, pair, pair + 2 * plane]).astype(jnp.int32)
    hidden_units, latents = w_gate.shape[1], w_enc.shape[1]
    w_gate, w_up = w_gate.T, w_up.T
    gains = (g[None] for g in (pre_gain, post_gain, final_gain))
    b_enc = b_enc[None]

    halved = shape((tokens, half), BF16)
    halved32 = shape((tokens, half), F32)
    pairs = shape((chips, 2, half), BF16)
    pair_rows = shape((2, width), F32)
    pair_half = shape((2, half), F32)
    units = shape((tokens, hidden_units), BF16)
    units32 = shape((tokens, hidden_units), F32)
    codes = shape((tokens, latents), F32)
    whole = pltpu.VMEM((2, width), F32)

    both = call(merge_kernel, shape((2, width), BF16), resid_clean, resid_corrupt)
    partner = swapped(both)
    partner, where, pre_gain, post_gain, final_gain = lax.optimization_barrier(
        (partner, where, *gains)
    )
    quads, stream = call(
        chip_rows_kernel, (shape((chips, 4, half), BF16), pair_rows), where, both, partner
    )
    own, own_corrupt = call(rows_kernel, (halved, halved), exchanged(quads))
    other = swapped(own)
    other, own_corrupt = lax.optimization_barrier((other, own_corrupt))
    other_corrupt = swapped(own_corrupt)

    sent, hidden, gate, up = call(
        forward_kernel,
        (halved, units, units32, units32),
        where, own, other, w_gate, w_up, w_down, pre_gain,
        scratch=[pltpu.VMEM((tokens, width), BF16)],
    )
    sent, other_corrupt = lax.optimization_barrier((sent, other_corrupt))
    arrived = swapped(sent)
    own_sum = call(forward_own_kernel, halved32, where, hidden, w_down)
    own_sum, own, other = lax.optimization_barrier((own_sum, own, other))
    clean_code = call(code_kernel, codes, where, own, other, w_enc, b_enc)
    arrived, own_sum, clean_code = lax.optimization_barrier((arrived, own_sum, clean_code))
    own_mlp = call(
        total_kernel, pair_half, exchanged(call(chip_sum_kernel, pairs, own_sum, arrived))
    )
    own_mlp, own_corrupt = lax.optimization_barrier((own_mlp, own_corrupt))
    other_mlp = swapped(own_mlp)
    change = call(
        change_kernel, codes, where, own_corrupt, other_corrupt, w_enc, b_enc, clean_code
    )
    other_mlp, change = lax.optimization_barrier((other_mlp, change))
    spread_grad, grad_output = call(
        output_kernel,
        (pairs, pair_rows),
        where, answer_ids.T, own_mlp, other_mlp, stream, unembed, final_gain, post_gain,
        scratch=[whole],
    )

    grad_own = exchanged(spread_grad)
    grad_other = swapped(grad_own)
    own_part = call(backward_own_half_kernel, units32, where, grad_own, w_down)
    grad_other, own_part = lax.optimization_barrier((grad_other, own_part))
    sent, grad_gate, grad_up = call(
        backward_kernel,
        (halved, units, units),
        where, own_part, grad_other, gate, up, w_gate, w_up, w_down,
    )
    arrived = swapped(sent)
    own_sum = call(backward_own_kernel, halved32, where, grad_gate, grad_up, w_gate, w_up)
    arrived, own_sum = lax.optimization_barrier((arrived, own_sum))
    own_normed = call(
        total_kernel, pair_half, exchanged(call(chip_sum_kernel, pairs, own_sum, arrived))
    )
    spread_stream = call(
        input_kernel,
        pairs,
        where, own_normed, swapped(own_normed), stream, grad_output, pre_gain,
        scratch=[whole],
    )

    last_own = exchanged(spread_stream)
    last_other = swapped(last_own)
    own_part = call(attribution_own_kernel, codes, where, last_own, w_dec)
    last_other, own_part = lax.optimization_barrier((last_other, own_part))
    return call(
        attribution_kernel,
        shape((1, latents), F32),
        where, own_part, last_other, w_dec, change,
        space=jax.ShapeDtypeStruct,
    )


def solution(mesh):
    fine = Mesh(mesh.devices.reshape(2, 2, 2, 4, 4), DEVICES)
    return jax.shard_map(
        local,
        mesh=fine,
        in_specs=(
            P(DEVICES, None),
            P(DEVICES, None),
            P(),
            P(),
            P(),
            P(),
            P(),
            P(None, DEVICES),
            P(None, DEVICES),
            P(DEVICES, None),
            P(None, DEVICES),
            P(DEVICES),
            P(DEVICES, None),
        ),
        out_specs=P(None, DEVICES),
        check_vma=False,
    )
```

time: 192 us -> 144 us (0.75)
  waiting for transfers between devices: 40.2 us -> 3.39 us
  blocking collectives: 66.6 us -> 102 us
  Pallas kernels: 43.3 us -> 19.6 us
  starting transfers between devices: 29 us -> 11.5 us
  local copies, waits for them, and re-layouts: 11.1 us -> 7.36 us
    all_to_all x4 -> x5, blocking collectives: 66.6 us -> 102 us  [exchanged(): return lax.all_to_all(blocks, CHIPS, 0, 0, tiled=True)]
    all_to_all x5 -> x0, waiting for transfers between devices: 33.8 us -> none  [exchanged(): return lax.all_to_all(blocks, axes, 0, 0, tiled=True)]
    pallas_call x11 -> x18, Pallas kernels: 43.3 us -> 19.6 us  [call(): pl.pallas_call(kernel, out_shape=jax.tree.map(lambda o: space(o.shape, o....]
    all_to_all x5 -> x0, starting transfers between devices: 22.6 us -> none  [exchanged(): return lax.all_to_all(blocks, axes, 0, 0, tiled=True)]
    ppermute x6 -> x9, starting transfers between devices: 6.42 us -> 11.5 us  [swapped(): return lax.ppermute(value, 'core', SWAP)]
    ppermute x6 -> x9, waiting for transfers between devices: 6.34 us -> 3.39 us  [swapped(): return lax.ppermute(value, 'core', SWAP)]
    unnamed x36 -> x26, local copies, waits for them, and re-layouts: 6.44 us -> 5.13 us
  transfers between devices with their start and end apart: 11 -> 9, of which waited for: 9 -> 5; matrix products, arithmetic and copies ran while one was open for 2% -> 2% of each run, Pallas kernels for 5% -> 8%
where the time goes in v1:
time: 144 us
  blocking collectives  102 us (71%)
  Pallas kernels  19.6 us (14%)
  starting transfers between devices  11.5 us (8%)
  local copies, waits for them, and re-layouts  7.36 us (5%)
  waiting for transfers between devices  3.39 us (2%)
    all_to_all x5, blocking collectives, exchanged(): return lax.all_to_all(blocks, CHIPS, 0, 0, tiled=True)  102 us
    pallas_call x18, Pallas kernels, call(): pl.pallas_call(kernel, out_shape=jax.tree.map(lambda o: space(o.shape, o....  19.6 us
    ppermute x9, starting transfers between devices, swapped(): return lax.ppermute(value, 'core', SWAP)  11.5 us
    unnamed x26, local copies, waits for them, and re-layouts  5.13 us
    ppermute x9, waiting for transfers between devices, swapped(): return lax.ppermute(value, 'core', SWAP)  3.39 us
  transfers between devices with their start and end apart: 9, of which 5 were waited for; matrix products, arithmetic and copies ran while one was open for 2% of the time, Pallas kernels for 8%

profile of v1, /device:TPU:1, one launch (start us, length us, event | category | flops | bytes accessed | tf_op | source)
XLA Modules:
  0.0 143.7 jit_solution(6714008726614734358)
XLA Ops:
  0.0 0.9 copy-done.7
  0.9 0.7 copy-done.8
  1.6 1.5 %collective-permute-start = (bf16[2,4608]{1,0:T(2,128)(2,1)S(1)}, bf16[2,4608]{1,0:T(2,128)(2,1)S(1)}, u32[]{:S(2)}, u32[]{:S(2)}) collective-permute-start(bf16[2,4608]{1,0:T(2,128)(2,1)S(1)} %shard_map.127.both), channel_id=1, source_target_pairs={{0,32},{32,0},{1,33},{33,1},{2,34},{34,2},{3,35},{35,3},{4,36},{36... | collective-permute-start | bytes 55304 | tf_op jit(solution)/shard_map/ppermute | solution.py:255
  3.1 0.1 pad_add_fusion.where
  3.2 0.7 broadcast_in_dim.12.gain.pre_gain
  3.9 0.7 broadcast_in_dim.13.post_gain
  4.6 0.7 broadcast_in_dim.14.final_gain
  5.4 0.0 collective-permute-done.partner
  5.4 0.7 shard_map.128
  6.1 30.5 %all_to_all.25.pieces = bf16[64,4,2304]{2,1,0:T(4,128)(2,1)S(1)} all-to-all(bf16[64,4,2304]{2,1,0:T(4,128)(2,1)S(1)} %get-tuple-element.45), channel_id=1, replica_groups=mesh['y_lo'=2,'core'=2,'y_hi'=2,'x'=4,'z'=4] {'x','z','y_lo','y_hi'}, dimensions={0} | all-to-all | bytes 2359296 | tf_op jit(solution)/shard_map/all_to_all | solution.py:251
  36.6 0.4 shard_map.129
  37.0 1.7 %collective-permute-start.1 = (bf16[128,2304]{1,0:T(8,128)(2,1)S(1)}, bf16[128,2304]{1,0:T(8,128)(2,1)S(1)}, u32[]{:S(2)}, u32[]{:S(2)}) collective-permute-start(bf16[128,2304]{1,0:T(8,128)(2,1)S(1)} %get-tuple-element.55.own), channel_id=1, source_target_pairs={{0,32},{32,0},{1,33},{33,1},{2,34},{34,2},{3,35},{35,3},{4,36},{36... | collective-permute-start | bytes 1769480 | tf_op jit(solution)/shard_map/ppermute | solution.py:255
  38.8 1.6 %collective-permute-done.1.other = bf16[128,2304]{1,0:T(8,128)(2,1)S(1)} collective-permute-done((bf16[128,2304]{1,0:T(8,128)(2,1)S(1)}, bf16[128,2304]{1,0:T(8,128)(2,1)S(1)}, u32[]{:S(2)}, u32[]{:S(2)}) %collective-permute-start.1) | collective-permute-done | bytes 589856 | tf_op jit(solution)/shard_map/ppermute | solution.py:255
  40.4 0.4 collective-permute-start.2
  40.8 1.7 %copy-done.1 = bf16[4608,288]{0,1:T(8,128)(2,1)S(1)} copy-done((bf16[4608,288]{0,1:T(8,128)(2,1)S(1)}, bf16[4608,288]{0,1:T(8,128)(2,1)}, u32[]{:S(2)}) %copy-start.1) | copy-done | bytes 2654232
  42.5 1.7 %copy-done.3 = bf16[4608,288]{0,1:T(8,128)(2,1)S(1)} copy-done((bf16[4608,288]{0,1:T(8,128)(2,1)S(1)}, bf16[4608,288]{0,1:T(8,128)(2,1)}, u32[]{:S(2)}) %copy-start.3) | copy-done | bytes 2654232
  44.3 3.6 %shard_map.130 = (bf16[128,2304]{1,0:T(8,128)(2,1)S(1)}, bf16[128,288]{1,0:T(8,128)(2,1)S(1)}, f32[128,288]{1,0:T(8,128)S(1)}, f32[128,288]{1,0:T(8,128)S(1)}) custom-call(s32[3]{0:T(128)S(1)} %pad_add_fusion.where, bf16[128,2304]{1,0:T(8,128)(2,1)S(1)} %get-tuple-element.55.own, bf16[128,2304]{1,0:T(8,128)(2,1)S(1)} %collective-permute-done.1.other, ...), custom_call_target="tpu_custom_call" | custom-call | tf_op jit(solution)/shard_map/pallas_call | solution.py:27
  47.9 0.0 copy-start.9
  47.9 0.2 collective-permute-start.3
  48.2 1.0 shard_map.131.own
  49.2 1.3 shard_map.132.clean_code
  50.5 0.2 shard_map.133
  50.7 17.6 %all_to_all.26.pieces = bf16[64,2,2304]{2,1,0:T(2,128)(2,1)S(1)} all-to-all(bf16[64,2,2304]{2,1,0:T(2,128)(2,1)S(1)} %shard_map.133), channel_id=1, replica_groups=mesh['y_lo'=2,'core'=2,'y_hi'=2,'x'=4,'z'=4] {'x','z','y_lo','y_hi'}, dimensions={0} | all-to-all | bytes 1179648 | tf_op jit(solution)/shard_map/all_to_all | solution.py:251
  68.3 0.2 shard_map.134.own
  68.6 1.9 %collective-permute-start.4 = (f32[2,2304]{1,0:T(2,128)S(1)}, f32[2,2304]{1,0:T(2,128)S(1)}, u32[]{:S(2)}, u32[]{:S(2)}) collective-permute-start(f32[2,2304]{1,0:T(2,128)S(1)} %shard_map.134.own), channel_id=1, source_target_pairs={{0,32},{32,0},{1,33},{33,1},{2,34},{34,2},{3,35},{35,3},{4,36},{36... | collective-permute-start | bytes 55304 | tf_op jit(solution)/shard_map/ppermute | solution.py:255
  70.5 1.3 shard_map.135.change
  71.8 0.0 copy-start.2
  71.9 0.0 copy-start.4
  71.9 1.1 shard_map.136
  73.0 18.1 %all_to_all.27.own = bf16[64,2,2304]{2,1,0:T(2,128)(2,1)S(1)} all-to-all(bf16[64,2,2304]{2,1,0:T(2,128)(2,1)S(1)} %get-tuple-element.67), channel_id=1, replica_groups=mesh['y_lo'=2,'core'=2,'y_hi'=2,'x'=4,'z'=4] {'x','z','y_lo','y_hi'}, dimensions={0} | all-to-all | bytes 1179648 | tf_op jit(solution)/shard_map/all_to_all | solution.py:251
  91.1 1.5 %collective-permute-start.5 = (bf16[64,2,2304]{2,1,0:T(2,128)(2,1)S(1)}, bf16[64,2,2304]{2,1,0:T(2,128)(2,1)S(1)}, u32[]{:S(2)}, u32[]{:S(2)}) collective-permute-start(bf16[64,2,2304]{2,1,0:T(2,128)(2,1)S(1)} %all_to_all.27.own), channel_id=1, source_target_pairs={{0,32},{32,0},{1,33},{33,1},{2,34},{34,2},{3,35},{35,3},{4,36},{36... | collective-permute-start | bytes 1769480 | tf_op jit(solution)/shard_map/ppermute | solution.py:255
  92.6 1.2 shard_map.137.own_part
  93.8 0.4 collective-permute-done.5.other
  94.2 2.5 %shard_map.138 = (bf16[128,2304]{1,0:T(8,128)(2,1)S(1)}, bf16[128,288]{1,0:T(8,128)(2,1)S(1)}, bf16[128,288]{1,0:T(8,128)(2,1)S(1)}) custom-call(s32[3]{0:T(128)S(1)} %pad_add_fusion.where, f32[128,288]{1,0:T(8,128)S(1)} %shard_map.137.own_part, bf16[64,2,2304]{2,1,0:T(2,128)(2,1)S(1)} %collective-permute-done.5.other, ...), custom_call_target="tpu_custom_call" | custom-call | tf_op jit(solution)/shard_map/pallas_call | solution.py:27
  96.8 0.6 collective-permute-start.6
  97.4 1.3 shard_map.139.own
  98.7 0.3 collective-permute-done.6.arrived
  99.0 0.2 shard_map.140
  99.2 17.6 %all_to_all.28.pieces = bf16[64,2,2304]{2,1,0:T(2,128)(2,1)S(1)} all-to-all(bf16[64,2,2304]{2,1,0:T(2,128)(2,1)S(1)} %shard_map.140), channel_id=1, replica_groups=mesh['y_lo'=2,'core'=2,'y_hi'=2,'x'=4,'z'=4] {'x','z','y_lo','y_hi'}, dimensions={0} | all-to-all | bytes 1179648 | tf_op jit(solution)/shard_map/all_to_all | solution.py:251
  116.8 0.2 shard_map.141.own
  117.0 1.9 %collective-permute-start.7 = (f32[2,2304]{1,0:T(2,128)S(1)}, f32[2,2304]{1,0:T(2,128)S(1)}, u32[]{:S(2)}, u32[]{:S(2)}) collective-permute-start(f32[2,2304]{1,0:T(2,128)S(1)} %shard_map.141.own), channel_id=1, source_target_pairs={{0,32},{32,0},{1,33},{33,1},{2,34},{34,2},{3,35},{35,3},{4,36},{36... | collective-permute-start | bytes 55304 | tf_op jit(solution)/shard_map/ppermute | solution.py:255
  119.0 0.8 collective-permute-done.7.other
  119.8 0.8 shard_map.142
  120.6 17.6 %all_to_all.29.own = bf16[64,2,2304]{2,1,0:T(2,128)(2,1)S(1)} all-to-all(bf16[64,2,2304]{2,1,0:T(2,128)(2,1)S(1)} %shard_map.142), channel_id=1, replica_groups=mesh['y_lo'=2,'core'=2,'y_hi'=2,'x'=4,'z'=4] {'x','z','y_lo','y_hi'}, dimensions={0} | all-to-all | bytes 1179648 | tf_op jit(solution)/shard_map/all_to_all | solution.py:251
  138.2 1.8 %collective-permute-start.8 = (bf16[64,2,2304]{2,1,0:T(2,128)(2,1)S(1)}, bf16[64,2,2304]{2,1,0:T(2,128)(2,1)S(1)}, u32[]{:S(2)}, u32[]{:S(2)}) collective-permute-start(bf16[64,2,2304]{2,1,0:T(2,128)(2,1)S(1)} %all_to_all.29.own), channel_id=1, source_target_pairs={{0,32},{32,0},{1,33},{33,1},{2,34},{34,2},{3,35},{35,3},{4,36},{36... | collective-permute-start | bytes 1769480 | tf_op jit(solution)/shard_map/ppermute | solution.py:255
  140.0 1.4 %shard_map.143.part = f32[128,512]{1,0:T(8,128)S(1)} custom-call(s32[3]{0:T(128)S(1)} %pad_add_fusion.where, bf16[64,2,2304]{2,1,0:T(2,128)(2,1)S(1)} %all_to_all.29.own, bf16[512,4608]{1,0:T(8,128)(2,1)S(1)} %bitcast.14), custom_call_target="tpu_custom_call" | custom-call | tf_op jit(solution)/shard_map/pallas_call | solution.py:27
  141.5 0.2 collective-permute-done.8.other
  141.6 2.0 %shard_map.144 = f32[1,512]{1,0:T(1,128)} custom-call(s32[3]{0:T(128)S(1)} %pad_add_fusion.where, f32[128,512]{1,0:T(8,128)S(1)} %shard_map.143.part, bf16[64,2,2304]{2,1,0:T(2,128)(2,1)S(1)} %collective-permute-done.8.other, bf16[512,4608]{1,0:T(8,128)(2,1)S(1)} %bitcast.14, f32[128,512]{1,0:T(8,128)S(1)} %shard_map.135.change), custom_call_target="tpu_custom_call" | custom-call | tf_op jit(solution)/shard_map/pallas_call | solution.py:27
  (24 shorter events, 0.1 us)
Async XLA Ops:
  0.0 40.8 %copy-start = (bf16[288,4608]{1,0:T(8,128)(2,1)S(1)}, bf16[288,4608]{1,0:T(8,128)(2,1)}, u32[]{:S(2)}) copy-start(bf16[288,4608]{1,0:T(8,128)(2,1)} %w_down.7) | copy-start | bytes 7962628
  0.0 0.9 copy-start.7
  0.9 0.7 copy-start.8
  1.6 3.8 %collective-permute-start = (bf16[2,4608]{1,0:T(2,128)(2,1)S(1)}, bf16[2,4608]{1,0:T(2,128)(2,1)S(1)}, u32[]{:S(2)}, u32[]{:S(2)}) collective-permute-start(bf16[2,4608]{1,0:T(2,128)(2,1)S(1)} %shard_map.127.both), channel_id=1, source_target_pairs={{0,32},{32,0},{1,33},{33,1},{2,34},{34,2},{3,35},{35,3},{4,36},{36... | collective-permute-start | bytes 55304 | tf_op jit(solution)/shard_map/ppermute | solution.py:255
  37.0 3.4 %collective-permute-start.1 = (bf16[128,2304]{1,0:T(8,128)(2,1)S(1)}, bf16[128,2304]{1,0:T(8,128)(2,1)S(1)}, u32[]{:S(2)}, u32[]{:S(2)}) collective-permute-start(bf16[128,2304]{1,0:T(8,128)(2,1)S(1)} %get-tuple-element.55.own), channel_id=1, source_target_pairs={{0,32},{32,0},{1,33},{33,1},{2,34},{34,2},{3,35},{35,3},{4,36},{36... | collective-permute-start | bytes 1769480 | tf_op jit(solution)/shard_map/ppermute | solution.py:255
  40.4 7.5 %collective-permute-start.2 = (bf16[128,2304]{1,0:T(8,128)(2,1)S(1)}, bf16[128,2304]{1,0:T(8,128)(2,1)S(1)}, u32[]{:S(2)}, u32[]{:S(2)}) collective-permute-start(bf16[128,2304]{1,0:T(8,128)(2,1)S(1)} %get-tuple-element.60.own), channel_id=1, source_target_pairs={{0,32},{32,0},{1,33},{33,1},{2,34},{34,2},{3,35},{35,3},{4,36},{36... | collective-permute-start | bytes 1769480 | tf_op jit(solution)/shard_map/ppermute | solution.py:255
  40.8 1.8 %copy-start.1 = (bf16[4608,288]{0,1:T(8,128)(2,1)S(1)}, bf16[4608,288]{0,1:T(8,128)(2,1)}, u32[]{:S(2)}) copy-start(bf16[4608,288]{0,1:T(8,128)(2,1)} %param.20) | copy-start | bytes 7962628
  42.5 1.7 %copy-start.3 = (bf16[4608,288]{0,1:T(8,128)(2,1)S(1)}, bf16[4608,288]{0,1:T(8,128)(2,1)}, u32[]{:S(2)}) copy-start(bf16[4608,288]{0,1:T(8,128)(2,1)} %param.21) | copy-start | bytes 7962628
  44.3 4.9 %copy-start.5 = (bf16[4608,512]{1,0:T(8,128)(2,1)S(1)}, bf16[4608,512]{1,0:T(8,128)(2,1)}, u32[]{:S(2)}) copy-start(bf16[4608,512]{1,0:T(8,128)(2,1)} %w_enc.3) | copy-start | bytes 14155780
  47.9 1.3 copy-start.9
  47.9 2.6 %collective-permute-start.3 = (bf16[128,2304]{1,0:T(8,128)(2,1)S(1)}, bf16[128,2304]{1,0:T(8,128)(2,1)S(1)}, u32[]{:S(2)}, u32[]{:S(2)}) collective-permute-start(bf16[128,2304]{1,0:T(8,128)(2,1)S(1)} %get-tuple-element.52), channel_id=1, source_target_pairs={{0,32},{32,0},{1,33},{33,1},{2,34},{34,2},{3,35},{35,3},{4,36},{36... | collective-permute-start | bytes 1769480 | tf_op jit(solution)/shard_map/ppermute | solution.py:255
  68.5 3.3 %copy-start.6 = (bf16[128,4608]{1,0:T(8,128)(2,1)S(1)}, bf16[128,4608]{1,0:T(8,128)(2,1)}, u32[]{:S(2)}) copy-start(bf16[128,4608]{1,0:T(8,128)(2,1)} %unembed.1) | copy-start | bytes 3538948
  68.6 3.3 %copy-start.10 = (s32[128,2]{0,1:T(2,128)S(1)}, s32[128,2]{0,1:T(2,128)}, u32[]{:S(2)}) copy-start(s32[128,2]{0,1:T(2,128)} %param.15) | copy-start | bytes 3076
  68.6 3.3 %collective-permute-start.4 = (f32[2,2304]{1,0:T(2,128)S(1)}, f32[2,2304]{1,0:T(2,128)S(1)}, u32[]{:S(2)}, u32[]{:S(2)}) collective-permute-start(f32[2,2304]{1,0:T(2,128)S(1)} %shard_map.134.own), channel_id=1, source_target_pairs={{0,32},{32,0},{1,33},{33,1},{2,34},{34,2},{3,35},{35,3},{4,36},{36... | collective-permute-start | bytes 55304 | tf_op jit(solution)/shard_map/ppermute | solution.py:255
  71.8 22.4 %copy-start.2 = (bf16[4608,288]{0,1:T(8,128)(2,1)S(1)}, bf16[4608,288]{0,1:T(8,128)(2,1)}, u32[]{:S(2)}) copy-start(bf16[4608,288]{0,1:T(8,128)(2,1)} %param.20) | copy-start | bytes 7962628
  71.9 22.4 %copy-start.4 = (bf16[4608,288]{0,1:T(8,128)(2,1)S(1)}, bf16[4608,288]{0,1:T(8,128)(2,1)}, u32[]{:S(2)}) copy-start(bf16[4608,288]{0,1:T(8,128)(2,1)} %param.21) | copy-start | bytes 7962628
  91.1 3.1 %collective-permute-start.5 = (bf16[64,2,2304]{2,1,0:T(2,128)(2,1)S(1)}, bf16[64,2,2304]{2,1,0:T(2,128)(2,1)S(1)}, u32[]{:S(2)}, u32[]{:S(2)}) collective-permute-start(bf16[64,2,2304]{2,1,0:T(2,128)(2,1)S(1)} %all_to_all.27.own), channel_id=1, source_target_pairs={{0,32},{32,0},{1,33},{33,1},{2,34},{34,2},{3,35},{35,3},{4,36},{36... | collective-permute-start | bytes 1769480 | tf_op jit(solution)/shard_map/ppermute | solution.py:255
  96.8 2.3 %collective-permute-start.6 = (bf16[128,2304]{1,0:T(8,128)(2,1)S(1)}, bf16[128,2304]{1,0:T(8,128)(2,1)S(1)}, u32[]{:S(2)}, u32[]{:S(2)}) collective-permute-start(bf16[128,2304]{1,0:T(8,128)(2,1)S(1)} %get-tuple-element.72), channel_id=1, source_target_pairs={{0,32},{32,0},{1,33},{33,1},{2,34},{34,2},{3,35},{35,3},{4,36},{36... | collective-permute-start | bytes 1769480 | tf_op jit(solution)/shard_map/ppermute | solution.py:255
  97.4 42.6 %slice-start = ((s8[4718592]{0:T(1024)(128)(4,1)}), s8[4194304]{0:T(1024)(128)(4,1)S(1)}, s32[]{:S(2)}) async-start(s8[4718592]{0:T(1024)(128)(4,1)} %bitcast.13), calls=%async_computation.5 | async-start | bytes 8388608
  97.4 42.6 %slice-start.1 = ((s8[4718592]{0:T(1024)(128)(4,1)}), s8[524288]{0:T(1024)(128)(4,1)S(1)}, s32[]{:S(2)}) async-start(s8[4718592]{0:T(1024)(128)(4,1)} %bitcast.13), calls=%async_computation.6 | async-start | bytes 1048576
  117.0 2.7 %collective-permute-start.7 = (f32[2,2304]{1,0:T(2,128)S(1)}, f32[2,2304]{1,0:T(2,128)S(1)}, u32[]{:S(2)}, u32[]{:S(2)}) collective-permute-start(f32[2,2304]{1,0:T(2,128)S(1)} %shard_map.141.own), channel_id=1, source_target_pairs={{0,32},{32,0},{1,33},{33,1},{2,34},{34,2},{3,35},{35,3},{4,36},{36... | collective-permute-start | bytes 55304 | tf_op jit(solution)/shard_map/ppermute | solution.py:255
  138.2 3.4 %collective-permute-start.8 = (bf16[64,2,2304]{2,1,0:T(2,128)(2,1)S(1)}, bf16[64,2,2304]{2,1,0:T(2,128)(2,1)S(1)}, u32[]{:S(2)}, u32[]{:S(2)}) collective-permute-start(bf16[64,2,2304]{2,1,0:T(2,128)(2,1)S(1)} %all_to_all.29.own), channel_id=1, source_target_pairs={{0,32},{32,0},{1,33},{33,1},{2,34},{34,2},{3,35},{35,3},{4,36},{36... | collective-permute-start | bytes 1769480 | tf_op jit(solution)/shard_map/ppermute | solution.py:255

commit v2 on v1

--- a/solution.py
+++ b/solution.py
@@ -13,6 +13,8 @@
 DEVICES = ("y_lo", "core", "y_hi", "x", "z")
 CHIPS = ("x", "z", "y_lo", "y_hi")
 SWAP = [(0, 1), (1, 0)]
+LIMIT = 16 << 20
+HINT = 10**10
 F32 = jnp.float32
 BF16 = jnp.bfloat16
 VMEM = pl.BlockSpec(memory_space=pltpu.VMEM)
@@ -23,17 +25,22 @@
     return jax.ShapeDtypeStruct(dims, dtype)
 
 
-def call(kernel, outs, *args, space=pltpu.VMEM, scratch=()):
+def call(kernel, outs, *args, space=pltpu.VMEM, scratch=(), flops=0, source=pltpu.VMEM):
     return pl.pallas_call(
         kernel,
         out_shape=jax.tree.map(lambda o: space(o.shape, o.dtype), outs),
-        in_specs=[SMEM if a.dtype == jnp.int32 else VMEM for a in args],
+        in_specs=[
+            SMEM if a.dtype == jnp.int32 else pl.BlockSpec(memory_space=source) for a in args
+        ],
         out_specs=jax.tree.map(lambda _: VMEM, outs),
         scratch_shapes=scratch,
-        compiler_params=pltpu.CompilerParams(vmem_limit_bytes=8 << 20),
+        compiler_params=pltpu.CompilerParams(vmem_limit_bytes=LIMIT),
+        cost_estimate=pl.CostEstimate(flops=flops, transcendentals=0, bytes_accessed=0)
+        if flops
+        else None,
     )(
         *(
-            a if a.dtype == jnp.int32 else pltpu.with_memory_space_constraint(a, pltpu.VMEM)
+            a if a.dtype == jnp.int32 else pltpu.with_memory_space_constraint(a, source)
             for a in args
         )
     )
@@ -70,27 +77,36 @@
     )
 
 
-def merge_kernel(clean, corrupt, out):
-    out[0:1] = clean[...]
-    out[1:2] = corrupt[...]
-
-
 def spread(value, out):
     for chip in range(out.shape[0]):
         out[chip] = value
 
 
-def chip_rows_kernel(where, both, partner, out, stream):
+def load_kernel(clean, corrupt, own_clean, own_corrupt, sems):
+    copies = [
+        pltpu.make_async_copy(clean, own_clean, sems.at[0]),
+        pltpu.make_async_copy(corrupt, own_corrupt, sems.at[1]),
+    ]
+    for copy in copies:
+        copy.start()
+    for copy in copies:
+        copy.wait()
+
+
+def gains_kernel(pre, post, final, out):
+    for i, gain in enumerate((pre, post, final)):
+        out[i : i + 1] = gain[...].reshape(1, gain.shape[0])
+
+
+def chip_rows_kernel(where, clean, corrupt, other_clean, other_corrupt, out, stream, rows):
     first = where[0] == 0
     mine, _ = halves(where, out.shape[2])
-    a, b = both[...].astype(F32), partner[...].astype(F32)
-    low, high = jnp.where(first, a, b), jnp.where(first, b, a)
-    stream[0:1] = low[0:1]
-    stream[1:2] = high[0:1]
-    a, b = both[:, mine].astype(F32), partner[:, mine].astype(F32)
-    low, high = jnp.where(first, a, b), jnp.where(first, b, a)
-    quad = jnp.concatenate([low[0:1], high[0:1], low[1:2], high[1:2]], axis=0)
-    spread(quad.astype(BF16), out)
+    for i, (a, b) in enumerate(((clean, other_clean), (corrupt, other_corrupt))):
+        a, b = a[...].astype(F32), b[...].astype(F32)
+        rows[2 * i : 2 * i + 1] = jnp.where(first, a, b)
+        rows[2 * i + 1 : 2 * i + 2] = jnp.where(first, b, a)
+    stream[...] = rows[0:2]
+    spread(rows[:, mine].astype(BF16), out)
 
 
 def rows_kernel(pieces, clean, corrupt):
@@ -104,8 +120,8 @@
     a, b = own[...].astype(F32), other[...].astype(F32)
     total = jnp.sum(a * a, axis=-1, keepdims=True) + jnp.sum(b * b, axis=-1, keepdims=True)
     inv = lax.rsqrt(total / (2 * width) + epsilon)
-    normed[:, mine] = (a * inv * gain[:, mine]).astype(BF16)
-    normed[:, theirs] = (b * inv * gain[:, theirs]).astype(BF16)
+    normed[:, mine] = (a * inv * gain[0:1, mine]).astype(BF16)
+    normed[:, theirs] = (b * inv * gain[0:1, theirs]).astype(BF16)
     gate_pre = dot_nt(normed[...], w_gate[...])
     up_proj = dot_nt(normed[...], w_up[...])
     gate[...] = gate_pre
@@ -139,7 +155,7 @@
     return out[...]
 
 
-def wanted_rows(where, answers, unembed, gain):
+def wanted_kernel(where, answers, unembed, gains, out):
     lanes = lax.broadcasted_iota(jnp.int32, (1, unembed.shape[0]), 1)
     rows = []
     for core in range(2):
@@ -147,34 +163,25 @@
         rows.append(
             (lanes == answers[0, token]).astype(F32) - (lanes == answers[1, token]).astype(F32)
         )
-    selector = jnp.concatenate(rows + rows + rows + rows, axis=0).astype(BF16)
-    return gain[...] * dot_nn(selector, unembed[...])[:2]
+    selector = jnp.concatenate(rows * 4, axis=0).astype(BF16)
+    out[...] = gains[2:3] * dot_nn(selector, unembed[...])[:2]
 
 
 def output_kernel(
-    where,
-    answers,
-    own,
-    other,
-    stream,
-    unembed,
-    final_gain,
-    post_gain,
-    out,
-    grad_output,
-    whole,
+    where, own, other, stream, weighted, gains, out, grad_output, whole
 ):
     mine, _ = halves(where, out.shape[2])
+    post_gain = gains[1:2]
     mlp_out = joined(where, own, other, whole)
     inv_post = lax.rsqrt(mean_row(mlp_out * mlp_out) + epsilon)
-    output = stream[...] + mlp_out * inv_post * post_gain[...]
+    output = stream[...] + mlp_out * inv_post * post_gain
     inv_final = lax.rsqrt(mean_row(output * output) + epsilon)
-    wanted = wanted_rows(where, answers, unembed, final_gain)
+    wanted = weighted[...]
     grad_out = inv_final * wanted - output * (inv_final * inv_final * inv_final) * mean_row(
         wanted * output
     )
     grad_output[...] = grad_out
-    post_grad = post_gain[...] * grad_out
+    post_grad = post_gain * grad_out
     whole[...] = inv_post * post_grad - mlp_out * (inv_post * inv_post * inv_post) * mean_row(
         post_grad * mlp_out
     )
@@ -207,11 +214,11 @@
     out[...] = dot_nn(grad_gate[...], w_gate[:, mine]) + dot_nn(grad_up[...], w_up[:, mine])
 
 
-def input_kernel(where, own, other, stream, grad_output, pre_gain, out, whole):
+def input_kernel(where, own, other, stream, grad_output, gains, out, whole):
     mine, _ = halves(where, out.shape[2])
     rows = stream[...]
     inv_pre = lax.rsqrt(mean_row(rows * rows) + epsilon)
-    pre_grad = pre_gain[...] * joined(where, own, other, whole)
+    pre_grad = gains[0:1] * joined(where, own, other, whole)
     whole[...] = (
         grad_output[...]
         + inv_pre * pre_grad
@@ -283,7 +290,6 @@
     where = jnp.stack([core_index, pair, pair + 2 * plane]).astype(jnp.int32)
     hidden_units, latents = w_gate.shape[1], w_enc.shape[1]
     w_gate, w_up = w_gate.T, w_up.T
-    gains = (g[None] for g in (pre_gain, post_gain, final_gain))
     b_enc = b_enc[None]
 
     halved = shape((tokens, half), BF16)
@@ -296,23 +302,37 @@
     codes = shape((tokens, latents), F32)
     whole = pltpu.VMEM((2, width), F32)
 
-    both = call(merge_kernel, shape((2, width), BF16), resid_clean, resid_corrupt)
-    partner = swapped(both)
-    partner, where, pre_gain, post_gain, final_gain = lax.optimization_barrier(
-        (partner, where, *gains)
-    )
+    partner = (swapped(resid_clean), swapped(resid_corrupt))
+    one_row = shape((1, width), BF16)
+    held = call(
+        load_kernel,
+        (one_row, one_row),
+        resid_clean, resid_corrupt,
+        source=pltpu.HBM,
+        scratch=[pltpu.SemaphoreType.DMA((2,))],
+    )
+    *partner, where, clean, corrupt = lax.optimization_barrier((*partner, where, *held))
     quads, stream = call(
-        chip_rows_kernel, (shape((chips, 4, half), BF16), pair_rows), where, both, partner
-    )
-    own, own_corrupt = call(rows_kernel, (halved, halved), exchanged(quads))
+        chip_rows_kernel,
+        (shape((chips, 4, half), BF16), pair_rows),
+        where, clean, corrupt, *partner,
+        scratch=[pltpu.VMEM((4, width), F32)],
+        flops=HINT,
+    )
+    own, own_corrupt = call(rows_kernel, (halved, halved), exchanged(quads), flops=HINT)
+    pre_gain, own_corrupt = lax.optimization_barrier((pre_gain, own_corrupt))
+    gains = call(gains_kernel, shape((3, width), F32), pre_gain, post_gain, final_gain)
+    weighted = call(wanted_kernel, pair_rows, where, answer_ids.T, unembed, gains)
     other = swapped(own)
-    other, own_corrupt = lax.optimization_barrier((other, own_corrupt))
+    other, own_corrupt, gains, weighted = lax.optimization_barrier(
+        (other, own_corrupt, gains, weighted)
+    )
     other_corrupt = swapped(own_corrupt)
 
     sent, hidden, gate, up = call(
         forward_kernel,
         (halved, units, units32, units32),
-        where, own, other, w_gate, w_up, w_down, pre_gain,
+        where, own, other, w_gate, w_up, w_down, gains,
         scratch=[pltpu.VMEM((tokens, width), BF16)],
     )
     sent, other_corrupt = lax.optimization_barrier((sent, other_corrupt))
@@ -333,7 +353,7 @@
     spread_grad, grad_output = call(
         output_kernel,
         (pairs, pair_rows),
-        where, answer_ids.T, own_mlp, other_mlp, stream, unembed, final_gain, post_gain,
+        where, own_mlp, other_mlp, stream, weighted, gains,
         scratch=[whole],
     )
 
@@ -355,7 +375,7 @@
     spread_stream = call(
         input_kernel,
         pairs,
-        where, own_normed, swapped(own_normed), stream, grad_output, pre_gain,
+        where, own_normed, swapped(own_normed), stream, grad_output, gains,
         scratch=[whole],
     )
 

time: 144 us -> 139 us (0.965)
  local copies, waits for them, and re-layouts: 7.36 us -> 0.06 us
  Pallas kernels: 19.6 us -> 21.1 us
    unnamed x26, local copies, waits for them, and re-layouts: 5.13 us -> 0.06 us
    broadcast_in_dim x3 -> x0, local copies, waits for them, and re-layouts: 2.23 us -> none  [local(): gains = (g[None] for g in (pre_gain, post_gain, final_gain))]
    pallas_call x18 -> x20, Pallas kernels: 19.6 us -> 21.1 us  [call(): pl.pallas_call(kernel, out_shape=jax.tree.map(lambda o: space(o.shape, o....]
    ppermute x9 -> x10, starting transfers between devices: 11.5 us -> 12.2 us  [swapped(): return lax.ppermute(value, 'core', SWAP)]
    ppermute x9 -> x10, waiting for transfers between devices: 3.39 us -> 3.09 us  [swapped(): return lax.ppermute(value, 'core', SWAP)]
  transfers between devices with their start and end apart: 9 -> 10, of which waited for: 5 -> 7; matrix products, arithmetic and copies ran while one was open for 2% -> 0% of each run, Pallas kernels for 8% -> 9%
where the time goes in v2:
time: 139 us; the launch traced here: 138 us
  blocking collectives  102 us (73%)
  Pallas kernels  21.1 us (15%)
  starting transfers between devices  12.2 us (9%)
  waiting for transfers between devices  3.09 us (2%)
    all_to_all x5, blocking collectives, exchanged(): return lax.all_to_all(blocks, CHIPS, 0, 0, tiled=True)  102 us
    pallas_call x20, Pallas kernels, call(): pl.pallas_call(kernel, out_shape=jax.tree.map(lambda o: space(o.shape, o....  21.1 us
    ppermute x10, starting transfers between devices, swapped(): return lax.ppermute(value, 'core', SWAP)  12.2 us
    ppermute x10, waiting for transfers between devices, swapped(): return lax.ppermute(value, 'core', SWAP)  3.09 us
  transfers between devices with their start and end apart: 10, of which 7 were waited for; matrix products, arithmetic and copies ran while one was open for 0% of the time, Pallas kernels for 9%

profile of v2, /device:TPU:1, one launch (start us, length us, event | category | flops | bytes accessed | tf_op | source)
XLA Modules:
  0.0 138.4 jit_solution(11825258608314930842)
XLA Ops:
  0.0 1.4 collective-permute-start
  1.4 0.0 collective-permute-start.1
  1.4 0.1 pad_add_fusion.where
  1.5 0.8 shard_map.127
  2.2 0.2 collective-permute-done.other_clean
  2.4 0.3 collective-permute-done.1.other_corrupt
  2.8 0.7 shard_map.128
  3.4 30.4 %all_to_all.25.pieces = bf16[64,4,2304]{2,1,0:T(4,128)(2,1)S(1)} all-to-all(bf16[64,4,2304]{2,1,0:T(4,128)(2,1)S(1)} %get-tuple-element.56), channel_id=1, replica_groups=mesh['y_lo'=2,'core'=2,'y_hi'=2,'x'=4,'z'=4] {'x','z','y_lo','y_hi'}, dimensions={0} | all-to-all | bytes 2359296 | tf_op jit(solution)/shard_map/all_to_all | solution.py:258
  33.9 0.0 copy-start.8
  33.9 0.0 copy-start
  33.9 0.0 copy-start.1
  33.9 0.0 copy-start.2
  33.9 0.4 shard_map.129
  34.3 1.9 %collective-permute-start.2 = (bf16[128,2304]{1,0:T(8,128)(2,1)S(1)}, bf16[128,2304]{1,0:T(8,128)(2,1)S(1)}, u32[]{:S(2)}, u32[]{:S(2)}) collective-permute-start(bf16[128,2304]{1,0:T(8,128)(2,1)S(1)} %get-tuple-element.68.own), channel_id=1, source_target_pairs={{0,32},{32,0},{1,33},{33,1},{2,34},{34,2},{3,35},{35,3},{4,36},{36... | collective-permute-start | bytes 1769480 | tf_op jit(solution)/shard_map/ppermute | solution.py:262
  36.2 0.8 shard_map.131.weighted
  37.1 0.8 collective-permute-done.2.other
  37.8 0.4 collective-permute-start.3
  38.2 3.6 %shard_map.132 = (bf16[128,2304]{1,0:T(8,128)(2,1)S(1)}, bf16[128,288]{1,0:T(8,128)(2,1)S(1)}, f32[128,288]{1,0:T(8,128)S(1)}, f32[128,288]{1,0:T(8,128)S(1)}) custom-call(s32[3]{0:T(128)S(1)} %pad_add_fusion.where, bf16[128,2304]{1,0:T(8,128)(2,1)S(1)} %get-tuple-element.68.own, bf16[128,2304]{1,0:T(8,128)(2,1)S(1)} %collective-permute-done.2.other, ...), custom_call_target="tpu_custom_call" | custom-call | tf_op jit(solution)/shard_map/pallas_call | solution.py:29
  41.9 0.0 copy-start.7
  41.9 0.0 collective-permute-done.3.other
  41.9 1.2 collective-permute-start.4
  43.1 1.0 shard_map.133.own
  44.2 1.3 shard_map.134.clean_code
  45.5 0.2 shard_map.135
  45.7 18.0 %all_to_all.26.pieces = bf16[64,2,2304]{2,1,0:T(2,128)(2,1)S(1)} all-to-all(bf16[64,2,2304]{2,1,0:T(2,128)(2,1)S(1)} %shard_map.135), channel_id=1, replica_groups=mesh['y_lo'=2,'core'=2,'y_hi'=2,'x'=4,'z'=4] {'x','z','y_lo','y_hi'}, dimensions={0} | all-to-all | bytes 1179648 | tf_op jit(solution)/shard_map/all_to_all | solution.py:258
  63.7 0.2 shard_map.136.own
  63.9 1.5 %collective-permute-start.5 = (f32[2,2304]{1,0:T(2,128)S(1)}, f32[2,2304]{1,0:T(2,128)S(1)}, u32[]{:S(2)}, u32[]{:S(2)}) collective-permute-start(f32[2,2304]{1,0:T(2,128)S(1)} %shard_map.136.own), channel_id=1, source_target_pairs={{0,32},{32,0},{1,33},{33,1},{2,34},{34,2},{3,35},{35,3},{4,36},{36... | collective-permute-start | bytes 55304 | tf_op jit(solution)/shard_map/ppermute | solution.py:262
  65.4 1.3 shard_map.137.change
  66.8 1.0 shard_map.138
  67.8 18.0 %all_to_all.27.own = bf16[64,2,2304]{2,1,0:T(2,128)(2,1)S(1)} all-to-all(bf16[64,2,2304]{2,1,0:T(2,128)(2,1)S(1)} %get-tuple-element.79), channel_id=1, replica_groups=mesh['y_lo'=2,'core'=2,'y_hi'=2,'x'=4,'z'=4] {'x','z','y_lo','y_hi'}, dimensions={0} | all-to-all | bytes 1179648 | tf_op jit(solution)/shard_map/all_to_all | solution.py:258
  85.8 1.5 %collective-permute-start.6 = (bf16[64,2,2304]{2,1,0:T(2,128)(2,1)S(1)}, bf16[64,2,2304]{2,1,0:T(2,128)(2,1)S(1)}, u32[]{:S(2)}, u32[]{:S(2)}) collective-permute-start(bf16[64,2,2304]{2,1,0:T(2,128)(2,1)S(1)} %all_to_all.27.own), channel_id=1, source_target_pairs={{0,32},{32,0},{1,33},{33,1},{2,34},{34,2},{3,35},{35,3},{4,36},{36... | collective-permute-start | bytes 1769480 | tf_op jit(solution)/shard_map/ppermute | solution.py:262
  87.3 1.2 shard_map.139.own_part
  88.5 0.4 collective-permute-done.6.other
  88.9 2.5 %shard_map.140 = (bf16[128,2304]{1,0:T(8,128)(2,1)S(1)}, bf16[128,288]{1,0:T(8,128)(2,1)S(1)}, bf16[128,288]{1,0:T(8,128)(2,1)S(1)}) custom-call(s32[3]{0:T(128)S(1)} %pad_add_fusion.where, f32[128,288]{1,0:T(8,128)S(1)} %shard_map.139.own_part, bf16[64,2,2304]{2,1,0:T(2,128)(2,1)S(1)} %collective-permute-done.6.other, ...), custom_call_target="tpu_custom_call" | custom-call | tf_op jit(solution)/shard_map/pallas_call | solution.py:29
  91.5 0.6 collective-permute-start.7
  92.1 1.3 shard_map.141.own
  93.4 0.3 collective-permute-done.7.arrived
  93.7 0.2 shard_map.142
  93.9 17.6 %all_to_all.28.pieces = bf16[64,2,2304]{2,1,0:T(2,128)(2,1)S(1)} all-to-all(bf16[64,2,2304]{2,1,0:T(2,128)(2,1)S(1)} %shard_map.142), channel_id=1, replica_groups=mesh['y_lo'=2,'core'=2,'y_hi'=2,'x'=4,'z'=4] {'x','z','y_lo','y_hi'}, dimensions={0} | all-to-all | bytes 1179648 | tf_op jit(solution)/shard_map/all_to_all | solution.py:258
  111.5 0.2 shard_map.143.own
  111.7 1.9 %collective-permute-start.8 = (f32[2,2304]{1,0:T(2,128)S(1)}, f32[2,2304]{1,0:T(2,128)S(1)}, u32[]{:S(2)}, u32[]{:S(2)}) collective-permute-start(f32[2,2304]{1,0:T(2,128)S(1)} %shard_map.143.own), channel_id=1, source_target_pairs={{0,32},{32,0},{1,33},{33,1},{2,34},{34,2},{3,35},{35,3},{4,36},{36... | collective-permute-start | bytes 55304 | tf_op jit(solution)/shard_map/ppermute | solution.py:262
  113.6 0.8 collective-permute-done.8.other
  114.5 0.8 shard_map.144
  115.2 17.6 %all_to_all.29.own = bf16[64,2,2304]{2,1,0:T(2,128)(2,1)S(1)} all-to-all(bf16[64,2,2304]{2,1,0:T(2,128)(2,1)S(1)} %shard_map.144), channel_id=1, replica_groups=mesh['y_lo'=2,'core'=2,'y_hi'=2,'x'=4,'z'=4] {'x','z','y_lo','y_hi'}, dimensions={0} | all-to-all | bytes 1179648 | tf_op jit(solution)/shard_map/all_to_all | solution.py:258
  132.9 1.8 %collective-permute-start.9 = (bf16[64,2,2304]{2,1,0:T(2,128)(2,1)S(1)}, bf16[64,2,2304]{2,1,0:T(2,128)(2,1)S(1)}, u32[]{:S(2)}, u32[]{:S(2)}) collective-permute-start(bf16[64,2,2304]{2,1,0:T(2,128)(2,1)S(1)} %all_to_all.29.own), channel_id=1, source_target_pairs={{0,32},{32,0},{1,33},{33,1},{2,34},{34,2},{3,35},{35,3},{4,36},{36... | collective-permute-start | bytes 1769480 | tf_op jit(solution)/shard_map/ppermute | solution.py:262
  134.7 1.4 %shard_map.145.part = f32[128,512]{1,0:T(8,128)S(1)} custom-call(s32[3]{0:T(128)S(1)} %pad_add_fusion.where, bf16[64,2,2304]{2,1,0:T(2,128)(2,1)S(1)} %all_to_all.29.own, bf16[512,4608]{1,0:T(8,128)(2,1)S(1)} %bitcast.16), custom_call_target="tpu_custom_call" | custom-call | tf_op jit(solution)/shard_map/pallas_call | solution.py:29
  136.2 0.2 collective-permute-done.9.other
  136.3 2.0 %shard_map.146 = f32[1,512]{1,0:T(1,128)} custom-call(s32[3]{0:T(128)S(1)} %pad_add_fusion.where, f32[128,512]{1,0:T(8,128)S(1)} %shard_map.145.part, bf16[64,2,2304]{2,1,0:T(2,128)(2,1)S(1)} %collective-permute-done.9.other, bf16[512,4608]{1,0:T(8,128)(2,1)S(1)} %bitcast.16, f32[128,512]{1,0:T(8,128)S(1)} %shard_map.137.change), custom_call_target="tpu_custom_call" | custom-call | tf_op jit(solution)/shard_map/pallas_call | solution.py:29
  (26 shorter events, 0.1 us)
Async XLA Ops:
  0.0 2.4 %collective-permute-start = (bf16[1,4608]{1,0:T(2,128)(2,1)}, bf16[1,4608]{1,0:T(2,128)(2,1)S(1)}, u32[]{:S(2)}, u32[]{:S(2)}) collective-permute-start(bf16[1,4608]{1,0:T(2,128)(2,1)} %clean.1), channel_id=1, source_target_pairs={{0,32},{32,0},{1,33},{33,1},{2,34},{34,2},{3,35},{35,3},{4,36},{36... | collective-permute-start | bytes 27656 | tf_op jit(solution)/shard_map/ppermute | solution.py:262
  1.4 1.4 %collective-permute-start.1 = (bf16[1,4608]{1,0:T(2,128)(2,1)}, bf16[1,4608]{1,0:T(2,128)(2,1)S(1)}, u32[]{:S(2)}, u32[]{:S(2)}) collective-permute-start(bf16[1,4608]{1,0:T(2,128)(2,1)} %corrupt.1), channel_id=1, source_target_pairs={{0,32},{32,0},{1,33},{33,1},{2,34},{34,2},{3,35},{35,3},{4,36},{36... | collective-permute-start | bytes 27656 | tf_op jit(solution)/shard_map/ppermute | solution.py:262
  33.8 2.4 %copy-start.4 = (f32[4608]{0:T(1024)S(1)}, f32[4608]{0:T(1024)}, u32[]{:S(2)}) copy-start(f32[4608]{0:T(1024)} %pre) | copy-start | bytes 55300
  33.8 2.4 %copy-start.5 = (f32[4608]{0:T(1024)S(1)}, f32[4608]{0:T(1024)}, u32[]{:S(2)}) copy-start(f32[4608]{0:T(1024)} %post.1) | copy-start | bytes 55300
  33.8 2.4 %copy-start.6 = (f32[4608]{0:T(1024)S(1)}, f32[4608]{0:T(1024)}, u32[]{:S(2)}) copy-start(f32[4608]{0:T(1024)} %final.1) | copy-start | bytes 55300
  33.8 2.4 %copy-start.3 = (bf16[128,4608]{1,0:T(8,128)(2,1)S(1)}, bf16[128,4608]{1,0:T(8,128)(2,1)}, u32[]{:S(2)}) copy-start(bf16[128,4608]{1,0:T(8,128)(2,1)} %unembed.1) | copy-start | bytes 3538948
  33.9 2.4 %copy-start.8 = (s32[128,2]{0,1:T(2,128)S(1)}, s32[128,2]{0,1:T(2,128)}, u32[]{:S(2)}) copy-start(s32[128,2]{0,1:T(2,128)} %param.15) | copy-start | bytes 3076
  33.9 4.3 %copy-start = (bf16[288,4608]{1,0:T(8,128)(2,1)S(1)}, bf16[288,4608]{1,0:T(8,128)(2,1)}, u32[]{:S(2)}) copy-start(bf16[288,4608]{1,0:T(8,128)(2,1)} %w_down.7) | copy-start | bytes 7962628
  33.9 4.3 %copy-start.1 = (bf16[4608,288]{0,1:T(8,128)(2,1)S(1)}, bf16[4608,288]{0,1:T(8,128)(2,1)}, u32[]{:S(2)}) copy-start(bf16[4608,288]{0,1:T(8,128)(2,1)} %param.20) | copy-start | bytes 7962628
  33.9 4.3 %copy-start.2 = (bf16[4608,288]{0,1:T(8,128)(2,1)S(1)}, bf16[4608,288]{0,1:T(8,128)(2,1)}, u32[]{:S(2)}) copy-start(bf16[4608,288]{0,1:T(8,128)(2,1)} %param.21) | copy-start | bytes 7962628
  34.3 3.5 %collective-permute-start.2 = (bf16[128,2304]{1,0:T(8,128)(2,1)S(1)}, bf16[128,2304]{1,0:T(8,128)(2,1)S(1)}, u32[]{:S(2)}, u32[]{:S(2)}) collective-permute-start(bf16[128,2304]{1,0:T(8,128)(2,1)S(1)} %get-tuple-element.68.own), channel_id=1, source_target_pairs={{0,32},{32,0},{1,33},{33,1},{2,34},{34,2},{3,35},{35,3},{4,36},{36... | collective-permute-start | bytes 1769480 | tf_op jit(solution)/shard_map/ppermute | solution.py:262
  37.8 4.1 %collective-permute-start.3 = (bf16[128,2304]{1,0:T(8,128)(2,1)S(1)}, bf16[128,2304]{1,0:T(8,128)(2,1)S(1)}, u32[]{:S(2)}, u32[]{:S(2)}) collective-permute-start(bf16[128,2304]{1,0:T(8,128)(2,1)S(1)} %get-tuple-element.73.own), channel_id=1, source_target_pairs={{0,32},{32,0},{1,33},{33,1},{2,34},{34,2},{3,35},{35,3},{4,36},{36... | collective-permute-start | bytes 1769480 | tf_op jit(solution)/shard_map/ppermute | solution.py:262
  38.2 5.9 %slice-start = ((s8[4718592]{0:T(1024)(128)(4,1)}), s8[4194304]{0:T(1024)(128)(4,1)S(1)}, s32[]{:S(2)}) async-start(s8[4718592]{0:T(1024)(128)(4,1)} %bitcast.13), calls=%async_computation.5 | async-start | bytes 8388608
  38.2 5.9 %slice-start.1 = ((s8[4718592]{0:T(1024)(128)(4,1)}), s8[524288]{0:T(1024)(128)(4,1)S(1)}, s32[]{:S(2)}) async-start(s8[4718592]{0:T(1024)(128)(4,1)} %bitcast.13), calls=%async_computation.6 | async-start | bytes 1048576
  41.9 2.3 %copy-start.7 = (f32[512]{0:T(512)S(1)}, f32[512]{0:T(512)}, u32[]{:S(2)}) copy-start(f32[512]{0:T(512)} %param.24) | copy-start | bytes 6148
  41.9 3.6 %collective-permute-start.4 = (bf16[128,2304]{1,0:T(8,128)(2,1)S(1)}, bf16[128,2304]{1,0:T(8,128)(2,1)S(1)}, u32[]{:S(2)}, u32[]{:S(2)}) collective-permute-start(bf16[128,2304]{1,0:T(8,128)(2,1)S(1)} %get-tuple-element.65), channel_id=1, source_target_pairs={{0,32},{32,0},{1,33},{33,1},{2,34},{34,2},{3,35},{35,3},{4,36},{36... | collective-permute-start | bytes 1769480 | tf_op jit(solution)/shard_map/ppermute | solution.py:262
  63.9 2.9 %collective-permute-start.5 = (f32[2,2304]{1,0:T(2,128)S(1)}, f32[2,2304]{1,0:T(2,128)S(1)}, u32[]{:S(2)}, u32[]{:S(2)}) collective-permute-start(f32[2,2304]{1,0:T(2,128)S(1)} %shard_map.136.own), channel_id=1, source_target_pairs={{0,32},{32,0},{1,33},{33,1},{2,34},{34,2},{3,35},{35,3},{4,36},{36... | collective-permute-start | bytes 55304 | tf_op jit(solution)/shard_map/ppermute | solution.py:262
  85.8 3.1 %collective-permute-start.6 = (bf16[64,2,2304]{2,1,0:T(2,128)(2,1)S(1)}, bf16[64,2,2304]{2,1,0:T(2,128)(2,1)S(1)}, u32[]{:S(2)}, u32[]{:S(2)}) collective-permute-start(bf16[64,2,2304]{2,1,0:T(2,128)(2,1)S(1)} %all_to_all.27.own), channel_id=1, source_target_pairs={{0,32},{32,0},{1,33},{33,1},{2,34},{34,2},{3,35},{35,3},{4,36},{36... | collective-permute-start | bytes 1769480 | tf_op jit(solution)/shard_map/ppermute | solution.py:262
  91.5 2.3 %collective-permute-start.7 = (bf16[128,2304]{1,0:T(8,128)(2,1)S(1)}, bf16[128,2304]{1,0:T(8,128)(2,1)S(1)}, u32[]{:S(2)}, u32[]{:S(2)}) collective-permute-start(bf16[128,2304]{1,0:T(8,128)(2,1)S(1)} %get-tuple-element.84), channel_id=1, source_target_pairs={{0,32},{32,0},{1,33},{33,1},{2,34},{34,2},{3,35},{35,3},{4,36},{36... | collective-permute-start | bytes 1769480 | tf_op jit(solution)/shard_map/ppermute | solution.py:262
  92.1 42.6 %slice-start.2 = ((s8[4718592]{0:T(1024)(128)(4,1)}), s8[4194304]{0:T(1024)(128)(4,1)S(1)}, s32[]{:S(2)}) async-start(s8[4718592]{0:T(1024)(128)(4,1)} %bitcast.15), calls=%async_computation.7 | async-start | bytes 8388608
  92.1 42.6 %slice-start.3 = ((s8[4718592]{0:T(1024)(128)(4,1)}), s8[524288]{0:T(1024)(128)(4,1)S(1)}, s32[]{:S(2)}) async-start(s8[4718592]{0:T(1024)(128)(4,1)} %bitcast.15), calls=%async_computation.8 | async-start | bytes 1048576
  111.7 2.7 %collective-permute-start.8 = (f32[2,2304]{1,0:T(2,128)S(1)}, f32[2,2304]{1,0:T(2,128)S(1)}, u32[]{:S(2)}, u32[]{:S(2)}) collective-permute-start(f32[2,2304]{1,0:T(2,128)S(1)} %shard_map.143.own), channel_id=1, source_target_pairs={{0,32},{32,0},{1,33},{33,1},{2,34},{34,2},{3,35},{35,3},{4,36},{36... | collective-permute-start | bytes 55304 | tf_op jit(solution)/shard_map/ppermute | solution.py:262
  132.9 3.4 %collective-permute-start.9 = (bf16[64,2,2304]{2,1,0:T(2,128)(2,1)S(1)}, bf16[64,2,2304]{2,1,0:T(2,128)(2,1)S(1)}, u32[]{:S(2)}, u32[]{:S(2)}) collective-permute-start(bf16[64,2,2304]{2,1,0:T(2,128)(2,1)S(1)} %all_to_all.29.own), channel_id=1, source_target_pairs={{0,32},{32,0},{1,33},{33,1},{2,34},{34,2},{3,35},{35,3},{4,36},{36... | collective-permute-start | bytes 1769480 | tf_op jit(solution)/shard_map/ppermute | solution.py:262

commit v3 on v2

--- a/solution.py
+++ b/solution.py
@@ -14,7 +14,8 @@
 CHIPS = ("x", "z", "y_lo", "y_hi")
 SWAP = [(0, 1), (1, 0)]
 LIMIT = 16 << 20
-HINT = 10**10
+HINT = 10**11
+CHUNK = 768
 F32 = jnp.float32
 BF16 = jnp.bfloat16
 VMEM = pl.BlockSpec(memory_space=pltpu.VMEM)
@@ -109,24 +110,33 @@
     spread(rows[:, mine].astype(BF16), out)
 
 
-def rows_kernel(pieces, clean, corrupt):
+def rows_kernel(pieces, *refs):
+    clean, corrupt = refs[-2:]
     clean[...] = pieces[:, :2].reshape(clean.shape)
     corrupt[...] = pieces[:, 2:].reshape(corrupt.shape)
 
 
-def forward_kernel(where, own, other, w_gate, w_up, w_down, gain, send, hidden, gate, up, normed):
+def forward_kernel(where, own, other, w_gate, w_up, w_down, gain, send, hidden, gate, up):
     width = own.shape[1]
-    mine, theirs = halves(where, width)
-    a, b = own[...].astype(F32), other[...].astype(F32)
-    total = jnp.sum(a * a, axis=-1, keepdims=True) + jnp.sum(b * b, axis=-1, keepdims=True)
+    _, theirs = halves(where, width)
+    total = 0.0
+    for ref in (own, other):
+        for at in range(0, width, CHUNK):
+            part = ref[:, at : at + CHUNK].astype(F32)
+            total = total + jnp.sum(part * part, axis=-1, keepdims=True)
     inv = lax.rsqrt(total / (2 * width) + epsilon)
-    normed[:, mine] = (a * inv * gain[0:1, mine]).astype(BF16)
-    normed[:, theirs] = (b * inv * gain[0:1, theirs]).astype(BF16)
-    gate_pre = dot_nt(normed[...], w_gate[...])
-    up_proj = dot_nt(normed[...], w_up[...])
+    gate_pre, up_proj = None, None
+    for base, ref in ((where[0], own), (1 - where[0], other)):
+        for at in range(0, width, CHUNK):
+            lanes = pl.ds(pl.multiple_of(base * width + at, 128), CHUNK)
+            part = ref[:, at : at + CHUNK].astype(F32)
+            part = (part * inv * gain[0:1, lanes]).astype(BF16)
+            g, u = dot_nt(w_gate[:, lanes], part), dot_nt(w_up[:, lanes], part)
+            gate_pre = g if gate_pre is None else gate_pre + g
+            up_proj = u if up_proj is None else up_proj + u
     gate[...] = gate_pre
     up[...] = up_proj
-    act = (gelu_tanh(gate_pre) * up_proj).astype(BF16)
+    act = (gelu_tanh(gate_pre) * up_proj).T.astype(BF16)
     hidden[...] = act
     send[...] = dot_nn(act, w_down[:, theirs]).astype(BF16)
 
@@ -190,7 +200,7 @@
 
 def backward_own_half_kernel(where, own, w_down, out):
     mine, _ = halves(where, own.shape[2])
-    out[...] = dot_nt(own[...].reshape(out.shape[0], own.shape[2]), w_down[:, mine])
+    out[...] = dot_nt(w_down[:, mine], own[...].reshape(out.shape[1], own.shape[2]))
 
 
 def backward_kernel(
@@ -199,11 +209,11 @@
     width = other.shape[2]
     _, theirs = halves(where, width)
     grad_hidden = own_part[...] + dot_nt(
-        other[...].reshape(own_part.shape[0], width), w_down[:, theirs]
+        w_down[:, theirs], other[...].reshape(own_part.shape[1], width)
     )
     gate_pre = gate[...]
-    to_gate = (grad_hidden * up[...] * gelu_slope(gate_pre)).astype(BF16)
-    to_up = (grad_hidden * gelu_tanh(gate_pre)).astype(BF16)
+    to_gate = (grad_hidden * up[...] * gelu_slope(gate_pre)).T.astype(BF16)
+    to_up = (grad_hidden * gelu_tanh(gate_pre)).T.astype(BF16)
     grad_gate[...] = to_gate
     grad_up[...] = to_up
     send[...] = (dot_nn(to_gate, w_gate[:, theirs]) + dot_nn(to_up, w_up[:, theirs])).astype(BF16)
@@ -244,14 +254,14 @@
 
 def attribution_own_kernel(where, own, w_dec, out):
     mine, _ = halves(where, own.shape[2])
-    out[...] = dot_nt(own[...].reshape(out.shape[0], own.shape[2]), w_dec[:, mine])
+    out[...] = dot_nt(w_dec[:, mine], own[...].reshape(out.shape[1], own.shape[2]))
 
 
 def attribution_kernel(where, part, other, w_dec, change, out):
     width = other.shape[2]
     _, theirs = halves(where, width)
-    projected = part[...] + dot_nt(other[...].reshape(part.shape[0], width), w_dec[:, theirs])
-    out[...] = jnp.sum(change[...] * projected, axis=0, keepdims=True)
+    projected = part[...] + dot_nt(w_dec[:, theirs], other[...].reshape(part.shape[1], width))
+    out[...] = jnp.sum(change[...] * projected.T, axis=0, keepdims=True)
 
 
 def exchanged(blocks):
@@ -298,7 +308,7 @@
     pair_rows = shape((2, width), F32)
     pair_half = shape((2, half), F32)
     units = shape((tokens, hidden_units), BF16)
-    units32 = shape((tokens, hidden_units), F32)
+    units32 = shape((hidden_units, tokens), F32)
     codes = shape((tokens, latents), F32)
     whole = pltpu.VMEM((2, width), F32)
 
@@ -319,7 +329,12 @@
         scratch=[pltpu.VMEM((4, width), F32)],
         flops=HINT,
     )
-    own, own_corrupt = call(rows_kernel, (halved, halved), exchanged(quads), flops=HINT)
+    own, own_corrupt = call(
+        rows_kernel,
+        (halved, halved),
+        exchanged(quads), w_enc, w_gate, w_up, w_down, unembed, pre_gain, post_gain, final_gain,
+        flops=HINT,
+    )
     pre_gain, own_corrupt = lax.optimization_barrier((pre_gain, own_corrupt))
     gains = call(gains_kernel, shape((3, width), F32), pre_gain, post_gain, final_gain)
     weighted = call(wanted_kernel, pair_rows, where, answer_ids.T, unembed, gains)
@@ -333,23 +348,18 @@
         forward_kernel,
         (halved, units, units32, units32),
         where, own, other, w_gate, w_up, w_down, gains,
-        scratch=[pltpu.VMEM((tokens, width), BF16)],
     )
     sent, other_corrupt = lax.optimization_barrier((sent, other_corrupt))
     arrived = swapped(sent)
     own_sum = call(forward_own_kernel, halved32, where, hidden, w_down)
-    own_sum, own, other = lax.optimization_barrier((own_sum, own, other))
-    clean_code = call(code_kernel, codes, where, own, other, w_enc, b_enc)
-    arrived, own_sum, clean_code = lax.optimization_barrier((arrived, own_sum, clean_code))
+    arrived, own_sum = lax.optimization_barrier((arrived, own_sum))
     own_mlp = call(
         total_kernel, pair_half, exchanged(call(chip_sum_kernel, pairs, own_sum, arrived))
     )
-    own_mlp, own_corrupt = lax.optimization_barrier((own_mlp, own_corrupt))
+    own_mlp, own = lax.optimization_barrier((own_mlp, own))
     other_mlp = swapped(own_mlp)
-    change = call(
-        change_kernel, codes, where, own_corrupt, other_corrupt, w_enc, b_enc, clean_code
-    )
-    other_mlp, change = lax.optimization_barrier((other_mlp, change))
+    clean_code = call(code_kernel, codes, where, own, other, w_enc, b_enc)
+    other_mlp, clean_code = lax.optimization_barrier((other_mlp, clean_code))
     spread_grad, grad_output = call(
         output_kernel,
         (pairs, pair_rows),
@@ -372,16 +382,24 @@
     own_normed = call(
         total_kernel, pair_half, exchanged(call(chip_sum_kernel, pairs, own_sum, arrived))
     )
+    own_normed, own_corrupt = lax.optimization_barrier((own_normed, own_corrupt))
+    other_normed = swapped(own_normed)
+    change = call(
+        change_kernel, codes, where, own_corrupt, other_corrupt, w_enc, b_enc, clean_code
+    )
+    other_normed, change = lax.optimization_barrier((other_normed, change))
     spread_stream = call(
         input_kernel,
         pairs,
-        where, own_normed, swapped(own_normed), stream, grad_output, gains,
+        where, own_normed, other_normed, stream, grad_output, gains,
         scratch=[whole],
     )
 
     last_own = exchanged(spread_stream)
     last_other = swapped(last_own)
-    own_part = call(attribution_own_kernel, codes, where, last_own, w_dec)
+    own_part = call(
+        attribution_own_kernel, shape((latents, tokens), F32), where, last_own, w_dec
+    )
     last_other, own_part = lax.optimization_barrier((last_other, own_part))
     return call(
         attribution_kernel,

time: 139 us -> 137 us (0.986)
  Pallas kernels: 21.1 us -> 19.5 us
  starting transfers between devices: 12.2 us -> 10.8 us
    pallas_call x20, Pallas kernels: 21.1 us -> 19.5 us  [call(): pl.pallas_call(kernel, out_shape=jax.tree.map(lambda o: space(o.shape, o....]
where the time goes in v3:
time: 137 us; the launch traced here: 136 us
  blocking collectives  102 us (74%)
  Pallas kernels  19.5 us (14%)
  starting transfers between devices  10.8 us (8%)
  waiting for transfers between devices  3.39 us (2%)
    all_to_all x5, blocking collectives, exchanged(): return lax.all_to_all(blocks, CHIPS, 0, 0, tiled=True)  102 us
    pallas_call x20, Pallas kernels, call(): pl.pallas_call(kernel, out_shape=jax.tree.map(lambda o: space(o.shape, o....  19.5 us
    ppermute x10, starting transfers between devices, swapped(): return lax.ppermute(value, 'core', SWAP)  10.8 us
    ppermute x10, waiting for transfers between devices, swapped(): return lax.ppermute(value, 'core', SWAP)  3.39 us
  transfers between devices with their start and end apart: 10, of which 7 were waited for; matrix products, arithmetic and copies ran while one was open for 0% of the time, Pallas kernels for 9%

profile of v3, /device:TPU:1, one launch (start us, length us, event | category | flops | bytes accessed | tf_op | source)
XLA Modules:
  0.0 136.3 jit_solution(2626647881932844334)
XLA Ops:
  0.0 1.4 %collective-permute-start = (bf16[1,4608]{1,0:T(2,128)(2,1)}, bf16[1,4608]{1,0:T(2,128)(2,1)S(1)}, u32[]{:S(2)}, u32[]{:S(2)}) collective-permute-start(bf16[1,4608]{1,0:T(2,128)(2,1)} %clean.1), channel_id=1, source_target_pairs={{0,32},{32,0},{1,33},{33,1},{2,34},{34,2},{3,35},{35,3},{4,36},{36... | collective-permute-start | bytes 27656 | tf_op jit(solution)/shard_map/ppermute | solution.py:272
  1.4 0.1 pad_add_fusion.where
  1.5 0.8 shard_map.127
  2.2 0.2 collective-permute-done.other_clean
  2.4 0.3 collective-permute-done.1.other_corrupt
  2.8 0.0 copy-start.4
  2.8 0.0 copy-start.5
  2.8 0.0 copy-start.6
  2.8 0.0 copy-start.7
  2.8 0.7 shard_map.128
  3.5 30.7 %all_to_all.25.pieces = bf16[64,4,2304]{2,1,0:T(4,128)(2,1)S(1)} all-to-all(bf16[64,4,2304]{2,1,0:T(4,128)(2,1)S(1)} %get-tuple-element.56), channel_id=1, replica_groups=mesh['y_lo'=2,'core'=2,'y_hi'=2,'x'=4,'z'=4] {'x','z','y_lo','y_hi'}, dimensions={0} | all-to-all | bytes 2359296 | tf_op jit(solution)/shard_map/all_to_all | solution.py:268
  34.2 0.0 copy-start.9
  34.3 0.4 shard_map.129
  34.7 1.9 %collective-permute-start.2 = (bf16[128,2304]{1,0:T(8,128)(2,1)S(1)}, bf16[128,2304]{1,0:T(8,128)(2,1)S(1)}, u32[]{:S(2)}, u32[]{:S(2)}) collective-permute-start(bf16[128,2304]{1,0:T(8,128)(2,1)S(1)} %get-tuple-element.70.own), channel_id=1, source_target_pairs={{0,32},{32,0},{1,33},{33,1},{2,34},{34,2},{3,35},{35,3},{4,36},{36... | collective-permute-start | bytes 1769480 | tf_op jit(solution)/shard_map/ppermute | solution.py:272
  36.6 0.8 shard_map.131.weighted
  37.4 0.8 collective-permute-done.2.other
  38.2 0.4 collective-permute-start.3
  38.5 2.9 %shard_map.132 = (bf16[128,2304]{1,0:T(8,128)(2,1)S(1)}, bf16[128,288]{1,0:T(8,128)(2,1)S(1)}, f32[288,128]{1,0:T(8,128)S(1)}, f32[288,128]{1,0:T(8,128)S(1)}) custom-call(s32[3]{0:T(128)S(1)} %pad_add_fusion.where, bf16[128,2304]{1,0:T(8,128)(2,1)S(1)} %get-tuple-element.70.own, bf16[128,2304]{1,0:T(8,128)(2,1)S(1)} %collective-permute-done.2.other, ...), custom_call_target="tpu_custom_call" | custom-call | tf_op jit(solution)/shard_map/pallas_call | solution.py:30
  41.5 0.0 collective-permute-done.3.other
  41.5 0.2 collective-permute-start.4
  41.7 1.0 shard_map.133.own
  42.7 0.0 copy-start.8
  42.7 0.8 collective-permute-done.4.arrived
  43.6 0.2 shard_map.134
  43.8 17.8 %all_to_all.26.pieces = bf16[64,2,2304]{2,1,0:T(2,128)(2,1)S(1)} all-to-all(bf16[64,2,2304]{2,1,0:T(2,128)(2,1)S(1)} %shard_map.134), channel_id=1, replica_groups=mesh['y_lo'=2,'core'=2,'y_hi'=2,'x'=4,'z'=4] {'x','z','y_lo','y_hi'}, dimensions={0} | all-to-all | bytes 1179648 | tf_op jit(solution)/shard_map/all_to_all | solution.py:268
  61.6 0.2 shard_map.135.own
  61.8 1.7 %collective-permute-start.5 = (f32[2,2304]{1,0:T(2,128)S(1)}, f32[2,2304]{1,0:T(2,128)S(1)}, u32[]{:S(2)}, u32[]{:S(2)}) collective-permute-start(f32[2,2304]{1,0:T(2,128)S(1)} %shard_map.135.own), channel_id=1, source_target_pairs={{0,32},{32,0},{1,33},{33,1},{2,34},{34,2},{3,35},{35,3},{4,36},{36... | collective-permute-start | bytes 55304 | tf_op jit(solution)/shard_map/ppermute | solution.py:272
  63.5 1.3 shard_map.136.clean_code
  64.8 1.0 shard_map.137
  65.9 18.0 %all_to_all.27.own = bf16[64,2,2304]{2,1,0:T(2,128)(2,1)S(1)} all-to-all(bf16[64,2,2304]{2,1,0:T(2,128)(2,1)S(1)} %get-tuple-element.74), channel_id=1, replica_groups=mesh['y_lo'=2,'core'=2,'y_hi'=2,'x'=4,'z'=4] {'x','z','y_lo','y_hi'}, dimensions={0} | all-to-all | bytes 1179648 | tf_op jit(solution)/shard_map/all_to_all | solution.py:268
  83.9 1.5 %collective-permute-start.6 = (bf16[64,2,2304]{2,1,0:T(2,128)(2,1)S(1)}, bf16[64,2,2304]{2,1,0:T(2,128)(2,1)S(1)}, u32[]{:S(2)}, u32[]{:S(2)}) collective-permute-start(bf16[64,2,2304]{2,1,0:T(2,128)(2,1)S(1)} %all_to_all.27.own), channel_id=1, source_target_pairs={{0,32},{32,0},{1,33},{33,1},{2,34},{34,2},{3,35},{35,3},{4,36},{36... | collective-permute-start | bytes 1769480 | tf_op jit(solution)/shard_map/ppermute | solution.py:272
  85.3 1.1 shard_map.138.own_part
  86.4 0.6 collective-permute-done.6.other
  87.0 2.0 %shard_map.139 = (bf16[128,2304]{1,0:T(8,128)(2,1)S(1)}, bf16[128,288]{1,0:T(8,128)(2,1)S(1)}, bf16[128,288]{1,0:T(8,128)(2,1)S(1)}) custom-call(s32[3]{0:T(128)S(1)} %pad_add_fusion.where, f32[288,128]{1,0:T(8,128)S(1)} %shard_map.138.own_part, bf16[64,2,2304]{2,1,0:T(2,128)(2,1)S(1)} %collective-permute-done.6.other, ...), custom_call_target="tpu_custom_call" | custom-call | tf_op jit(solution)/shard_map/pallas_call | solution.py:30
  88.9 0.4 collective-permute-start.7
  89.4 1.3 shard_map.140.own
  90.7 0.3 collective-permute-done.7.arrived
  91.0 0.2 shard_map.141
  91.2 17.8 %all_to_all.28.pieces = bf16[64,2,2304]{2,1,0:T(2,128)(2,1)S(1)} all-to-all(bf16[64,2,2304]{2,1,0:T(2,128)(2,1)S(1)} %shard_map.141), channel_id=1, replica_groups=mesh['y_lo'=2,'core'=2,'y_hi'=2,'x'=4,'z'=4] {'x','z','y_lo','y_hi'}, dimensions={0} | all-to-all | bytes 1179648 | tf_op jit(solution)/shard_map/all_to_all | solution.py:268
  109.0 0.2 shard_map.142.own
  109.2 1.9 %collective-permute-start.8 = (f32[2,2304]{1,0:T(2,128)S(1)}, f32[2,2304]{1,0:T(2,128)S(1)}, u32[]{:S(2)}, u32[]{:S(2)}) collective-permute-start(f32[2,2304]{1,0:T(2,128)S(1)} %shard_map.142.own), channel_id=1, source_target_pairs={{0,32},{32,0},{1,33},{33,1},{2,34},{34,2},{3,35},{35,3},{4,36},{36... | collective-permute-start | bytes 55304 | tf_op jit(solution)/shard_map/ppermute | solution.py:272
  111.1 1.3 shard_map.143.change
  112.5 0.8 shard_map.144
  113.2 18.0 %all_to_all.29.own = bf16[64,2,2304]{2,1,0:T(2,128)(2,1)S(1)} all-to-all(bf16[64,2,2304]{2,1,0:T(2,128)(2,1)S(1)} %shard_map.144), channel_id=1, replica_groups=mesh['y_lo'=2,'core'=2,'y_hi'=2,'x'=4,'z'=4] {'x','z','y_lo','y_hi'}, dimensions={0} | all-to-all | bytes 1179648 | tf_op jit(solution)/shard_map/all_to_all | solution.py:268
  131.2 1.5 %collective-permute-start.9 = (bf16[64,2,2304]{2,1,0:T(2,128)(2,1)S(1)}, bf16[64,2,2304]{2,1,0:T(2,128)(2,1)S(1)}, u32[]{:S(2)}, u32[]{:S(2)}) collective-permute-start(bf16[64,2,2304]{2,1,0:T(2,128)(2,1)S(1)} %all_to_all.29.own), channel_id=1, source_target_pairs={{0,32},{32,0},{1,33},{33,1},{2,34},{34,2},{3,35},{35,3},{4,36},{36... | collective-permute-start | bytes 1769480 | tf_op jit(solution)/shard_map/ppermute | solution.py:272
  132.7 1.3 shard_map.145.part
  134.0 0.3 collective-permute-done.9.other
  134.3 2.0 %shard_map.146 = f32[1,512]{1,0:T(1,128)} custom-call(s32[3]{0:T(128)S(1)} %pad_add_fusion.where, f32[512,128]{1,0:T(8,128)S(1)} %shard_map.145.part, bf16[64,2,2304]{2,1,0:T(2,128)(2,1)S(1)} %collective-permute-done.9.other, bf16[512,4608]{1,0:T(8,128)(2,1)S(1)} %bitcast.16, f32[128,512]{1,0:T(8,128)S(1)} %shard_map.143.change), custom_call_target="tpu_custom_call" | custom-call | tf_op jit(solution)/shard_map/pallas_call | solution.py:30
  (23 shorter events, 0.0 us)
Async XLA Ops:
  0.0 2.4 %collective-permute-start = (bf16[1,4608]{1,0:T(2,128)(2,1)}, bf16[1,4608]{1,0:T(2,128)(2,1)S(1)}, u32[]{:S(2)}, u32[]{:S(2)}) collective-permute-start(bf16[1,4608]{1,0:T(2,128)(2,1)} %clean.1), channel_id=1, source_target_pairs={{0,32},{32,0},{1,33},{33,1},{2,34},{34,2},{3,35},{35,3},{4,36},{36... | collective-permute-start | bytes 27656 | tf_op jit(solution)/shard_map/ppermute | solution.py:272
  1.4 1.4 %collective-permute-start.1 = (bf16[1,4608]{1,0:T(2,128)(2,1)}, bf16[1,4608]{1,0:T(2,128)(2,1)S(1)}, u32[]{:S(2)}, u32[]{:S(2)}) collective-permute-start(bf16[1,4608]{1,0:T(2,128)(2,1)} %corrupt.1), channel_id=1, source_target_pairs={{0,32},{32,0},{1,33},{33,1},{2,34},{34,2},{3,35},{35,3},{4,36},{36... | collective-permute-start | bytes 27656 | tf_op jit(solution)/shard_map/ppermute | solution.py:272
  2.8 31.4 %copy-start = (bf16[288,4608]{1,0:T(8,128)(2,1)S(1)}, bf16[288,4608]{1,0:T(8,128)(2,1)}, u32[]{:S(2)}) copy-start(bf16[288,4608]{1,0:T(8,128)(2,1)} %w_down.7) | copy-start | bytes 7962628
  2.8 31.4 %copy-start.1 = (bf16[4608,288]{0,1:T(8,128)(2,1)S(1)}, bf16[4608,288]{0,1:T(8,128)(2,1)}, u32[]{:S(2)}) copy-start(bf16[4608,288]{0,1:T(8,128)(2,1)} %param.20) | copy-start | bytes 7962628
  2.8 31.4 %copy-start.2 = (bf16[4608,288]{0,1:T(8,128)(2,1)S(1)}, bf16[4608,288]{0,1:T(8,128)(2,1)}, u32[]{:S(2)}) copy-start(bf16[4608,288]{0,1:T(8,128)(2,1)} %param.21) | copy-start | bytes 7962628
  2.8 31.4 %copy-start.3 = (bf16[4608,512]{1,0:T(8,128)(2,1)S(1)}, bf16[4608,512]{1,0:T(8,128)(2,1)}, u32[]{:S(2)}) copy-start(bf16[4608,512]{1,0:T(8,128)(2,1)} %w_enc.3) | copy-start | bytes 14155780
  2.8 31.4 %copy-start.4 = (bf16[128,4608]{1,0:T(8,128)(2,1)S(1)}, bf16[128,4608]{1,0:T(8,128)(2,1)}, u32[]{:S(2)}) copy-start(bf16[128,4608]{1,0:T(8,128)(2,1)} %unembed.1) | copy-start | bytes 3538948
  2.8 31.4 %copy-start.5 = (f32[4608]{0:T(1024)S(1)}, f32[4608]{0:T(1024)}, u32[]{:S(2)}) copy-start(f32[4608]{0:T(1024)} %pre) | copy-start | bytes 55300
  2.8 31.4 %copy-start.6 = (f32[4608]{0:T(1024)S(1)}, f32[4608]{0:T(1024)}, u32[]{:S(2)}) copy-start(f32[4608]{0:T(1024)} %post.1) | copy-start | bytes 55300
  2.8 31.4 %copy-start.7 = (f32[4608]{0:T(1024)S(1)}, f32[4608]{0:T(1024)}, u32[]{:S(2)}) copy-start(f32[4608]{0:T(1024)} %final.1) | copy-start | bytes 55300
  34.2 2.3 %copy-start.9 = (s32[128,2]{0,1:T(2,128)S(1)}, s32[128,2]{0,1:T(2,128)}, u32[]{:S(2)}) copy-start(s32[128,2]{0,1:T(2,128)} %param.15) | copy-start | bytes 3076
  34.7 3.5 %collective-permute-start.2 = (bf16[128,2304]{1,0:T(8,128)(2,1)S(1)}, bf16[128,2304]{1,0:T(8,128)(2,1)S(1)}, u32[]{:S(2)}, u32[]{:S(2)}) collective-permute-start(bf16[128,2304]{1,0:T(8,128)(2,1)S(1)} %get-tuple-element.70.own), channel_id=1, source_target_pairs={{0,32},{32,0},{1,33},{33,1},{2,34},{34,2},{3,35},{35,3},{4,36},{36... | collective-permute-start | bytes 1769480 | tf_op jit(solution)/shard_map/ppermute | solution.py:272
  38.2 3.3 %collective-permute-start.3 = (bf16[128,2304]{1,0:T(8,128)(2,1)S(1)}, bf16[128,2304]{1,0:T(8,128)(2,1)S(1)}, u32[]{:S(2)}, u32[]{:S(2)}) collective-permute-start(bf16[128,2304]{1,0:T(8,128)(2,1)S(1)} %get-tuple-element.85.own), channel_id=1, source_target_pairs={{0,32},{32,0},{1,33},{33,1},{2,34},{34,2},{3,35},{35,3},{4,36},{36... | collective-permute-start | bytes 1769480 | tf_op jit(solution)/shard_map/ppermute | solution.py:272
  41.5 2.1 %collective-permute-start.4 = (bf16[128,2304]{1,0:T(8,128)(2,1)S(1)}, bf16[128,2304]{1,0:T(8,128)(2,1)S(1)}, u32[]{:S(2)}, u32[]{:S(2)}) collective-permute-start(bf16[128,2304]{1,0:T(8,128)(2,1)S(1)} %get-tuple-element.65), channel_id=1, source_target_pairs={{0,32},{32,0},{1,33},{33,1},{2,34},{34,2},{3,35},{35,3},{4,36},{36... | collective-permute-start | bytes 1769480 | tf_op jit(solution)/shard_map/ppermute | solution.py:272
  42.7 20.8 %copy-start.8 = (f32[512]{0:T(512)S(1)}, f32[512]{0:T(512)}, u32[]{:S(2)}) copy-start(f32[512]{0:T(512)} %param.24) | copy-start | bytes 6148
  61.8 3.1 %collective-permute-start.5 = (f32[2,2304]{1,0:T(2,128)S(1)}, f32[2,2304]{1,0:T(2,128)S(1)}, u32[]{:S(2)}, u32[]{:S(2)}) collective-permute-start(f32[2,2304]{1,0:T(2,128)S(1)} %shard_map.135.own), channel_id=1, source_target_pairs={{0,32},{32,0},{1,33},{33,1},{2,34},{34,2},{3,35},{35,3},{4,36},{36... | collective-permute-start | bytes 55304 | tf_op jit(solution)/shard_map/ppermute | solution.py:272
  83.9 3.1 %collective-permute-start.6 = (bf16[64,2,2304]{2,1,0:T(2,128)(2,1)S(1)}, bf16[64,2,2304]{2,1,0:T(2,128)(2,1)S(1)}, u32[]{:S(2)}, u32[]{:S(2)}) collective-permute-start(bf16[64,2,2304]{2,1,0:T(2,128)(2,1)S(1)} %all_to_all.27.own), channel_id=1, source_target_pairs={{0,32},{32,0},{1,33},{33,1},{2,34},{34,2},{3,35},{35,3},{4,36},{36... | collective-permute-start | bytes 1769480 | tf_op jit(solution)/shard_map/ppermute | solution.py:272
  88.9 2.1 %collective-permute-start.7 = (bf16[128,2304]{1,0:T(8,128)(2,1)S(1)}, bf16[128,2304]{1,0:T(8,128)(2,1)S(1)}, u32[]{:S(2)}, u32[]{:S(2)}) collective-permute-start(bf16[128,2304]{1,0:T(8,128)(2,1)S(1)} %get-tuple-element.79), channel_id=1, source_target_pairs={{0,32},{32,0},{1,33},{33,1},{2,34},{34,2},{3,35},{35,3},{4,36},{36... | collective-permute-start | bytes 1769480 | tf_op jit(solution)/shard_map/ppermute | solution.py:272
  109.0 23.7 %slice-start = ((s8[4718592]{0:T(1024)(128)(4,1)}), s8[4194304]{0:T(1024)(128)(4,1)S(1)}, s32[]{:S(2)}) async-start(s8[4718592]{0:T(1024)(128)(4,1)} %bitcast.15), calls=%async_computation.5 | async-start | bytes 8388608
  109.2 23.5 %slice-start.1 = ((s8[4718592]{0:T(1024)(128)(4,1)}), s8[524288]{0:T(1024)(128)(4,1)S(1)}, s32[]{:S(2)}) async-start(s8[4718592]{0:T(1024)(128)(4,1)} %bitcast.15), calls=%async_computation.6 | async-start | bytes 1048576
  109.2 3.3 %collective-permute-start.8 = (f32[2,2304]{1,0:T(2,128)S(1)}, f32[2,2304]{1,0:T(2,128)S(1)}, u32[]{:S(2)}, u32[]{:S(2)}) collective-permute-start(f32[2,2304]{1,0:T(2,128)S(1)} %shard_map.142.own), channel_id=1, source_target_pairs={{0,32},{32,0},{1,33},{33,1},{2,34},{34,2},{3,35},{35,3},{4,36},{36... | collective-permute-start | bytes 55304 | tf_op jit(solution)/shard_map/ppermute | solution.py:272
  131.2 3.1 %collective-permute-start.9 = (bf16[64,2,2304]{2,1,0:T(2,128)(2,1)S(1)}, bf16[64,2,2304]{2,1,0:T(2,128)(2,1)S(1)}, u32[]{:S(2)}, u32[]{:S(2)}) collective-permute-start(bf16[64,2,2304]{2,1,0:T(2,128)(2,1)S(1)} %all_to_all.29.own), channel_id=1, source_target_pairs={{0,32},{32,0},{1,33},{33,1},{2,34},{34,2},{3,35},{35,3},{4,36},{36... | collective-permute-start | bytes 1769480 | tf_op jit(solution)/shard_map/ppermute | solution.py:272

commit v4 on v3

--- a/solution.py
+++ b/solution.py
@@ -12,6 +12,7 @@
 
 DEVICES = ("y_lo", "core", "y_hi", "x", "z")
 CHIPS = ("x", "z", "y_lo", "y_hi")
+CORES = ("core", *CHIPS)
 SWAP = [(0, 1), (1, 0)]
 LIMIT = 16 << 20
 HINT = 10**11
@@ -147,22 +148,47 @@
 
 
 def chip_sum_kernel(own, arrived, out):
-    out[...] = (own[...] + arrived[...].astype(F32)).astype(BF16).reshape(out.shape)
+    width = out.shape[3]
+    for core in range(2):
+        part = slice(core * width, (core + 1) * width)
+        total = own[:, part] + arrived[:, part].astype(F32)
+        out[core] = total.astype(BF16).reshape(out.shape[1:])
 
 
 def total_kernel(pieces, out):
-    rows = pieces.shape[0] * pieces.shape[1]
+    rows = pieces.shape[1] * pieces.shape[2]
+    width = pieces.shape[3]
     token = lax.broadcasted_iota(jnp.int32, (8, rows), 0)
     source = lax.broadcasted_iota(jnp.int32, (8, rows), 1)
     pick = (source % 2 == token).astype(F32).astype(BF16)
-    out[...] = dot_nn(pick, pieces[...].reshape(rows, out.shape[1]))[: out.shape[0]]
+    for core in range(2):
+        part = dot_nn(pick, pieces[core].reshape(rows, width))
+        out[:, core * width : (core + 1) * width] = part[: out.shape[0]]
 
 
 def joined(where, own, other, out):
-    mine, theirs = halves(where, own.shape[1])
-    out[:, mine] = own[...]
-    out[:, theirs] = other[...]
+    width = own.shape[1] // 2
+    for core, ref in ((where[0], own), (1 - where[0], other)):
+        for i in range(2):
+            out[:, quarter(2 * i + core, width)] = ref[:, i * width : (i + 1) * width]
     return out[...]
+
+
+def quarter(index, width):
+    return pl.ds(pl.multiple_of(index * width, 128), width)
+
+
+def spread_quarters(where, whole, out):
+    width = out.shape[3]
+    for core in range(2):
+        value = whole[:, quarter(2 * core + where[0], width)].astype(BF16)
+        for chip in range(out.shape[1]):
+            out[core, chip] = value
+
+
+def token_rows(pieces):
+    rows = pieces.shape[1] * pieces.shape[2]
+    return jnp.concatenate([pieces[i].reshape(rows, pieces.shape[3]) for i in range(2)], axis=1)
 
 
 def wanted_kernel(where, answers, unembed, gains, out):
@@ -180,7 +206,6 @@
 def output_kernel(
     where, own, other, stream, weighted, gains, out, grad_output, whole
 ):
-    mine, _ = halves(where, out.shape[2])
     post_gain = gains[1:2]
     mlp_out = joined(where, own, other, whole)
     inv_post = lax.rsqrt(mean_row(mlp_out * mlp_out) + epsilon)
@@ -195,22 +220,19 @@
     whole[...] = inv_post * post_grad - mlp_out * (inv_post * inv_post * inv_post) * mean_row(
         post_grad * mlp_out
     )
-    spread(whole[:, mine].astype(BF16), out)
+    spread_quarters(where, whole, out)
 
 
 def backward_own_half_kernel(where, own, w_down, out):
-    mine, _ = halves(where, own.shape[2])
-    out[...] = dot_nt(w_down[:, mine], own[...].reshape(out.shape[1], own.shape[2]))
+    mine, _ = halves(where, 2 * own.shape[3])
+    out[...] = dot_nt(w_down[:, mine], token_rows(own))
 
 
 def backward_kernel(
     where, own_part, other, gate, up, w_gate, w_up, w_down, send, grad_gate, grad_up
 ):
-    width = other.shape[2]
-    _, theirs = halves(where, width)
-    grad_hidden = own_part[...] + dot_nt(
-        w_down[:, theirs], other[...].reshape(own_part.shape[1], width)
-    )
+    _, theirs = halves(where, 2 * other.shape[3])
+    grad_hidden = own_part[...] + dot_nt(w_down[:, theirs], token_rows(other))
     gate_pre = gate[...]
     to_gate = (grad_hidden * up[...] * gelu_slope(gate_pre)).T.astype(BF16)
     to_up = (grad_hidden * gelu_tanh(gate_pre)).T.astype(BF16)
@@ -225,7 +247,6 @@
 
 
 def input_kernel(where, own, other, stream, grad_output, gains, out, whole):
-    mine, _ = halves(where, out.shape[2])
     rows = stream[...]
     inv_pre = lax.rsqrt(mean_row(rows * rows) + epsilon)
     pre_grad = gains[0:1] * joined(where, own, other, whole)
@@ -234,7 +255,7 @@
         + inv_pre * pre_grad
         - rows * (inv_pre * inv_pre * inv_pre) * mean_row(pre_grad * rows)
     )
-    spread(whole[:, mine].astype(BF16), out)
+    spread_quarters(where, whole, out)
 
 
 def code_of(where, own, other, w_enc, b_enc):
@@ -253,19 +274,23 @@
 
 
 def attribution_own_kernel(where, own, w_dec, out):
-    mine, _ = halves(where, own.shape[2])
-    out[...] = dot_nt(w_dec[:, mine], own[...].reshape(out.shape[1], own.shape[2]))
+    mine, _ = halves(where, 2 * own.shape[3])
+    out[...] = dot_nt(w_dec[:, mine], token_rows(own))
 
 
 def attribution_kernel(where, part, other, w_dec, change, out):
-    width = other.shape[2]
-    _, theirs = halves(where, width)
-    projected = part[...] + dot_nt(w_dec[:, theirs], other[...].reshape(part.shape[1], width))
+    _, theirs = halves(where, 2 * other.shape[3])
+    projected = part[...] + dot_nt(w_dec[:, theirs], token_rows(other))
     out[...] = jnp.sum(change[...] * projected.T, axis=0, keepdims=True)
 
 
 def exchanged(blocks):
     return lax.all_to_all(blocks, CHIPS, 0, 0, tiled=True)
+
+
+def exchanged_by_core(blocks):
+    flat = blocks.reshape(-1, *blocks.shape[2:])
+    return lax.all_to_all(flat, CORES, 0, 0, tiled=True).reshape(blocks.shape)
 
 
 def swapped(value):
@@ -304,7 +329,7 @@
 
     halved = shape((tokens, half), BF16)
     halved32 = shape((tokens, half), F32)
-    pairs = shape((chips, 2, half), BF16)
+    pairs = shape((2, chips, 2, half // 2), BF16)
     pair_rows = shape((2, width), F32)
     pair_half = shape((2, half), F32)
     units = shape((tokens, hidden_units), BF16)
@@ -354,7 +379,7 @@
     own_sum = call(forward_own_kernel, halved32, where, hidden, w_down)
     arrived, own_sum = lax.optimization_barrier((arrived, own_sum))
     own_mlp = call(
-        total_kernel, pair_half, exchanged(call(chip_sum_kernel, pairs, own_sum, arrived))
+        total_kernel, pair_half, exchanged_by_core(call(chip_sum_kernel, pairs, own_sum, arrived))
     )
     own_mlp, own = lax.optimization_barrier((own_mlp, own))
     other_mlp = swapped(own_mlp)
@@ -367,7 +392,7 @@
         scratch=[whole],
     )
 
-    grad_own = exchanged(spread_grad)
+    grad_own = exchanged_by_core(spread_grad)
     grad_other = swapped(grad_own)
     own_part = call(backward_own_half_kernel, units32, where, grad_own, w_down)
     grad_other, own_part = lax.optimization_barrier((grad_other, own_part))
@@ -380,7 +405,7 @@
     own_sum = call(backward_own_kernel, halved32, where, grad_gate, grad_up, w_gate, w_up)
     arrived, own_sum = lax.optimization_barrier((arrived, own_sum))
     own_normed = call(
-        total_kernel, pair_half, exchanged(call(chip_sum_kernel, pairs, own_sum, arrived))
+        total_kernel, pair_half, exchanged_by_core(call(chip_sum_kernel, pairs, own_sum, arrived))
     )
     own_normed, own_corrupt = lax.optimization_barrier((own_normed, own_corrupt))
     other_normed = swapped(own_normed)
@@ -395,7 +420,7 @@
         scratch=[whole],
     )
 
-    last_own = exchanged(spread_stream)
+    last_own = exchanged_by_core(spread_stream)
     last_other = swapped(last_own)
     own_part = call(
         attribution_own_kernel, shape((latents, tokens), F32), where, last_own, w_dec

time: 137 us -> 134 us (0.978)
  starting transfers between devices: 10.8 us -> 7.96 us
    all_to_all x0 -> x4, blocking collectives: none -> 71.9 us  [exchanged_by_core(): return lax.all_to_all(flat, CORES, 0, 0, tiled=True).reshape(blocks.shape)]
    all_to_all x5 -> x1, blocking collectives: 102 us -> 30.7 us  [exchanged(): return lax.all_to_all(blocks, CHIPS, 0, 0, tiled=True)]
    ppermute x10, starting transfers between devices: 10.8 us -> 7.96 us  [swapped(): return lax.ppermute(value, 'core', SWAP)]
where the time goes in v4:
time: 134 us
  blocking collectives  103 us (77%)
  Pallas kernels  19.5 us (15%)
  starting transfers between devices  7.96 us (6%)
  waiting for transfers between devices  3.38 us (3%)
    all_to_all x4, blocking collectives, exchanged_by_core(): return lax.all_to_all(flat, CORES, 0, 0, tiled=True).reshape(blocks.shape)  71.9 us
    all_to_all x1, blocking collectives, exchanged(): return lax.all_to_all(blocks, CHIPS, 0, 0, tiled=True)  30.7 us
    pallas_call x20, Pallas kernels, call(): pl.pallas_call(kernel, out_shape=jax.tree.map(lambda o: space(o.shape, o....  19.5 us
    ppermute x10, starting transfers between devices, swapped(): return lax.ppermute(value, 'core', SWAP)  7.96 us
    ppermute x10, waiting for transfers between devices, swapped(): return lax.ppermute(value, 'core', SWAP)  3.38 us
  transfers between devices with their start and end apart: 10, of which 7 were waited for; matrix products, arithmetic and copies ran while one was open for 0% of the time, Pallas kernels for 9%

profile of v4, /device:TPU:1, one launch (start us, length us, event | category | flops | bytes accessed | tf_op | source)
XLA Modules:
  0.0 133.8 jit_solution(10590692019698790033)
XLA Ops:
  0.0 1.4 %collective-permute-start = (bf16[1,4608]{1,0:T(2,128)(2,1)}, bf16[1,4608]{1,0:T(2,128)(2,1)S(1)}, u32[]{:S(2)}, u32[]{:S(2)}) collective-permute-start(bf16[1,4608]{1,0:T(2,128)(2,1)} %clean.1), channel_id=1, source_target_pairs={{0,32},{32,0},{1,33},{33,1},{2,34},{34,2},{3,35},{35,3},{4,36},{36... | collective-permute-start | bytes 27656 | tf_op jit(solution)/shard_map/ppermute | solution.py:297
  1.4 0.1 pad_add_fusion.where
  1.5 0.8 shard_map.127
  2.2 0.2 collective-permute-done.other_clean
  2.4 0.3 collective-permute-done.1.other_corrupt
  2.8 0.0 copy-start.4
  2.8 0.0 copy-start.5
  2.8 0.0 copy-start.6
  2.8 0.0 copy-start.7
  2.8 0.7 shard_map.128
  3.5 30.7 %all_to_all.25.pieces = bf16[64,4,2304]{2,1,0:T(4,128)(2,1)S(1)} all-to-all(bf16[64,4,2304]{2,1,0:T(4,128)(2,1)S(1)} %get-tuple-element.56), channel_id=1, replica_groups=mesh['y_lo'=2,'core'=2,'y_hi'=2,'x'=4,'z'=4] {'x','z','y_lo','y_hi'}, dimensions={0} | all-to-all | bytes 2359296 | tf_op jit(solution)/shard_map/all_to_all | solution.py:288
  34.2 0.0 copy-start.9
  34.3 0.4 shard_map.129
  34.7 1.9 %collective-permute-start.2 = (bf16[128,2304]{1,0:T(8,128)(2,1)S(1)}, bf16[128,2304]{1,0:T(8,128)(2,1)S(1)}, u32[]{:S(2)}, u32[]{:S(2)}) collective-permute-start(bf16[128,2304]{1,0:T(8,128)(2,1)S(1)} %get-tuple-element.70.own), channel_id=1, source_target_pairs={{0,32},{32,0},{1,33},{33,1},{2,34},{34,2},{3,35},{35,3},{4,36},{36... | collective-permute-start | bytes 1769480 | tf_op jit(solution)/shard_map/ppermute | solution.py:297
  36.6 0.8 shard_map.131.weighted
  37.4 0.8 collective-permute-done.2.other
  38.2 0.4 collective-permute-start.3
  38.5 2.9 %shard_map.132 = (bf16[128,2304]{1,0:T(8,128)(2,1)S(1)}, bf16[128,288]{1,0:T(8,128)(2,1)S(1)}, f32[288,128]{1,0:T(8,128)S(1)}, f32[288,128]{1,0:T(8,128)S(1)}) custom-call(s32[3]{0:T(128)S(1)} %pad_add_fusion.where, bf16[128,2304]{1,0:T(8,128)(2,1)S(1)} %get-tuple-element.70.own, bf16[128,2304]{1,0:T(8,128)(2,1)S(1)} %collective-permute-done.2.other, ...), custom_call_target="tpu_custom_call" | custom-call | tf_op jit(solution)/shard_map/pallas_call | solution.py:31
  41.5 0.2 collective-permute-start.4
  41.7 1.0 shard_map.133.own
  42.7 0.0 copy-start.8
  42.7 0.8 collective-permute-done.4.arrived
  43.6 0.2 shard_map.134
  43.8 17.6 %all_to_all.26 = bf16[128,2,1152]{2,1,0:T(2,128)(2,1)S(1)} all-to-all(bf16[128,2,1152]{2,1,0:T(2,128)(2,1)S(1)} %bitcast.32), channel_id=1, replica_groups=mesh['y_lo'=2,'core'=2,'y_hi'=2,'x'=4,'z'=4] {'core','x','z','y_lo','y_hi'}, dimensions={0} | all-to-all | bytes 1179648 | tf_op jit(solution)/shard_map/all_to_all | solution.py:293
  61.4 0.2 shard_map.135.own
  61.6 0.9 collective-permute-start.5
  62.5 1.3 shard_map.136.clean_code
  63.9 1.0 shard_map.137
  64.9 18.0 %all_to_all.27 = bf16[128,2,1152]{2,1,0:T(2,128)(2,1)S(1)} all-to-all(bf16[128,2,1152]{2,1,0:T(2,128)(2,1)S(1)} %bitcast.34), channel_id=1, replica_groups=mesh['y_lo'=2,'core'=2,'y_hi'=2,'x'=4,'z'=4] {'core','x','z','y_lo','y_hi'}, dimensions={0} | all-to-all | bytes 1179648 | tf_op jit(solution)/shard_map/all_to_all | solution.py:293
  82.9 0.8 collective-permute-start.6
  83.8 1.1 shard_map.138.own_part
  84.8 0.6 collective-permute-done.6.other
  85.4 2.0 %shard_map.139 = (bf16[128,2304]{1,0:T(8,128)(2,1)S(1)}, bf16[128,288]{1,0:T(8,128)(2,1)S(1)}, bf16[128,288]{1,0:T(8,128)(2,1)S(1)}) custom-call(s32[3]{0:T(128)S(1)} %pad_add_fusion.where, f32[288,128]{1,0:T(8,128)S(1)} %shard_map.138.own_part, bf16[2,64,2,1152]{3,2,1,0:T(2,128)(2,1)S(1)} %collective-permute-done.6.other, ...), custom_call_target="tpu_custom_call" | custom-call | tf_op jit(solution)/shard_map/pallas_call | solution.py:31
  87.4 0.5 collective-permute-start.7
  87.8 1.3 shard_map.140.own
  89.1 0.3 collective-permute-done.7.arrived
  89.4 0.2 shard_map.141
  89.6 18.2 %all_to_all.28 = bf16[128,2,1152]{2,1,0:T(2,128)(2,1)S(1)} all-to-all(bf16[128,2,1152]{2,1,0:T(2,128)(2,1)S(1)} %bitcast.33), channel_id=1, replica_groups=mesh['y_lo'=2,'core'=2,'y_hi'=2,'x'=4,'z'=4] {'core','x','z','y_lo','y_hi'}, dimensions={0} | all-to-all | bytes 1179648 | tf_op jit(solution)/shard_map/all_to_all | solution.py:293
  107.9 0.2 shard_map.142.own
  108.1 0.0 slice-start.1
  108.1 1.1 collective-permute-start.8
  109.2 1.3 shard_map.143.change
  110.6 0.8 shard_map.144
  111.3 18.0 %all_to_all.29 = bf16[128,2,1152]{2,1,0:T(2,128)(2,1)S(1)} all-to-all(bf16[128,2,1152]{2,1,0:T(2,128)(2,1)S(1)} %bitcast.25), channel_id=1, replica_groups=mesh['y_lo'=2,'core'=2,'y_hi'=2,'x'=4,'z'=4] {'core','x','z','y_lo','y_hi'}, dimensions={0} | all-to-all | bytes 1179648 | tf_op jit(solution)/shard_map/all_to_all | solution.py:293
  129.3 0.8 collective-permute-start.9
  130.2 1.3 shard_map.145.part
  131.5 0.3 collective-permute-done.9.other
  131.8 2.0 %shard_map.146 = f32[1,512]{1,0:T(1,128)} custom-call(s32[3]{0:T(128)S(1)} %pad_add_fusion.where, f32[512,128]{1,0:T(8,128)S(1)} %shard_map.145.part, bf16[2,64,2,1152]{3,2,1,0:T(2,128)(2,1)S(1)} %collective-permute-done.9.other, bf16[512,4608]{1,0:T(8,128)(2,1)S(1)} %bitcast.24, f32[128,512]{1,0:T(8,128)S(1)} %shard_map.143.change), custom_call_target="tpu_custom_call" | custom-call | tf_op jit(solution)/shard_map/pallas_call | solution.py:31
  (23 shorter events, 0.1 us)
Async XLA Ops:
  0.0 2.4 %collective-permute-start = (bf16[1,4608]{1,0:T(2,128)(2,1)}, bf16[1,4608]{1,0:T(2,128)(2,1)S(1)}, u32[]{:S(2)}, u32[]{:S(2)}) collective-permute-start(bf16[1,4608]{1,0:T(2,128)(2,1)} %clean.1), channel_id=1, source_target_pairs={{0,32},{32,0},{1,33},{33,1},{2,34},{34,2},{3,35},{35,3},{4,36},{36... | collective-permute-start | bytes 27656 | tf_op jit(solution)/shard_map/ppermute | solution.py:297
  1.4 1.4 %collective-permute-start.1 = (bf16[1,4608]{1,0:T(2,128)(2,1)}, bf16[1,4608]{1,0:T(2,128)(2,1)S(1)}, u32[]{:S(2)}, u32[]{:S(2)}) collective-permute-start(bf16[1,4608]{1,0:T(2,128)(2,1)} %corrupt.1), channel_id=1, source_target_pairs={{0,32},{32,0},{1,33},{33,1},{2,34},{34,2},{3,35},{35,3},{4,36},{36... | collective-permute-start | bytes 27656 | tf_op jit(solution)/shard_map/ppermute | solution.py:297
  2.8 31.4 %copy-start = (bf16[288,4608]{1,0:T(8,128)(2,1)S(1)}, bf16[288,4608]{1,0:T(8,128)(2,1)}, u32[]{:S(2)}) copy-start(bf16[288,4608]{1,0:T(8,128)(2,1)} %w_down.7) | copy-start | bytes 7962628
  2.8 31.4 %copy-start.1 = (bf16[4608,288]{0,1:T(8,128)(2,1)S(1)}, bf16[4608,288]{0,1:T(8,128)(2,1)}, u32[]{:S(2)}) copy-start(bf16[4608,288]{0,1:T(8,128)(2,1)} %param.20) | copy-start | bytes 7962628
  2.8 31.4 %copy-start.2 = (bf16[4608,288]{0,1:T(8,128)(2,1)S(1)}, bf16[4608,288]{0,1:T(8,128)(2,1)}, u32[]{:S(2)}) copy-start(bf16[4608,288]{0,1:T(8,128)(2,1)} %param.21) | copy-start | bytes 7962628
  2.8 31.4 %copy-start.3 = (bf16[4608,512]{1,0:T(8,128)(2,1)S(1)}, bf16[4608,512]{1,0:T(8,128)(2,1)}, u32[]{:S(2)}) copy-start(bf16[4608,512]{1,0:T(8,128)(2,1)} %w_enc.3) | copy-start | bytes 14155780
  2.8 31.4 %copy-start.4 = (bf16[128,4608]{1,0:T(8,128)(2,1)S(1)}, bf16[128,4608]{1,0:T(8,128)(2,1)}, u32[]{:S(2)}) copy-start(bf16[128,4608]{1,0:T(8,128)(2,1)} %unembed.1) | copy-start | bytes 3538948
  2.8 31.4 %copy-start.5 = (f32[4608]{0:T(1024)S(1)}, f32[4608]{0:T(1024)}, u32[]{:S(2)}) copy-start(f32[4608]{0:T(1024)} %pre) | copy-start | bytes 55300
  2.8 31.4 %copy-start.6 = (f32[4608]{0:T(1024)S(1)}, f32[4608]{0:T(1024)}, u32[]{:S(2)}) copy-start(f32[4608]{0:T(1024)} %post.1) | copy-start | bytes 55300
  2.8 31.4 %copy-start.7 = (f32[4608]{0:T(1024)S(1)}, f32[4608]{0:T(1024)}, u32[]{:S(2)}) copy-start(f32[4608]{0:T(1024)} %final.1) | copy-start | bytes 55300
  34.2 2.3 %copy-start.9 = (s32[128,2]{0,1:T(2,128)S(1)}, s32[128,2]{0,1:T(2,128)}, u32[]{:S(2)}) copy-start(s32[128,2]{0,1:T(2,128)} %param.15) | copy-start | bytes 3076
  34.7 3.5 %collective-permute-start.2 = (bf16[128,2304]{1,0:T(8,128)(2,1)S(1)}, bf16[128,2304]{1,0:T(8,128)(2,1)S(1)}, u32[]{:S(2)}, u32[]{:S(2)}) collective-permute-start(bf16[128,2304]{1,0:T(8,128)(2,1)S(1)} %get-tuple-element.70.own), channel_id=1, source_target_pairs={{0,32},{32,0},{1,33},{33,1},{2,34},{34,2},{3,35},{35,3},{4,36},{36... | collective-permute-start | bytes 1769480 | tf_op jit(solution)/shard_map/ppermute | solution.py:297
  38.2 3.3 %collective-permute-start.3 = (bf16[128,2304]{1,0:T(8,128)(2,1)S(1)}, bf16[128,2304]{1,0:T(8,128)(2,1)S(1)}, u32[]{:S(2)}, u32[]{:S(2)}) collective-permute-start(bf16[128,2304]{1,0:T(8,128)(2,1)S(1)} %get-tuple-element.85.own), channel_id=1, source_target_pairs={{0,32},{32,0},{1,33},{33,1},{2,34},{34,2},{3,35},{35,3},{4,36},{36... | collective-permute-start | bytes 1769480 | tf_op jit(solution)/shard_map/ppermute | solution.py:297
  41.5 2.1 %collective-permute-start.4 = (bf16[128,2304]{1,0:T(8,128)(2,1)S(1)}, bf16[128,2304]{1,0:T(8,128)(2,1)S(1)}, u32[]{:S(2)}, u32[]{:S(2)}) collective-permute-start(bf16[128,2304]{1,0:T(8,128)(2,1)S(1)} %get-tuple-element.65), channel_id=1, source_target_pairs={{0,32},{32,0},{1,33},{33,1},{2,34},{34,2},{3,35},{35,3},{4,36},{36... | collective-permute-start | bytes 1769480 | tf_op jit(solution)/shard_map/ppermute | solution.py:297
  42.7 19.8 %copy-start.8 = (f32[512]{0:T(512)S(1)}, f32[512]{0:T(512)}, u32[]{:S(2)}) copy-start(f32[512]{0:T(512)} %param.24) | copy-start | bytes 6148
  61.6 2.3 %collective-permute-start.5 = (f32[2,2304]{1,0:T(2,128)S(1)}, f32[2,2304]{1,0:T(2,128)S(1)}, u32[]{:S(2)}, u32[]{:S(2)}) collective-permute-start(f32[2,2304]{1,0:T(2,128)S(1)} %shard_map.135.own), channel_id=1, source_target_pairs={{0,32},{32,0},{1,33},{33,1},{2,34},{34,2},{3,35},{35,3},{4,36},{36... | collective-permute-start | bytes 55304 | tf_op jit(solution)/shard_map/ppermute | solution.py:297
  82.9 2.5 %collective-permute-start.6 = (bf16[2,64,2,1152]{3,2,1,0:T(2,128)(2,1)S(1)}, bf16[2,64,2,1152]{3,2,1,0:T(2,128)(2,1)S(1)}, u32[]{:S(2)}, u32[]{:S(2)}) collective-permute-start(bf16[2,64,2,1152]{3,2,1,0:T(2,128)(2,1)S(1)} %bitcast.28), channel_id=1, source_target_pairs={{0,32},{32,0},{1,33},{33,1},{2,34},{34,2},{3,35},{35,3},{4,36},{36... | collective-permute-start | bytes 1769480 | tf_op jit(solution)/shard_map/ppermute | solution.py:297
  87.4 2.1 %collective-permute-start.7 = (bf16[128,2304]{1,0:T(8,128)(2,1)S(1)}, bf16[128,2304]{1,0:T(8,128)(2,1)S(1)}, u32[]{:S(2)}, u32[]{:S(2)}) collective-permute-start(bf16[128,2304]{1,0:T(8,128)(2,1)S(1)} %get-tuple-element.79), channel_id=1, source_target_pairs={{0,32},{32,0},{1,33},{33,1},{2,34},{34,2},{3,35},{35,3},{4,36},{36... | collective-permute-start | bytes 1769480 | tf_op jit(solution)/shard_map/ppermute | solution.py:297
  107.9 22.3 %slice-start = ((s8[4718592]{0:T(1024)(128)(4,1)}), s8[4194304]{0:T(1024)(128)(4,1)S(1)}, s32[]{:S(2)}) async-start(s8[4718592]{0:T(1024)(128)(4,1)} %bitcast.23), calls=%async_computation.5 | async-start | bytes 8388608
  108.1 22.1 %slice-start.1 = ((s8[4718592]{0:T(1024)(128)(4,1)}), s8[524288]{0:T(1024)(128)(4,1)S(1)}, s32[]{:S(2)}) async-start(s8[4718592]{0:T(1024)(128)(4,1)} %bitcast.23), calls=%async_computation.6 | async-start | bytes 1048576
  108.1 2.4 %collective-permute-start.8 = (f32[2,2304]{1,0:T(2,128)S(1)}, f32[2,2304]{1,0:T(2,128)S(1)}, u32[]{:S(2)}, u32[]{:S(2)}) collective-permute-start(f32[2,2304]{1,0:T(2,128)S(1)} %shard_map.142.own), channel_id=1, source_target_pairs={{0,32},{32,0},{1,33},{33,1},{2,34},{34,2},{3,35},{35,3},{4,36},{36... | collective-permute-start | bytes 55304 | tf_op jit(solution)/shard_map/ppermute | solution.py:297
  129.3 2.5 %collective-permute-start.9 = (bf16[2,64,2,1152]{3,2,1,0:T(2,128)(2,1)S(1)}, bf16[2,64,2,1152]{3,2,1,0:T(2,128)(2,1)S(1)}, u32[]{:S(2)}, u32[]{:S(2)}) collective-permute-start(bf16[2,64,2,1152]{3,2,1,0:T(2,128)(2,1)S(1)} %bitcast.30), channel_id=1, source_target_pairs={{0,32},{32,0},{1,33},{33,1},{2,34},{34,2},{3,35},{35,3},{4,36},{36... | collective-permute-start | bytes 1769480 | tf_op jit(solution)/shard_map/ppermute | solution.py:297

commit v5 on v4

--- a/solution.py
+++ b/solution.py
@@ -11,8 +11,8 @@
 gelu_cubic = 0.044715
 
 DEVICES = ("y_lo", "core", "y_hi", "x", "z")
-CHIPS = ("x", "z", "y_lo", "y_hi")
-CORES = ("core", *CHIPS)
+CHIPS = ("y_hi", "z", "y_lo", "x")
+CORES = (*CHIPS, "core")
 SWAP = [(0, 1), (1, 0)]
 LIMIT = 16 << 20
 HINT = 10**11
@@ -152,17 +152,17 @@
     for core in range(2):
         part = slice(core * width, (core + 1) * width)
         total = own[:, part] + arrived[:, part].astype(F32)
-        out[core] = total.astype(BF16).reshape(out.shape[1:])
+        out[:, core] = total.astype(BF16).reshape(out.shape[0], 2, width)
 
 
 def total_kernel(pieces, out):
-    rows = pieces.shape[1] * pieces.shape[2]
+    rows = pieces.shape[0] * pieces.shape[2]
     width = pieces.shape[3]
     token = lax.broadcasted_iota(jnp.int32, (8, rows), 0)
     source = lax.broadcasted_iota(jnp.int32, (8, rows), 1)
     pick = (source % 2 == token).astype(F32).astype(BF16)
     for core in range(2):
-        part = dot_nn(pick, pieces[core].reshape(rows, width))
+        part = dot_nn(pick, pieces[:, core].reshape(rows, width))
         out[:, core * width : (core + 1) * width] = part[: out.shape[0]]
 
 
@@ -182,13 +182,13 @@
     width = out.shape[3]
     for core in range(2):
         value = whole[:, quarter(2 * core + where[0], width)].astype(BF16)
-        for chip in range(out.shape[1]):
-            out[core, chip] = value
+        for chip in range(out.shape[0]):
+            out[chip, core] = value
 
 
 def token_rows(pieces):
-    rows = pieces.shape[1] * pieces.shape[2]
-    return jnp.concatenate([pieces[i].reshape(rows, pieces.shape[3]) for i in range(2)], axis=1)
+    rows = pieces.shape[0] * pieces.shape[2]
+    return jnp.concatenate([pieces[:, i].reshape(rows, pieces.shape[3]) for i in range(2)], axis=1)
 
 
 def wanted_kernel(where, answers, unembed, gains, out):
@@ -329,7 +329,7 @@
 
     halved = shape((tokens, half), BF16)
     halved32 = shape((tokens, half), F32)
-    pairs = shape((2, chips, 2, half // 2), BF16)
+    pairs = shape((chips, 2, 2, half // 2), BF16)
     pair_rows = shape((2, width), F32)
     pair_half = shape((2, half), F32)
     units = shape((tokens, hidden_units), BF16)

time: 134 us -> 132 us (0.985)
  starting transfers between devices: 7.96 us -> 6.46 us
    ppermute x10, starting transfers between devices: 7.96 us -> 6.46 us  [swapped(): return lax.ppermute(value, 'core', SWAP)]
where the time goes in v5:
time: 132 us
  blocking collectives  102 us (77%)
  Pallas kernels  19.5 us (15%)
  starting transfers between devices  6.46 us (5%)
  waiting for transfers between devices  3.38 us (3%)
    all_to_all x4, blocking collectives, exchanged_by_core(): return lax.all_to_all(flat, CORES, 0, 0, tiled=True).reshape(blocks.shape)  71.6 us
    all_to_all x1, blocking collectives, exchanged(): return lax.all_to_all(blocks, CHIPS, 0, 0, tiled=True)  30.9 us
    pallas_call x20, Pallas kernels, call(): pl.pallas_call(kernel, out_shape=jax.tree.map(lambda o: space(o.shape, o....  19.5 us
    ppermute x10, starting transfers between devices, swapped(): return lax.ppermute(value, 'core', SWAP)  6.46 us
    ppermute x10, waiting for transfers between devices, swapped(): return lax.ppermute(value, 'core', SWAP)  3.38 us
  transfers between devices with their start and end apart: 10, of which 7 were waited for; matrix products, arithmetic and copies ran while one was open for 0% of the time, Pallas kernels for 9%

profile of v5, /device:TPU:1, one launch (start us, length us, event | category | flops | bytes accessed | tf_op | source)
XLA Modules:
  0.0 132.2 jit_solution(18376012844304586513)
XLA Ops:
  0.0 1.4 %collective-permute-start = (bf16[1,4608]{1,0:T(2,128)(2,1)}, bf16[1,4608]{1,0:T(2,128)(2,1)S(1)}, u32[]{:S(2)}, u32[]{:S(2)}) collective-permute-start(bf16[1,4608]{1,0:T(2,128)(2,1)} %clean.1), channel_id=1, source_target_pairs={{0,32},{32,0},{1,33},{33,1},{2,34},{34,2},{3,35},{35,3},{4,36},{36... | collective-permute-start | bytes 27656 | tf_op jit(solution)/shard_map/ppermute | solution.py:297
  1.4 0.1 pad_add_fusion.where
  1.5 0.8 shard_map.127
  2.2 0.2 collective-permute-done.other_clean
  2.4 0.3 collective-permute-done.1.other_corrupt
  2.8 0.0 copy-start.4
  2.8 0.0 copy-start.5
  2.8 0.0 copy-start.6
  2.8 0.0 copy-start.7
  2.8 0.7 shard_map.128
  3.5 30.9 %all_to_all.25.pieces = bf16[64,4,2304]{2,1,0:T(4,128)(2,1)S(1)} all-to-all(bf16[64,4,2304]{2,1,0:T(4,128)(2,1)S(1)} %get-tuple-element.56), channel_id=1, replica_groups=mesh['y_lo'=2,'core'=2,'y_hi'=2,'x'=4,'z'=4] {'y_hi','z','y_lo','x'}, dimensions={0} | all-to-all | bytes 2359296 | tf_op jit(solution)/shard_map/all_to_all | solution.py:288
  34.4 0.0 copy-start.9
  34.5 0.4 shard_map.129
  34.9 1.7 %collective-permute-start.2 = (bf16[128,2304]{1,0:T(8,128)(2,1)S(1)}, bf16[128,2304]{1,0:T(8,128)(2,1)S(1)}, u32[]{:S(2)}, u32[]{:S(2)}) collective-permute-start(bf16[128,2304]{1,0:T(8,128)(2,1)S(1)} %get-tuple-element.70.own), channel_id=1, source_target_pairs={{0,32},{32,0},{1,33},{33,1},{2,34},{34,2},{3,35},{35,3},{4,36},{36... | collective-permute-start | bytes 1769480 | tf_op jit(solution)/shard_map/ppermute | solution.py:297
  36.6 0.8 shard_map.131.weighted
  37.5 0.8 collective-permute-done.2.other
  38.3 0.4 collective-permute-start.3
  38.6 2.9 %shard_map.132 = (bf16[128,2304]{1,0:T(8,128)(2,1)S(1)}, bf16[128,288]{1,0:T(8,128)(2,1)S(1)}, f32[288,128]{1,0:T(8,128)S(1)}, f32[288,128]{1,0:T(8,128)S(1)}) custom-call(s32[3]{0:T(128)S(1)} %pad_add_fusion.where, bf16[128,2304]{1,0:T(8,128)(2,1)S(1)} %get-tuple-element.70.own, bf16[128,2304]{1,0:T(8,128)(2,1)S(1)} %collective-permute-done.2.other, ...), custom_call_target="tpu_custom_call" | custom-call | tf_op jit(solution)/shard_map/pallas_call | solution.py:31
  41.6 0.2 collective-permute-start.4
  41.8 1.0 shard_map.133.own
  42.8 0.0 copy-start.8
  42.8 0.8 collective-permute-done.4.arrived
  43.7 0.2 shard_map.134
  43.9 17.8 %all_to_all.26 = bf16[128,2,1152]{2,1,0:T(2,128)(2,1)S(1)} all-to-all(bf16[128,2,1152]{2,1,0:T(2,128)(2,1)S(1)} %bitcast.32), channel_id=1, replica_groups=mesh['y_lo'=2,'core'=2,'y_hi'=2,'x'=4,'z'=4] {'y_hi','z','y_lo','x','core'}, dimensions={0} | all-to-all | bytes 1179648 | tf_op jit(solution)/shard_map/all_to_all | solution.py:293
  61.7 0.2 shard_map.135.own
  61.9 0.6 collective-permute-start.5
  62.5 1.3 %shard_map.136.clean_code = f32[128,512]{1,0:T(8,128)S(1)} custom-call(s32[3]{0:T(128)S(1)} %pad_add_fusion.where, bf16[128,2304]{1,0:T(8,128)(2,1)S(1)} %get-tuple-element.70.own, bf16[128,2304]{1,0:T(8,128)(2,1)S(1)} %collective-permute-done.2.other, bf16[4608,512]{1,0:T(8,128)(2,1)S(1)} %copy-done.3, f32[1,512]{1,0:T(1,128)S(1)} %bitcast.35), custom_call_target="tpu_custom_call" | custom-call | tf_op jit(solution)/shard_map/pallas_call | solution.py:31
  63.8 1.0 shard_map.137
  64.9 17.8 %all_to_all.27 = bf16[128,2,1152]{2,1,0:T(2,128)(2,1)S(1)} all-to-all(bf16[128,2,1152]{2,1,0:T(2,128)(2,1)S(1)} %bitcast.34), channel_id=1, replica_groups=mesh['y_lo'=2,'core'=2,'y_hi'=2,'x'=4,'z'=4] {'y_hi','z','y_lo','x','core'}, dimensions={0} | all-to-all | bytes 1179648 | tf_op jit(solution)/shard_map/all_to_all | solution.py:293
  82.7 0.5 collective-permute-start.6
  83.2 1.1 shard_map.138.own_part
  84.3 0.6 collective-permute-done.6.other
  84.8 2.0 %shard_map.139 = (bf16[128,2304]{1,0:T(8,128)(2,1)S(1)}, bf16[128,288]{1,0:T(8,128)(2,1)S(1)}, bf16[128,288]{1,0:T(8,128)(2,1)S(1)}) custom-call(s32[3]{0:T(128)S(1)} %pad_add_fusion.where, f32[288,128]{1,0:T(8,128)S(1)} %shard_map.138.own_part, bf16[64,2,2,1152]{3,2,1,0:T(2,128)(2,1)S(1)} %collective-permute-done.6.other, ...), custom_call_target="tpu_custom_call" | custom-call | tf_op jit(solution)/shard_map/pallas_call | solution.py:31
  86.8 0.5 collective-permute-start.7
  87.3 1.3 shard_map.140.own
  88.6 0.3 collective-permute-done.7.arrived
  88.9 0.2 shard_map.141
  89.1 18.1 %all_to_all.28 = bf16[128,2,1152]{2,1,0:T(2,128)(2,1)S(1)} all-to-all(bf16[128,2,1152]{2,1,0:T(2,128)(2,1)S(1)} %bitcast.33), channel_id=1, replica_groups=mesh['y_lo'=2,'core'=2,'y_hi'=2,'x'=4,'z'=4] {'y_hi','z','y_lo','x','core'}, dimensions={0} | all-to-all | bytes 1179648 | tf_op jit(solution)/shard_map/all_to_all | solution.py:293
  107.2 0.2 shard_map.142.own
  107.4 0.0 slice-start.1
  107.4 0.7 collective-permute-start.8
  108.2 1.3 %shard_map.143.change = f32[128,512]{1,0:T(8,128)S(1)} custom-call(s32[3]{0:T(128)S(1)} %pad_add_fusion.where, bf16[128,2304]{1,0:T(8,128)(2,1)S(1)} %get-tuple-element.85.own, bf16[128,2304]{1,0:T(8,128)(2,1)S(1)} %collective-permute-done.3.other, bf16[4608,512]{1,0:T(8,128)(2,1)S(1)} %copy-done.3, f32[1,512]{1,0:T(1,128)S(1)} %bitcast.36, ...), custom_call_target="tpu_custom_call" | custom-call | tf_op jit(solution)/shard_map/pallas_call | solution.py:31
  109.5 0.8 shard_map.144
  110.3 17.8 %all_to_all.29 = bf16[128,2,1152]{2,1,0:T(2,128)(2,1)S(1)} all-to-all(bf16[128,2,1152]{2,1,0:T(2,128)(2,1)S(1)} %bitcast.25), channel_id=1, replica_groups=mesh['y_lo'=2,'core'=2,'y_hi'=2,'x'=4,'z'=4] {'y_hi','z','y_lo','x','core'}, dimensions={0} | all-to-all | bytes 1179648 | tf_op jit(solution)/shard_map/all_to_all | solution.py:293
  128.1 0.5 collective-permute-start.9
  128.6 1.3 %shard_map.145.part = f32[512,128]{1,0:T(8,128)S(1)} custom-call(s32[3]{0:T(128)S(1)} %pad_add_fusion.where, bf16[64,2,2,1152]{3,2,1,0:T(2,128)(2,1)S(1)} %bitcast.31, bf16[512,4608]{1,0:T(8,128)(2,1)S(1)} %bitcast.24), custom_call_target="tpu_custom_call" | custom-call | tf_op jit(solution)/shard_map/pallas_call | solution.py:31
  130.0 0.3 collective-permute-done.9.other
  130.3 2.0 %shard_map.146 = f32[1,512]{1,0:T(1,128)} custom-call(s32[3]{0:T(128)S(1)} %pad_add_fusion.where, f32[512,128]{1,0:T(8,128)S(1)} %shard_map.145.part, bf16[64,2,2,1152]{3,2,1,0:T(2,128)(2,1)S(1)} %collective-permute-done.9.other, bf16[512,4608]{1,0:T(8,128)(2,1)S(1)} %bitcast.24, f32[128,512]{1,0:T(8,128)S(1)} %shard_map.143.change), custom_call_target="tpu_custom_call" | custom-call | tf_op jit(solution)/shard_map/pallas_call | solution.py:31
  (23 shorter events, 0.1 us)
Async XLA Ops:
  0.0 2.4 %collective-permute-start = (bf16[1,4608]{1,0:T(2,128)(2,1)}, bf16[1,4608]{1,0:T(2,128)(2,1)S(1)}, u32[]{:S(2)}, u32[]{:S(2)}) collective-permute-start(bf16[1,4608]{1,0:T(2,128)(2,1)} %clean.1), channel_id=1, source_target_pairs={{0,32},{32,0},{1,33},{33,1},{2,34},{34,2},{3,35},{35,3},{4,36},{36... | collective-permute-start | bytes 27656 | tf_op jit(solution)/shard_map/ppermute | solution.py:297
  1.4 1.4 %collective-permute-start.1 = (bf16[1,4608]{1,0:T(2,128)(2,1)}, bf16[1,4608]{1,0:T(2,128)(2,1)S(1)}, u32[]{:S(2)}, u32[]{:S(2)}) collective-permute-start(bf16[1,4608]{1,0:T(2,128)(2,1)} %corrupt.1), channel_id=1, source_target_pairs={{0,32},{32,0},{1,33},{33,1},{2,34},{34,2},{3,35},{35,3},{4,36},{36... | collective-permute-start | bytes 27656 | tf_op jit(solution)/shard_map/ppermute | solution.py:297
  2.8 31.6 %copy-start = (bf16[288,4608]{1,0:T(8,128)(2,1)S(1)}, bf16[288,4608]{1,0:T(8,128)(2,1)}, u32[]{:S(2)}) copy-start(bf16[288,4608]{1,0:T(8,128)(2,1)} %w_down.7) | copy-start | bytes 7962628
  2.8 31.6 %copy-start.1 = (bf16[4608,288]{0,1:T(8,128)(2,1)S(1)}, bf16[4608,288]{0,1:T(8,128)(2,1)}, u32[]{:S(2)}) copy-start(bf16[4608,288]{0,1:T(8,128)(2,1)} %param.20) | copy-start | bytes 7962628
  2.8 31.6 %copy-start.2 = (bf16[4608,288]{0,1:T(8,128)(2,1)S(1)}, bf16[4608,288]{0,1:T(8,128)(2,1)}, u32[]{:S(2)}) copy-start(bf16[4608,288]{0,1:T(8,128)(2,1)} %param.21) | copy-start | bytes 7962628
  2.8 31.6 %copy-start.3 = (bf16[4608,512]{1,0:T(8,128)(2,1)S(1)}, bf16[4608,512]{1,0:T(8,128)(2,1)}, u32[]{:S(2)}) copy-start(bf16[4608,512]{1,0:T(8,128)(2,1)} %w_enc.3) | copy-start | bytes 14155780
  2.8 31.6 %copy-start.4 = (bf16[128,4608]{1,0:T(8,128)(2,1)S(1)}, bf16[128,4608]{1,0:T(8,128)(2,1)}, u32[]{:S(2)}) copy-start(bf16[128,4608]{1,0:T(8,128)(2,1)} %unembed.1) | copy-start | bytes 3538948
  2.8 31.6 %copy-start.5 = (f32[4608]{0:T(1024)S(1)}, f32[4608]{0:T(1024)}, u32[]{:S(2)}) copy-start(f32[4608]{0:T(1024)} %pre) | copy-start | bytes 55300
  2.8 31.6 %copy-start.6 = (f32[4608]{0:T(1024)S(1)}, f32[4608]{0:T(1024)}, u32[]{:S(2)}) copy-start(f32[4608]{0:T(1024)} %post.1) | copy-start | bytes 55300
  2.8 31.6 %copy-start.7 = (f32[4608]{0:T(1024)S(1)}, f32[4608]{0:T(1024)}, u32[]{:S(2)}) copy-start(f32[4608]{0:T(1024)} %final.1) | copy-start | bytes 55300
  34.4 2.2 %copy-start.9 = (s32[128,2]{0,1:T(2,128)S(1)}, s32[128,2]{0,1:T(2,128)}, u32[]{:S(2)}) copy-start(s32[128,2]{0,1:T(2,128)} %param.15) | copy-start | bytes 3076
  34.9 3.4 %collective-permute-start.2 = (bf16[128,2304]{1,0:T(8,128)(2,1)S(1)}, bf16[128,2304]{1,0:T(8,128)(2,1)S(1)}, u32[]{:S(2)}, u32[]{:S(2)}) collective-permute-start(bf16[128,2304]{1,0:T(8,128)(2,1)S(1)} %get-tuple-element.70.own), channel_id=1, source_target_pairs={{0,32},{32,0},{1,33},{33,1},{2,34},{34,2},{3,35},{35,3},{4,36},{36... | collective-permute-start | bytes 1769480 | tf_op jit(solution)/shard_map/ppermute | solution.py:297
  38.3 3.3 %collective-permute-start.3 = (bf16[128,2304]{1,0:T(8,128)(2,1)S(1)}, bf16[128,2304]{1,0:T(8,128)(2,1)S(1)}, u32[]{:S(2)}, u32[]{:S(2)}) collective-permute-start(bf16[128,2304]{1,0:T(8,128)(2,1)S(1)} %get-tuple-element.85.own), channel_id=1, source_target_pairs={{0,32},{32,0},{1,33},{33,1},{2,34},{34,2},{3,35},{35,3},{4,36},{36... | collective-permute-start | bytes 1769480 | tf_op jit(solution)/shard_map/ppermute | solution.py:297
  41.6 2.1 %collective-permute-start.4 = (bf16[128,2304]{1,0:T(8,128)(2,1)S(1)}, bf16[128,2304]{1,0:T(8,128)(2,1)S(1)}, u32[]{:S(2)}, u32[]{:S(2)}) collective-permute-start(bf16[128,2304]{1,0:T(8,128)(2,1)S(1)} %get-tuple-element.65), channel_id=1, source_target_pairs={{0,32},{32,0},{1,33},{33,1},{2,34},{34,2},{3,35},{35,3},{4,36},{36... | collective-permute-start | bytes 1769480 | tf_op jit(solution)/shard_map/ppermute | solution.py:297
  42.8 19.7 %copy-start.8 = (f32[512]{0:T(512)S(1)}, f32[512]{0:T(512)}, u32[]{:S(2)}) copy-start(f32[512]{0:T(512)} %param.24) | copy-start | bytes 6148
  61.9 1.9 %collective-permute-start.5 = (f32[2,2304]{1,0:T(2,128)S(1)}, f32[2,2304]{1,0:T(2,128)S(1)}, u32[]{:S(2)}, u32[]{:S(2)}) collective-permute-start(f32[2,2304]{1,0:T(2,128)S(1)} %shard_map.135.own), channel_id=1, source_target_pairs={{0,32},{32,0},{1,33},{33,1},{2,34},{34,2},{3,35},{35,3},{4,36},{36... | collective-permute-start | bytes 55304 | tf_op jit(solution)/shard_map/ppermute | solution.py:297
  82.7 2.1 %collective-permute-start.6 = (bf16[64,2,2,1152]{3,2,1,0:T(2,128)(2,1)S(1)}, bf16[64,2,2,1152]{3,2,1,0:T(2,128)(2,1)S(1)}, u32[]{:S(2)}, u32[]{:S(2)}) collective-permute-start(bf16[64,2,2,1152]{3,2,1,0:T(2,128)(2,1)S(1)} %bitcast.28), channel_id=1, source_target_pairs={{0,32},{32,0},{1,33},{33,1},{2,34},{34,2},{3,35},{35,3},{4,36},{36... | collective-permute-start | bytes 1769480 | tf_op jit(solution)/shard_map/ppermute | solution.py:297
  86.8 2.1 %collective-permute-start.7 = (bf16[128,2304]{1,0:T(8,128)(2,1)S(1)}, bf16[128,2304]{1,0:T(8,128)(2,1)S(1)}, u32[]{:S(2)}, u32[]{:S(2)}) collective-permute-start(bf16[128,2304]{1,0:T(8,128)(2,1)S(1)} %get-tuple-element.79), channel_id=1, source_target_pairs={{0,32},{32,0},{1,33},{33,1},{2,34},{34,2},{3,35},{35,3},{4,36},{36... | collective-permute-start | bytes 1769480 | tf_op jit(solution)/shard_map/ppermute | solution.py:297
  107.2 21.4 %slice-start = ((s8[4718592]{0:T(1024)(128)(4,1)}), s8[4194304]{0:T(1024)(128)(4,1)S(1)}, s32[]{:S(2)}) async-start(s8[4718592]{0:T(1024)(128)(4,1)} %bitcast.23), calls=%async_computation.5 | async-start | bytes 8388608
  107.4 21.2 %slice-start.1 = ((s8[4718592]{0:T(1024)(128)(4,1)}), s8[524288]{0:T(1024)(128)(4,1)S(1)}, s32[]{:S(2)}) async-start(s8[4718592]{0:T(1024)(128)(4,1)} %bitcast.23), calls=%async_computation.6 | async-start | bytes 1048576
  107.4 2.1 %collective-permute-start.8 = (f32[2,2304]{1,0:T(2,128)S(1)}, f32[2,2304]{1,0:T(2,128)S(1)}, u32[]{:S(2)}, u32[]{:S(2)}) collective-permute-start(f32[2,2304]{1,0:T(2,128)S(1)} %shard_map.142.own), channel_id=1, source_target_pairs={{0,32},{32,0},{1,33},{33,1},{2,34},{34,2},{3,35},{35,3},{4,36},{36... | collective-permute-start | bytes 55304 | tf_op jit(solution)/shard_map/ppermute | solution.py:297
  128.1 2.1 %collective-permute-start.9 = (bf16[64,2,2,1152]{3,2,1,0:T(2,128)(2,1)S(1)}, bf16[64,2,2,1152]{3,2,1,0:T(2,128)(2,1)S(1)}, u32[]{:S(2)}, u32[]{:S(2)}) collective-permute-start(bf16[64,2,2,1152]{3,2,1,0:T(2,128)(2,1)S(1)} %bitcast.30), channel_id=1, source_target_pairs={{0,32},{32,0},{1,33},{33,1},{2,34},{34,2},{3,35},{35,3},{4,36},{36... | collective-permute-start | bytes 1769480 | tf_op jit(solution)/shard_map/ppermute | solution.py:297

commit v6 on v5

--- a/solution.py
+++ b/solution.py
@@ -79,11 +79,6 @@
     )
 
 
-def spread(value, out):
-    for chip in range(out.shape[0]):
-        out[chip] = value
-
-
 def load_kernel(clean, corrupt, own_clean, own_corrupt, sems):
     copies = [
         pltpu.make_async_copy(clean, own_clean, sems.at[0]),
@@ -102,19 +97,21 @@
 
 def chip_rows_kernel(where, clean, corrupt, other_clean, other_corrupt, out, stream, rows):
     first = where[0] == 0
-    mine, _ = halves(where, out.shape[2])
     for i, (a, b) in enumerate(((clean, other_clean), (corrupt, other_corrupt))):
         a, b = a[...].astype(F32), b[...].astype(F32)
         rows[2 * i : 2 * i + 1] = jnp.where(first, a, b)
         rows[2 * i + 1 : 2 * i + 2] = jnp.where(first, b, a)
     stream[...] = rows[0:2]
-    spread(rows[:, mine].astype(BF16), out)
+    spread_quarters(where, rows, out)
 
 
 def rows_kernel(pieces, *refs):
     clean, corrupt = refs[-2:]
-    clean[...] = pieces[:, :2].reshape(clean.shape)
-    corrupt[...] = pieces[:, 2:].reshape(corrupt.shape)
+    width = pieces.shape[3]
+    for core in range(2):
+        lanes = slice(core * width, (core + 1) * width)
+        clean[:, lanes] = pieces[:, core, :2].reshape(clean.shape[0], width)
+        corrupt[:, lanes] = pieces[:, core, 2:].reshape(corrupt.shape[0], width)
 
 
 def forward_kernel(where, own, other, w_gate, w_up, w_down, gain, send, hidden, gate, up):
@@ -282,10 +279,6 @@
     _, theirs = halves(where, 2 * other.shape[3])
     projected = part[...] + dot_nt(w_dec[:, theirs], token_rows(other))
     out[...] = jnp.sum(change[...] * projected.T, axis=0, keepdims=True)
-
-
-def exchanged(blocks):
-    return lax.all_to_all(blocks, CHIPS, 0, 0, tiled=True)
 
 
 def exchanged_by_core(blocks):
@@ -349,7 +342,7 @@
     *partner, where, clean, corrupt = lax.optimization_barrier((*partner, where, *held))
     quads, stream = call(
         chip_rows_kernel,
-        (shape((chips, 4, half), BF16), pair_rows),
+        (shape((chips, 2, 4, half // 2), BF16), pair_rows),
         where, clean, corrupt, *partner,
         scratch=[pltpu.VMEM((4, width), F32)],
         flops=HINT,
@@ -357,7 +350,7 @@
     own, own_corrupt = call(
         rows_kernel,
         (halved, halved),
-        exchanged(quads), w_enc, w_gate, w_up, w_down, unembed, pre_gain, post_gain, final_gain,
+        exchanged_by_core(quads), w_enc, w_gate, w_up, w_down, unembed, pre_gain, post_gain, final_gain,
         flops=HINT,
     )
     pre_gain, own_corrupt = lax.optimization_barrier((pre_gain, own_corrupt))

time: 132 us -> 132 us (level)
    all_to_all x4 -> x5, blocking collectives: 71.6 us -> 103 us  [exchanged_by_core(): return lax.all_to_all(flat, CORES, 0, 0, tiled=True).reshape(blocks.shape)]
    all_to_all x1 -> x0, blocking collectives: 30.9 us -> none  [exchanged(): return lax.all_to_all(blocks, CHIPS, 0, 0, tiled=True)]
where the time goes in v6:
time: 132 us
  blocking collectives  103 us (78%)
  Pallas kernels  19.6 us (15%)
  starting transfers between devices  5.47 us (4%)
  waiting for transfers between devices  3.39 us (3%)
    all_to_all x5, blocking collectives, exchanged_by_core(): return lax.all_to_all(flat, CORES, 0, 0, tiled=True).reshape(blocks.shape)  103 us
    pallas_call x20, Pallas kernels, call(): pl.pallas_call(kernel, out_shape=jax.tree.map(lambda o: space(o.shape, o....  19.6 us
    ppermute x10, starting transfers between devices, swapped(): return lax.ppermute(value, 'core', SWAP)  5.47 us
    ppermute x10, waiting for transfers between devices, swapped(): return lax.ppermute(value, 'core', SWAP)  3.39 us
  transfers between devices with their start and end apart: 10, of which 7 were waited for; matrix products, arithmetic and copies ran while one was open for 0% of the time, Pallas kernels for 9%

profile of v6, /device:TPU:1, one launch (start us, length us, event | category | flops | bytes accessed | tf_op | source)
XLA Modules:
  0.0 131.5 jit_solution(6574959174693798004)
XLA Ops:
  0.0 1.4 %collective-permute-start = (bf16[1,4608]{1,0:T(2,128)(2,1)}, bf16[1,4608]{1,0:T(2,128)(2,1)S(1)}, u32[]{:S(2)}, u32[]{:S(2)}) collective-permute-start(bf16[1,4608]{1,0:T(2,128)(2,1)} %clean.1), channel_id=1, source_target_pairs={{0,32},{32,0},{1,33},{33,1},{2,34},{34,2},{3,35},{35,3},{4,36},{36... | collective-permute-start | bytes 27656 | tf_op jit(solution)/shard_map/ppermute | solution.py:290
  1.4 0.1 pad_add_fusion.where
  1.5 0.8 shard_map.127
  2.2 0.2 collective-permute-done.other_clean
  2.4 0.3 collective-permute-done.1.other_corrupt
  2.8 0.0 copy-start.4
  2.8 0.0 copy-start.5
  2.8 0.0 copy-start.6
  2.8 0.0 copy-start.7
  2.8 0.7 shard_map.128
  3.5 31.1 %all_to_all.25 = bf16[128,4,1152]{2,1,0:T(4,128)(2,1)S(1)} all-to-all(bf16[128,4,1152]{2,1,0:T(4,128)(2,1)S(1)} %bitcast.36), channel_id=1, replica_groups=mesh['y_lo'=2,'core'=2,'y_hi'=2,'x'=4,'z'=4] {'y_hi','z','y_lo','x','core'}, dimensions={0} | all-to-all | bytes 2359296 | tf_op jit(solution)/shard_map/all_to_all | solution.py:286
  34.7 0.0 copy-start.9
  34.7 0.5 shard_map.129
  35.2 0.7 collective-permute-start.2
  36.0 0.8 shard_map.131.weighted
  36.8 0.8 collective-permute-done.2.other
  37.6 0.4 collective-permute-start.3
  38.0 2.9 %shard_map.132 = (bf16[128,2304]{1,0:T(8,128)(2,1)S(1)}, bf16[128,288]{1,0:T(8,128)(2,1)S(1)}, f32[288,128]{1,0:T(8,128)S(1)}, f32[288,128]{1,0:T(8,128)S(1)}) custom-call(s32[3]{0:T(128)S(1)} %pad_add_fusion.where, bf16[128,2304]{1,0:T(8,128)(2,1)S(1)} %get-tuple-element.70.own, bf16[128,2304]{1,0:T(8,128)(2,1)S(1)} %collective-permute-done.2.other, ...), custom_call_target="tpu_custom_call" | custom-call | tf_op jit(solution)/shard_map/pallas_call | solution.py:31
  40.9 0.2 collective-permute-start.4
  41.1 1.0 shard_map.133.own
  42.1 0.0 copy-start.8
  42.1 0.8 collective-permute-done.4.arrived
  43.0 0.2 shard_map.134
  43.2 17.8 %all_to_all.26 = bf16[128,2,1152]{2,1,0:T(2,128)(2,1)S(1)} all-to-all(bf16[128,2,1152]{2,1,0:T(2,128)(2,1)S(1)} %bitcast.34), channel_id=1, replica_groups=mesh['y_lo'=2,'core'=2,'y_hi'=2,'x'=4,'z'=4] {'y_hi','z','y_lo','x','core'}, dimensions={0} | all-to-all | bytes 1179648 | tf_op jit(solution)/shard_map/all_to_all | solution.py:286
  61.0 0.2 shard_map.135.own
  61.2 0.6 collective-permute-start.5
  61.8 1.3 %shard_map.136.clean_code = f32[128,512]{1,0:T(8,128)S(1)} custom-call(s32[3]{0:T(128)S(1)} %pad_add_fusion.where, bf16[128,2304]{1,0:T(8,128)(2,1)S(1)} %get-tuple-element.70.own, bf16[128,2304]{1,0:T(8,128)(2,1)S(1)} %collective-permute-done.2.other, bf16[4608,512]{1,0:T(8,128)(2,1)S(1)} %copy-done.3, f32[1,512]{1,0:T(1,128)S(1)} %bitcast.39), custom_call_target="tpu_custom_call" | custom-call | tf_op jit(solution)/shard_map/pallas_call | solution.py:31
  63.1 1.0 shard_map.137
  64.2 17.8 %all_to_all.27 = bf16[128,2,1152]{2,1,0:T(2,128)(2,1)S(1)} all-to-all(bf16[128,2,1152]{2,1,0:T(2,128)(2,1)S(1)} %bitcast.38), channel_id=1, replica_groups=mesh['y_lo'=2,'core'=2,'y_hi'=2,'x'=4,'z'=4] {'y_hi','z','y_lo','x','core'}, dimensions={0} | all-to-all | bytes 1179648 | tf_op jit(solution)/shard_map/all_to_all | solution.py:286
  82.0 0.5 collective-permute-start.6
  82.5 1.1 shard_map.138.own_part
  83.6 0.6 collective-permute-done.6.other
  84.1 2.0 %shard_map.139 = (bf16[128,2304]{1,0:T(8,128)(2,1)S(1)}, bf16[128,288]{1,0:T(8,128)(2,1)S(1)}, bf16[128,288]{1,0:T(8,128)(2,1)S(1)}) custom-call(s32[3]{0:T(128)S(1)} %pad_add_fusion.where, f32[288,128]{1,0:T(8,128)S(1)} %shard_map.138.own_part, bf16[64,2,2,1152]{3,2,1,0:T(2,128)(2,1)S(1)} %collective-permute-done.6.other, ...), custom_call_target="tpu_custom_call" | custom-call | tf_op jit(solution)/shard_map/pallas_call | solution.py:31
  86.1 0.4 collective-permute-start.7
  86.6 1.3 shard_map.140.own
  87.9 0.3 collective-permute-done.7.arrived
  88.2 0.2 shard_map.141
  88.4 18.1 %all_to_all.28 = bf16[128,2,1152]{2,1,0:T(2,128)(2,1)S(1)} all-to-all(bf16[128,2,1152]{2,1,0:T(2,128)(2,1)S(1)} %bitcast.35), channel_id=1, replica_groups=mesh['y_lo'=2,'core'=2,'y_hi'=2,'x'=4,'z'=4] {'y_hi','z','y_lo','x','core'}, dimensions={0} | all-to-all | bytes 1179648 | tf_op jit(solution)/shard_map/all_to_all | solution.py:286
  106.5 0.2 shard_map.142.own
  106.7 0.0 slice-start.1
  106.7 0.7 collective-permute-start.8
  107.5 1.3 %shard_map.143.change = f32[128,512]{1,0:T(8,128)S(1)} custom-call(s32[3]{0:T(128)S(1)} %pad_add_fusion.where, bf16[128,2304]{1,0:T(8,128)(2,1)S(1)} %get-tuple-element.85.own, bf16[128,2304]{1,0:T(8,128)(2,1)S(1)} %collective-permute-done.3.other, bf16[4608,512]{1,0:T(8,128)(2,1)S(1)} %copy-done.3, f32[1,512]{1,0:T(1,128)S(1)} %bitcast.40, ...), custom_call_target="tpu_custom_call" | custom-call | tf_op jit(solution)/shard_map/pallas_call | solution.py:31
  108.8 0.8 shard_map.144
  109.6 17.8 %all_to_all.29 = bf16[128,2,1152]{2,1,0:T(2,128)(2,1)S(1)} all-to-all(bf16[128,2,1152]{2,1,0:T(2,128)(2,1)S(1)} %bitcast.27), channel_id=1, replica_groups=mesh['y_lo'=2,'core'=2,'y_hi'=2,'x'=4,'z'=4] {'y_hi','z','y_lo','x','core'}, dimensions={0} | all-to-all | bytes 1179648 | tf_op jit(solution)/shard_map/all_to_all | solution.py:286
  127.4 0.5 collective-permute-start.9
  127.9 1.3 %shard_map.145.part = f32[512,128]{1,0:T(8,128)S(1)} custom-call(s32[3]{0:T(128)S(1)} %pad_add_fusion.where, bf16[64,2,2,1152]{3,2,1,0:T(2,128)(2,1)S(1)} %bitcast.33, bf16[512,4608]{1,0:T(8,128)(2,1)S(1)} %bitcast.26), custom_call_target="tpu_custom_call" | custom-call | tf_op jit(solution)/shard_map/pallas_call | solution.py:31
  129.3 0.3 collective-permute-done.9.other
  129.5 2.0 %shard_map.146 = f32[1,512]{1,0:T(1,128)} custom-call(s32[3]{0:T(128)S(1)} %pad_add_fusion.where, f32[512,128]{1,0:T(8,128)S(1)} %shard_map.145.part, bf16[64,2,2,1152]{3,2,1,0:T(2,128)(2,1)S(1)} %collective-permute-done.9.other, bf16[512,4608]{1,0:T(8,128)(2,1)S(1)} %bitcast.26, f32[128,512]{1,0:T(8,128)S(1)} %shard_map.143.change), custom_call_target="tpu_custom_call" | custom-call | tf_op jit(solution)/shard_map/pallas_call | solution.py:31
  (23 shorter events, 0.1 us)
Async XLA Ops:
  0.0 2.4 %collective-permute-start = (bf16[1,4608]{1,0:T(2,128)(2,1)}, bf16[1,4608]{1,0:T(2,128)(2,1)S(1)}, u32[]{:S(2)}, u32[]{:S(2)}) collective-permute-start(bf16[1,4608]{1,0:T(2,128)(2,1)} %clean.1), channel_id=1, source_target_pairs={{0,32},{32,0},{1,33},{33,1},{2,34},{34,2},{3,35},{35,3},{4,36},{36... | collective-permute-start | bytes 27656 | tf_op jit(solution)/shard_map/ppermute | solution.py:290
  1.4 1.4 %collective-permute-start.1 = (bf16[1,4608]{1,0:T(2,128)(2,1)}, bf16[1,4608]{1,0:T(2,128)(2,1)S(1)}, u32[]{:S(2)}, u32[]{:S(2)}) collective-permute-start(bf16[1,4608]{1,0:T(2,128)(2,1)} %corrupt.1), channel_id=1, source_target_pairs={{0,32},{32,0},{1,33},{33,1},{2,34},{34,2},{3,35},{35,3},{4,36},{36... | collective-permute-start | bytes 27656 | tf_op jit(solution)/shard_map/ppermute | solution.py:290
  2.8 31.8 %copy-start = (bf16[288,4608]{1,0:T(8,128)(2,1)S(1)}, bf16[288,4608]{1,0:T(8,128)(2,1)}, u32[]{:S(2)}) copy-start(bf16[288,4608]{1,0:T(8,128)(2,1)} %w_down.7) | copy-start | bytes 7962628
  2.8 31.8 %copy-start.1 = (bf16[4608,288]{0,1:T(8,128)(2,1)S(1)}, bf16[4608,288]{0,1:T(8,128)(2,1)}, u32[]{:S(2)}) copy-start(bf16[4608,288]{0,1:T(8,128)(2,1)} %param.20) | copy-start | bytes 7962628
  2.8 31.8 %copy-start.2 = (bf16[4608,288]{0,1:T(8,128)(2,1)S(1)}, bf16[4608,288]{0,1:T(8,128)(2,1)}, u32[]{:S(2)}) copy-start(bf16[4608,288]{0,1:T(8,128)(2,1)} %param.21) | copy-start | bytes 7962628
  2.8 31.8 %copy-start.3 = (bf16[4608,512]{1,0:T(8,128)(2,1)S(1)}, bf16[4608,512]{1,0:T(8,128)(2,1)}, u32[]{:S(2)}) copy-start(bf16[4608,512]{1,0:T(8,128)(2,1)} %w_enc.3) | copy-start | bytes 14155780
  2.8 31.8 %copy-start.4 = (bf16[128,4608]{1,0:T(8,128)(2,1)S(1)}, bf16[128,4608]{1,0:T(8,128)(2,1)}, u32[]{:S(2)}) copy-start(bf16[128,4608]{1,0:T(8,128)(2,1)} %unembed.1) | copy-start | bytes 3538948
  2.8 31.8 %copy-start.5 = (f32[4608]{0:T(1024)S(1)}, f32[4608]{0:T(1024)}, u32[]{:S(2)}) copy-start(f32[4608]{0:T(1024)} %pre) | copy-start | bytes 55300
  2.8 31.8 %copy-start.6 = (f32[4608]{0:T(1024)S(1)}, f32[4608]{0:T(1024)}, u32[]{:S(2)}) copy-start(f32[4608]{0:T(1024)} %post.1) | copy-start | bytes 55300
  2.8 31.8 %copy-start.7 = (f32[4608]{0:T(1024)S(1)}, f32[4608]{0:T(1024)}, u32[]{:S(2)}) copy-start(f32[4608]{0:T(1024)} %final.1) | copy-start | bytes 55300
  34.7 1.3 copy-start.9
  35.2 2.4 %collective-permute-start.2 = (bf16[128,2304]{1,0:T(8,128)(2,1)S(1)}, bf16[128,2304]{1,0:T(8,128)(2,1)S(1)}, u32[]{:S(2)}, u32[]{:S(2)}) collective-permute-start(bf16[128,2304]{1,0:T(8,128)(2,1)S(1)} %get-tuple-element.70.own), channel_id=1, source_target_pairs={{0,32},{32,0},{1,33},{33,1},{2,34},{34,2},{3,35},{35,3},{4,36},{36... | collective-permute-start | bytes 1769480 | tf_op jit(solution)/shard_map/ppermute | solution.py:290
  37.6 3.3 %collective-permute-start.3 = (bf16[128,2304]{1,0:T(8,128)(2,1)S(1)}, bf16[128,2304]{1,0:T(8,128)(2,1)S(1)}, u32[]{:S(2)}, u32[]{:S(2)}) collective-permute-start(bf16[128,2304]{1,0:T(8,128)(2,1)S(1)} %get-tuple-element.85.own), channel_id=1, source_target_pairs={{0,32},{32,0},{1,33},{33,1},{2,34},{34,2},{3,35},{35,3},{4,36},{36... | collective-permute-start | bytes 1769480 | tf_op jit(solution)/shard_map/ppermute | solution.py:290
  40.9 2.1 %collective-permute-start.4 = (bf16[128,2304]{1,0:T(8,128)(2,1)S(1)}, bf16[128,2304]{1,0:T(8,128)(2,1)S(1)}, u32[]{:S(2)}, u32[]{:S(2)}) collective-permute-start(bf16[128,2304]{1,0:T(8,128)(2,1)S(1)} %get-tuple-element.65), channel_id=1, source_target_pairs={{0,32},{32,0},{1,33},{33,1},{2,34},{34,2},{3,35},{35,3},{4,36},{36... | collective-permute-start | bytes 1769480 | tf_op jit(solution)/shard_map/ppermute | solution.py:290
  42.1 19.7 %copy-start.8 = (f32[512]{0:T(512)S(1)}, f32[512]{0:T(512)}, u32[]{:S(2)}) copy-start(f32[512]{0:T(512)} %param.24) | copy-start | bytes 6148
  61.2 1.9 %collective-permute-start.5 = (f32[2,2304]{1,0:T(2,128)S(1)}, f32[2,2304]{1,0:T(2,128)S(1)}, u32[]{:S(2)}, u32[]{:S(2)}) collective-permute-start(f32[2,2304]{1,0:T(2,128)S(1)} %shard_map.135.own), channel_id=1, source_target_pairs={{0,32},{32,0},{1,33},{33,1},{2,34},{34,2},{3,35},{35,3},{4,36},{36... | collective-permute-start | bytes 55304 | tf_op jit(solution)/shard_map/ppermute | solution.py:290
  82.0 2.1 %collective-permute-start.6 = (bf16[64,2,2,1152]{3,2,1,0:T(2,128)(2,1)S(1)}, bf16[64,2,2,1152]{3,2,1,0:T(2,128)(2,1)S(1)}, u32[]{:S(2)}, u32[]{:S(2)}) collective-permute-start(bf16[64,2,2,1152]{3,2,1,0:T(2,128)(2,1)S(1)} %bitcast.30), channel_id=1, source_target_pairs={{0,32},{32,0},{1,33},{33,1},{2,34},{34,2},{3,35},{35,3},{4,36},{36... | collective-permute-start | bytes 1769480 | tf_op jit(solution)/shard_map/ppermute | solution.py:290
  86.1 2.1 %collective-permute-start.7 = (bf16[128,2304]{1,0:T(8,128)(2,1)S(1)}, bf16[128,2304]{1,0:T(8,128)(2,1)S(1)}, u32[]{:S(2)}, u32[]{:S(2)}) collective-permute-start(bf16[128,2304]{1,0:T(8,128)(2,1)S(1)} %get-tuple-element.79), channel_id=1, source_target_pairs={{0,32},{32,0},{1,33},{33,1},{2,34},{34,2},{3,35},{35,3},{4,36},{36... | collective-permute-start | bytes 1769480 | tf_op jit(solution)/shard_map/ppermute | solution.py:290
  106.5 21.4 %slice-start = ((s8[4718592]{0:T(1024)(128)(4,1)}), s8[4194304]{0:T(1024)(128)(4,1)S(1)}, s32[]{:S(2)}) async-start(s8[4718592]{0:T(1024)(128)(4,1)} %bitcast.25), calls=%async_computation.5 | async-start | bytes 8388608
  106.7 21.2 %slice-start.1 = ((s8[4718592]{0:T(1024)(128)(4,1)}), s8[524288]{0:T(1024)(128)(4,1)S(1)}, s32[]{:S(2)}) async-start(s8[4718592]{0:T(1024)(128)(4,1)} %bitcast.25), calls=%async_computation.6 | async-start | bytes 1048576
  106.7 2.1 %collective-permute-start.8 = (f32[2,2304]{1,0:T(2,128)S(1)}, f32[2,2304]{1,0:T(2,128)S(1)}, u32[]{:S(2)}, u32[]{:S(2)}) collective-permute-start(f32[2,2304]{1,0:T(2,128)S(1)} %shard_map.142.own), channel_id=1, source_target_pairs={{0,32},{32,0},{1,33},{33,1},{2,34},{34,2},{3,35},{35,3},{4,36},{36... | collective-permute-start | bytes 55304 | tf_op jit(solution)/shard_map/ppermute | solution.py:290
  127.4 2.1 %collective-permute-start.9 = (bf16[64,2,2,1152]{3,2,1,0:T(2,128)(2,1)S(1)}, bf16[64,2,2,1152]{3,2,1,0:T(2,128)(2,1)S(1)}, u32[]{:S(2)}, u32[]{:S(2)}) collective-permute-start(bf16[64,2,2,1152]{3,2,1,0:T(2,128)(2,1)S(1)} %bitcast.32), channel_id=1, source_target_pairs={{0,32},{32,0},{1,33},{33,1},{2,34},{34,2},{3,35},{35,3},{4,36},{36... | collective-permute-start | bytes 1769480 | tf_op jit(solution)/shard_map/ppermute | solution.py:290
